TPU v7x, 32 devices: a whole 2x2x4 slice. The times are simulated.
32 devices in a mesh: groups: 2 (over y), seq: 4 (over x, core), chan: 4 (over z).
Axes of the slice: x: 2, y: 2, z: 4, core: 2. Of those that a mesh axis runs over, the one named last changes fastest.
Arguments:
- tokens: bfloat16 [4096, 4096], P(('groups', 'seq'), 'chan'), parts along dimension 0, may hold values from -6 to 6
- norm_gain: float32 [4096], replicated, may hold values from 0.5 to 1.5
- proj_weight: bfloat16 [4096, 3, 4096], P('seq', None, 'chan'), may hold values from -0.09375 to 0.09375
- short_filter: float32 [3, 3, 4096], P(None, None, 'chan'), may hold values from -2.5 to 2.5
- long_filter: float32 [4096, 2048], P('chan', 'seq'), may hold values from -4 to 4, as said below
- skip_gain: float32 [4096], P('chan'), may hold values from 0.5 to 1.5
- out_weight: bfloat16 [4096, 4096], P(None, 'chan'), may hold values from -0.09375 to 0.09375
Outputs:
- block_out: bfloat16 [4096, 4096], P(('groups', 'seq'), 'chan'), parts along dimension 0
There are 2 independent parts, one for each index of `groups`. A program takes and returns all parts, laid end to end along the dimension named above; an argument that names none is the same for every part. Nothing has to cross between parts.
Inputs may be any that keep to these rules, and one draw needn't show every extreme that they name: `long_filter`: filter taps of the sequence-long convolution.
All inputs are finite; a program needn't handle non-finite values.
Results may differ from a plain program's by a relative error of at most 0.012.
Values may be sent and summed in bfloat16 or wider, within the bound.
A program may use at most 128 MiB of HBM per device.

v0:
```python
import functools
import math

import jax
import jax.numpy as jnp
import numpy as np
from jax import lax
from jax.experimental import pallas as pl
from jax.experimental.pallas import tpu as pltpu
from jax.sharding import PartitionSpec as P

SHORT = 3


EPSILON = 1e-06
HIGHEST = lax.Precision.HIGHEST


def from_behind(value, axis, steps):
    count = lax.axis_size(axis)
    initial, last = (max(0, -steps), min(count, count - steps))
    return lax.ppermute(value, axis, [(source, source + steps) for source in range(initial, last)])


def angle_table(row_count, col_count, period, sign):
    row_index = lax.iota(jnp.int32, row_count)[:, None]
    col_index = lax.iota(jnp.int32, col_count)[None, :]
    angles = (row_index * col_index % period).astype(jnp.float32) * (sign * 2.0 * math.pi / period)
    return (jnp.cos(angles), jnp.sin(angles))


def forward_spectrum(signal_rows, first, second):
    channels = signal_rows.shape[0]
    grid_rows = signal_rows.reshape(channels, first, second)
    cos_first, sin_first = angle_table(first, first, first, -1.0)
    part_re = jnp.einsum("cab,ak->ckb", grid_rows, cos_first, precision=HIGHEST)
    part_im = jnp.einsum("cab,ak->ckb", grid_rows, sin_first, precision=HIGHEST)
    twist_cos, twist_sin = angle_table(first, second, first * second, -1.0)
    part_re, part_im = (
        part_re * twist_cos - part_im * twist_sin,
        part_re * twist_sin + part_im * twist_cos,
    )
    cos_second, sin_second = angle_table(second, second, second, -1.0)
    spectrum_real = jnp.einsum("ckb,bm->ckm", part_re, cos_second, precision=HIGHEST) - jnp.einsum(
        "ckb,bm->ckm", part_im, sin_second, precision=HIGHEST
    )
    spec_im = jnp.einsum("ckb,bm->ckm", part_re, sin_second, precision=HIGHEST) + jnp.einsum(
        "ckb,bm->ckm", part_im, cos_second, precision=HIGHEST
    )
    return (spectrum_real, spec_im)


def inverse_spectrum(spectrum_real, spec_im, first, second):
    channels = spectrum_real.shape[0]
    cos_second, sin_second = angle_table(second, second, second, 1.0)
    part_re = jnp.einsum("ckm,bm->ckb", spectrum_real, cos_second, precision=HIGHEST) - jnp.einsum(
        "ckm,bm->ckb", spec_im, sin_second, precision=HIGHEST
    )
    part_im = jnp.einsum("ckm,bm->ckb", spectrum_real, sin_second, precision=HIGHEST) + jnp.einsum(
        "ckm,bm->ckb", spec_im, cos_second, precision=HIGHEST
    )
    twist_cos, twist_sin = angle_table(first, second, first * second, 1.0)
    part_re, part_im = (
        part_re * twist_cos - part_im * twist_sin,
        part_re * twist_sin + part_im * twist_cos,
    )
    cos_first, sin_first = angle_table(first, first, first, 1.0)
    result = jnp.einsum("ckb,ak->cab", part_re, cos_first, precision=HIGHEST) - jnp.einsum(
        "ckb,ak->cab", part_im, sin_first, precision=HIGHEST
    )
    return result.reshape(channels, first * second) / (first * second)


def spectral_conv(signal_rows, filter_rows):
    channels, length = signal_rows.shape
    padded_len = 2 * length
    log_len = padded_len.bit_length() - 1
    first = 1 << log_len // 2
    second = padded_len // first
    zeros_tail = jnp.zeros((channels, length), jnp.float32)
    sig_re, sig_im = forward_spectrum(
        jnp.concatenate([signal_rows, zeros_tail], axis=1), first, second
    )
    tap_re, tap_im = forward_spectrum(
        jnp.concatenate([filter_rows, zeros_tail], axis=1), first, second
    )
    prod_re = sig_re * tap_re - sig_im * tap_im
    prod_im = sig_re * tap_im + sig_im * tap_re
    return inverse_spectrum(prod_re, prod_im, first, second)[:, :length]


def short_filter_output(projected, rim_cells, kernel_coefficients):
    count = kernel_coefficients.shape[0]
    steps_len = projected.shape[2]
    extended = jnp.concatenate([rim_cells, projected], axis=2).astype(jnp.float32)
    total = jnp.zeros(projected.shape, jnp.float32)
    for tap in range(count):
        total = (
            total
            + kernel_coefficients[tap][:, :, None]
            * extended[:, :, count - 1 - tap : count - 1 - tap + steps_len]
        )
    return total.astype(jnp.bfloat16)


def hyena_mixer(keys_rows, values_rows, long_taps, skip_part):
    middle = keys_rows.astype(jnp.float32) * values_rows.astype(jnp.float32)
    return (spectral_conv(middle, long_taps) + skip_part[:, None] * middle).astype(jnp.bfloat16)


def body(tokens, norm_gain, proj_weight, short_filter, long_filter, skip_gain, out_weight):
    seq_count = lax.axis_size("seq")
    local_rows = tokens.shape[0]
    local_chan = proj_weight.shape[2]
    subset = local_chan // seq_count
    length = local_rows * seq_count
    offset = lax.axis_index("seq") * subset
    whole = lax.all_gather(tokens, "chan", axis=1, tiled=True)
    wide = whole.astype(jnp.float32)
    rescaled_signal = (
        wide * lax.rsqrt(jnp.mean(wide * wide, axis=1, keepdims=True) + EPSILON) * norm_gain
    ).astype(jnp.bfloat16)
    projected = lax.dot_general(
        lax.all_gather(proj_weight, "seq", axis=0, tiled=True),
        rescaled_signal,
        (((0,), (1,)), ((), ())),
        preferred_element_type=jnp.float32,
    ).astype(jnp.bfloat16)
    taps_grid = long_filter.reshape(1, seq_count, subset, local_rows)
    long_taps = lax.all_to_all(taps_grid, "seq", split_axis=1, concat_axis=3, tiled=True).reshape(
        subset, length
    )
    skip_part = lax.dynamic_slice_in_dim(skip_gain, offset, subset, 0)
    rim_cells = from_behind(projected[:, :, local_rows - (SHORT - 1) :], "seq", 1)
    featured = short_filter_output(projected, rim_cells, short_filter)
    pair_grid = featured[1:].reshape(2, seq_count, subset, local_rows)
    moved = lax.all_to_all(pair_grid, "seq", split_axis=1, concat_axis=3, tiled=True).reshape(
        2, subset, length
    )
    result = hyena_mixer(moved[0], moved[1], long_taps, skip_part)
    returned = lax.all_to_all(
        result.reshape(1, subset, length), "seq", split_axis=2, concat_axis=0, tiled=True
    )
    returned = returned.reshape(local_chan, local_rows)
    gated = (featured[0].astype(jnp.float32) * returned.astype(jnp.float32)).astype(jnp.bfloat16)
    full_mix = lax.all_gather(gated, "chan", axis=0, tiled=True)
    update = lax.dot_general(
        full_mix, out_weight, (((0,), (0,)), ((), ())), preferred_element_type=jnp.float32
    )
    return (tokens.astype(jnp.float32) + update).astype(jnp.bfloat16)


TOKEN_CHUNKS = 8
WEIGHT_CHUNKS = 16
GATED_CHUNKS = 4
ANY = pl.BlockSpec(memory_space=pl.ANY)


def remote(src, dst, send_sem, recv_sem, where):
    return pltpu.make_async_remote_copy(
        src_ref=src,
        dst_ref=dst,
        send_sem=send_sem,
        recv_sem=recv_sem,
        device_id=where,
        device_id_type=pl.DeviceIdType.MESH,
    )


def greet(devices):
    barrier = pltpu.get_barrier_semaphore()
    for where, present in devices:

        @pl.when(present)
        def _():
            pl.semaphore_signal(
                barrier, inc=1, device_id=where, device_id_type=pl.DeviceIdType.MESH
            )

    pl.semaphore_wait(
        barrier, sum(jnp.asarray(present).astype(jnp.int32) for _, present in devices)
    )


class Line:
    def __init__(self, view, count, chunks, send_sem, recv_sem, place):
        self.view, self.count, self.chunks = view, count, chunks
        self.send_sem, self.recv_sem, self.place = send_sem, recv_sem, place
        self.me = lax.axis_index("chan")

    def copy(self, way, step, chunk, src=None):
        step_to = 1 if way == 0 else -1
        owner = jnp.clip(self.me - step * step_to, 0, self.count - 1)
        target = jnp.clip(self.me + step_to, 0, self.count - 1)
        block = self.view(owner, chunk)
        return remote(
            block if src is None else src,
            block,
            self.send_sem.at[way, step, chunk],
            self.recv_sem.at[way, step, chunk],
            self.place(target),
        )

    def sends(self, way, step):
        if way == 0:
            return (self.me - step >= 0) & (self.me + 1 < self.count)
        return (self.me + step < self.count) & (self.me - 1 >= 0)

    def receives(self, way, step):
        if way == 0:
            return self.me - 1 - step >= 0
        return self.me + 1 + step < self.count

    def arrived(self, way, step, chunk):
        step_to = 1 if way == 0 else -1
        owner = jnp.clip(self.me - (step + 1) * step_to, 0, self.count - 1)
        block = self.view(owner, chunk)
        remote(
            block,
            block,
            self.send_sem.at[way, step, chunk],
            self.recv_sem.at[way, step, chunk],
            self.place(self.me),
        ).wait_recv()
        return owner


def gather_inputs_kernel(
    sizes,
    tokens,
    weights,
    taps,
    all_tokens,
    all_weights,
    all_taps,
    token_room,
    weight_room,
    tap_room,
    local_sem,
    line_send,
    line_recv,
    mate_send,
    mate_recv,
    x_send,
    x_recv,
    y_send,
    y_recv,
    f_send,
    f_recv,
):
    chan_count = sizes
    y, s, z = (lax.axis_index(name) for name in ("groups", "seq", "chan"))
    x, core = s // 2, s % 2
    mate = (y, s + 1 - 2 * core, z)
    across = lambda to: (y, (1 - x) * 2 + to, z)
    beside = (1 - y, s, z)
    rows, width = tokens.shape
    branches, depth, columns = weights.shape[0], weights.shape[1], weights.shape[2] // 2
    lags = taps.shape[2]
    half, half_lags = depth // 2, lags // 2

    greet(
        [
            (mate, True),
            (across(0), True),
            (across(1), True),
            (beside, True),
            ((y, s, jnp.minimum(z + 1, chan_count - 1)), z + 1 < chan_count),
            ((y, s, jnp.maximum(z - 1, 0)), z > 0),
        ]
    )

    token_rows = rows // TOKEN_CHUNKS
    weight_rows = half // WEIGHT_CHUNKS

    def token_view(owner, chunk):
        return all_tokens.at[
            pl.ds(core * rows + chunk * token_rows, token_rows), pl.ds(owner * width, width)
        ]

    line = Line(
        token_view, chan_count, TOKEN_CHUNKS, line_send, line_recv, lambda to: (y, s, to)
    )

    def weight_view(owner, part, chunk):
        return all_weights.at[pl.ds(owner * depth + part * half + chunk * weight_rows, weight_rows)]

    def tap_view(owner, part):
        return all_taps.at[pl.ds(owner * lags + part * half_lags, half_lags)]

    pending = []
    for chunk in range(TOKEN_CHUNKS):
        own = tokens.at[pl.ds(chunk * token_rows, token_rows)]
        for way in range(2):

            @pl.when(line.sends(way, 0))
            def _():
                line.copy(way, 0, chunk, own).start()

    for to in range(2):
        copy = remote(
            taps.at[to, 1 - x, pl.ds(y * half_lags, half_lags)],
            tap_view(s, y),
            f_send.at[to],
            f_recv.at[core],
            across(to),
        )
        copy.start()
        pending.append(copy)
    for chunk in range(WEIGHT_CHUNKS):
        for to in range(2):
            view = weight_view(s, y, chunk)
            for b in range(branches):
                remote(
                    weights.at[
                        b,
                        pl.ds(y * half + chunk * weight_rows, weight_rows),
                        pl.ds(to * columns, columns),
                    ],
                    view.at[:, pl.ds(b * columns, columns)],
                    x_send.at[to, chunk],
                    x_recv.at[core, chunk],
                    across(to),
                ).start()
            pending.append(
                remote(view, view, x_send.at[to, chunk], x_recv.at[core, chunk], across(to))
            )
    own_view = all_tokens.at[pl.ds(core * rows, rows), pl.ds(z * width, width)]
    mate_copies = [
        remote(tokens, own_view, mate_send.at[0], mate_recv.at[0], mate),
        remote(
            all_weights.at[pl.ds(s * depth, depth)],
            all_weights.at[pl.ds(s * depth, depth)],
            mate_send.at[1],
            mate_recv.at[1],
            mate,
        ),
        remote(
            taps.at[1 - core, x],
            all_taps.at[pl.ds(s * lags, lags)],
            mate_send.at[2],
            mate_recv.at[2],
            mate,
        ),
    ]
    for copy in (mate_copies[0], mate_copies[2]):
        copy.start()
    for b in range(branches):
        remote(
            weights.at[b, :, pl.ds((1 - core) * columns, columns)],
            all_weights.at[pl.ds(s * depth, depth), pl.ds(b * columns, columns)],
            mate_send.at[1],
            mate_recv.at[1],
            mate,
        ).start()
    ins = [
        pltpu.make_async_copy(tokens, token_room, local_sem.at[0]),
        pltpu.make_async_copy(taps.at[core, x], tap_room, local_sem.at[1]),
    ] + [
        pltpu.make_async_copy(
            weights.at[b, :, pl.ds(core * columns, columns)],
            weight_room.at[:, pl.ds(b * columns, columns)],
            local_sem.at[2 + b],
        )
        for b in range(branches)
    ]
    outs = [
        pltpu.make_async_copy(token_room, own_view, local_sem.at[5]),
        pltpu.make_async_copy(tap_room, all_taps.at[pl.ds(s * lags, lags)], local_sem.at[6]),
    ] + [
        pltpu.make_async_copy(
            weight_room.at[:, pl.ds(b * columns, columns)],
            all_weights.at[pl.ds(s * depth, depth), pl.ds(b * columns, columns)],
            local_sem.at[7 + b],
        )
        for b in range(branches)
    ]
    for copy in ins:
        copy.start()
    for first, second in zip(ins, outs):
        first.wait()
        second.start()

    def to_mate(way, step, chunk, owner):
        block = token_view(owner, chunk)
        index = 3 + (way * (chan_count - 1) + step) * TOKEN_CHUNKS + chunk
        return remote(block, block, mate_send.at[index], mate_recv.at[index], mate)

    for origin in range(2):
        view = tap_view((1 - x) * 2 + origin, y)
        remote(view, view, f_send.at[origin], f_recv.at[origin], beside).wait_recv()
        copy = remote(view, view, f_send.at[2 + origin], f_recv.at[2 + origin], beside)
        copy.start()
        pending.append(copy)

    steps = (chan_count - 1) * TOKEN_CHUNKS
    forwarded = 0
    for at in range(steps):
        step, chunk = divmod(at, TOKEN_CHUNKS)
        for way in range(2):

            @pl.when(line.receives(way, step))
            def _():
                owner = line.arrived(way, step, chunk)
                to_mate(way, step, chunk, owner).start()

            if step + 1 < chan_count - 1:

                @pl.when(line.receives(way, step) & line.sends(way, step + 1))
                def _():
                    line.copy(way, step + 1, chunk).start()

        while forwarded * steps < (at + 1) * WEIGHT_CHUNKS and forwarded < WEIGHT_CHUNKS:
            if (forwarded + 1) * steps > (at + 1) * WEIGHT_CHUNKS:
                break
            for origin in range(2):
                view = weight_view((1 - x) * 2 + origin, y, forwarded)
                remote(
                    view, view, x_send.at[origin, forwarded], x_recv.at[origin, forwarded], beside
                ).wait_recv()
                copy = remote(
                    view, view, y_send.at[origin, forwarded], y_recv.at[origin, forwarded], beside
                )
                copy.start()
                pending.append(copy)
            forwarded += 1
    for origin in range(2):
        owner = (1 - x) * 2 + origin
        for chunk in range(WEIGHT_CHUNKS):
            view = weight_view(owner, 1 - y, chunk)
            remote(
                view, view, y_send.at[origin, chunk], y_recv.at[origin, chunk], beside
            ).wait_recv()
        view = tap_view(owner, 1 - y)
        remote(view, view, f_send.at[2 + origin], f_recv.at[2 + origin], beside).wait_recv()
    for copy in outs:
        copy.wait()
    for copy in mate_copies:
        copy.wait_send()
    other_core = 1 - core
    mate_s = s + 1 - 2 * core
    for src, dst, index in (
        (tokens, all_tokens.at[pl.ds(other_core * rows, rows), pl.ds(z * width, width)], 0),
        (
            all_weights.at[pl.ds(mate_s * depth, depth)],
            all_weights.at[pl.ds(mate_s * depth, depth)],
            1,
        ),
        (taps.at[0, 0], all_taps.at[pl.ds(mate_s * lags, lags)], 2),
    ):
        remote(src, dst, mate_send.at[index], mate_recv.at[index], mate).wait_recv()
    for at in range(steps):
        step, chunk = divmod(at, TOKEN_CHUNKS)
        for way in range(2):

            @pl.when(line.sends(way, step))
            def _():
                line.copy(way, step, chunk).wait_send()

            @pl.when(line.receives(way, step))
            def _():
                sign = 1 if way == 0 else -1
                owner = jnp.clip(z - (step + 1) * sign, 0, chan_count - 1)
                to_mate(way, step, chunk, owner).wait_send()
                block = all_tokens.at[
                    pl.ds(other_core * rows + chunk * token_rows, token_rows),
                    pl.ds(owner * width, width),
                ]
                index = 3 + (way * (chan_count - 1) + step) * TOKEN_CHUNKS + chunk
                remote(block, block, mate_send.at[index], mate_recv.at[index], mate).wait_recv()

    for copy in pending:
        copy.wait_send()


def gather_inputs(tokens, weights, taps, chan_count):
    rows, width = tokens.shape
    branches, depth, both = weights.shape
    columns = branches * both // 2
    lags, share = taps.shape[2:]
    mate_count = 3 + 2 * (chan_count - 1) * TOKEN_CHUNKS
    dma = pltpu.SemaphoreType.DMA
    return pl.pallas_call(
        functools.partial(gather_inputs_kernel, chan_count),
        out_shape=(
            jax.ShapeDtypeStruct((2 * rows, chan_count * width), tokens.dtype),
            jax.ShapeDtypeStruct((4 * depth, columns), weights.dtype),
            jax.ShapeDtypeStruct((4 * lags, share), taps.dtype),
        ),
        in_specs=[ANY] * 3,
        out_specs=[ANY] * 3,
        scratch_shapes=[
            pltpu.VMEM((rows, width), tokens.dtype),
            pltpu.VMEM((depth, columns), weights.dtype),
            pltpu.VMEM((lags, share), taps.dtype),
            dma((10,)),
            dma((2, chan_count - 1, TOKEN_CHUNKS)),
            dma((2, chan_count - 1, TOKEN_CHUNKS)),
            dma((mate_count,)),
            dma((mate_count,)),
            dma((2, WEIGHT_CHUNKS)),
            dma((2, WEIGHT_CHUNKS)),
            dma((2, WEIGHT_CHUNKS)),
            dma((2, WEIGHT_CHUNKS)),
            dma((4,)),
            dma((4,)),
        ],
        compiler_params=pltpu.CompilerParams(
            collective_id=0, has_side_effects=True
        ),
        name="gather_inputs",
    )(tokens, weights, taps)


def fourier_tables(length):
    points = 2 * length
    first = 1 << ((points.bit_length() - 1) // 2)
    second = points // first
    kept = first // 2 + 1
    padded = -(-2 * kept // 8) * 8
    low = np.arange(kept)
    place = second * np.arange(first // 2)[None, :] + np.arange(second)[:, None]
    angle = (low[None, :, None] * place[:, None, :] % points) * (2 * np.pi / points)
    outer = np.zeros((second, padded, first // 2))
    outer[:, :kept] = np.cos(angle)
    outer[:, kept : 2 * kept] = -np.sin(angle)
    gain = np.where((low == 0) | (low == first // 2), 1.0, 2.0)[None, None, :] / points
    back = np.zeros((second, first // 2, padded))
    back[:, :, :kept] = np.cos(angle).transpose(0, 2, 1) * gain
    back[:, :, kept : 2 * kept] = -np.sin(angle).transpose(0, 2, 1) * gain
    inner = (np.arange(second)[:, None] * np.arange(second)[None, :] % second) * (
        2 * np.pi / second
    )
    cos, sin = np.cos(inner), np.sin(inner)
    ahead = np.block([[cos, sin], [-sin, cos]])
    behind = np.block([[cos, -sin], [sin, cos]])
    return first, second, kept, padded, [
        jnp.asarray(table, jnp.bfloat16) for table in (outer, ahead, behind, back)
    ]


def conv_phases(
    dims, signal, taps, skip, outer, ahead, behind, back, result, wide, spectra, total
):
    first, second, kept, padded = dims
    length, width = signal.shape
    reach = first // 2
    block = 64
    lanes = 128
    parts = width // lanes

    lanes = 128
    parts = width // lanes

    def ahead_outer():
        @pl.loop(0, length // block)
        def _(at):
            rows = pl.ds(pl.multiple_of(at * block, block), block)
            for part in range(parts):
                cols = pl.ds(part * lanes, lanes)
                wide[part, rows, :] = signal[rows, cols].astype(jnp.float32)
                wide[parts + part, rows, :] = taps[rows, cols].astype(jnp.float32)

        for part in range(parts):
            wide[parts + part, 0:1, :] = (
                wide[parts + part, 0:1, :] + skip[:, part * lanes : (part + 1) * lanes]
            )

        @pl.loop(0, second, unroll=4)
        def _(b):
            picked = jnp.concatenate(
                [wide.at[part][pl.ds(b, reach, stride=second), :] for part in range(2 * parts)],
                axis=1,
            ).astype(jnp.bfloat16)
            found = jnp.dot(outer[b], picked, preferred_element_type=jnp.float32)
            rows = pl.ds(pl.multiple_of(b * padded, 8), padded)
            for part in range(2 * parts):
                spectra[part, rows, :] = found[:, part * lanes : (part + 1) * lanes]

    def inner():
        def strided(start):
            return [
                spectra.at[part][pl.ds(start, second, stride=padded), :] for part in range(2 * parts)
            ]

        @pl.loop(0, kept, unroll=3)
        def _(k):
            real = jnp.concatenate(strided(k), axis=1)
            imag = jnp.concatenate(strided(k + kept), axis=1)
            both = jnp.concatenate([real, imag], axis=0).astype(jnp.bfloat16)
            freq = jnp.dot(ahead[...], both, preferred_element_type=jnp.float32)
            sr, si = freq[:second, :width], freq[second:, :width]
            hr, hi = freq[:second, width:], freq[second:, width:]
            product = jnp.concatenate([sr * hr - si * hi, sr * hi + si * hr], axis=0)
            inv = jnp.dot(
                behind[...], product.astype(jnp.bfloat16), preferred_element_type=jnp.float32
            )
            for part in range(parts):
                cols = slice(part * lanes, (part + 1) * lanes)
                spectra.at[part][pl.ds(k, second, stride=padded), :] = inv[:second, cols]
                spectra.at[part][pl.ds(k + kept, second, stride=padded), :] = inv[second:, cols]

    def back_outer():
        @pl.loop(0, second, unroll=4)
        def _(b):
            rows = pl.ds(pl.multiple_of(b * padded, 8), padded)
            filled = jnp.concatenate([spectra[part, rows, :] for part in range(parts)], axis=1)
            found = jnp.dot(back[b], filled.astype(jnp.bfloat16), preferred_element_type=jnp.float32)
            for part in range(parts):
                total.at[part][pl.ds(b, reach, stride=second), :] = found[
                    :, part * lanes : (part + 1) * lanes
                ]

        @pl.loop(0, length // block)
        def _(at):
            rows = pl.ds(pl.multiple_of(at * block, block), block)
            for part in range(parts):
                result[rows, part * lanes : (part + 1) * lanes] = total[part, rows, :].astype(
                    jnp.bfloat16
                )

    return ahead_outer, inner, back_outer


def long_conv_kernel(dims, *refs):
    for phase in conv_phases(dims, *refs):
        phase()


def long_conv(signal, taps, skip):
    length, width = signal.shape
    first, second, kept, padded, tables = fourier_tables(length)
    return pl.pallas_call(
        functools.partial(long_conv_kernel, (first, second, kept, padded)),
        out_shape=jax.ShapeDtypeStruct((length, width), jnp.bfloat16),
        scratch_shapes=[
            pltpu.VMEM((2 * width // 128, length, 128), jnp.float32),
            pltpu.VMEM((2 * width // 128, second * padded, 128), jnp.float32),
            pltpu.VMEM((width // 128, length, 128), jnp.float32),
        ],
        compiler_params=pltpu.CompilerParams(vmem_limit_bytes=56 * 1024 * 1024),
        cost_estimate=pl.CostEstimate(
            flops=2 * 64 * length * width * 40, bytes_accessed=6 * length * width, transcendentals=0
        ),
        name="long_conv",
    )(signal, taps, skip, *tables)


def mix_and_gather_kernel(
    dims,
    chan_count,
    gated,
    query,
    signal,
    taps,
    skip,
    outer,
    ahead,
    behind,
    back,
    full,
    wide,
    spectra,
    total,
    result,
    crossed,
    ready,
    room,
    local_sem,
    cross_sem,
    mate_send,
    mate_recv,
    line_send,
    line_recv,
):
    y, s, z = (lax.axis_index(name) for name in ("groups", "seq", "chan"))
    x, core = s // 2, s % 2
    mate = (y, s + 1 - 2 * core, z)
    across = (y, (1 - x) * 2 + core, z)
    _, rows, width = gated.shape
    half_chunks = GATED_CHUNKS // 2
    chunk_rows = rows // half_chunks
    greet(
        [
            (mate, True),
            (across, True),
            ((y, s, jnp.minimum(z + 1, chan_count - 1)), z + 1 < chan_count),
            ((y, s, jnp.maximum(z - 1, 0)), z > 0),
        ]
    )

    def column(part, owner, of):
        return ((owner * 2 + of) * 2 + part) * width

    lines = []
    for part in range(2):

        def view(owner, chunk, part=part):
            side, at = divmod(chunk, half_chunks)
            start = column(part, owner, core if side == 0 else 1 - core)
            return full.at[pl.ds(at * chunk_rows, chunk_rows), pl.ds(start, width)]

        lines.append(
            Line(
                view,
                chan_count,
                GATED_CHUNKS,
                line_send.at[part],
                line_recv.at[part],
                lambda to: (y, s, to),
            )
        )
    swaps = []

    def begin(part, source):
        line = lines[part]
        for at in range(half_chunks):
            piece = pl.ds(at * chunk_rows, chunk_rows)
            copy = remote(
                source.at[1 - core, piece],
                full.at[piece, pl.ds(column(part, z, core), width)],
                mate_send.at[part, at],
                mate_recv.at[part, at],
                mate,
            )
            copy.start()
            swaps.append(copy)
        for chunk in range(half_chunks):
            own = source.at[core, pl.ds(chunk * chunk_rows, chunk_rows)]
            for way in range(2):

                @pl.when(line.sends(way, 0))
                def _():
                    line.copy(way, 0, chunk, own).start()

        for at in range(half_chunks):
            block = full.at[
                pl.ds(at * chunk_rows, chunk_rows), pl.ds(column(part, z, 1 - core), width)
            ]
            remote(block, block, mate_send.at[part, at], mate_recv.at[part, at], mate).wait_recv()
            for way in range(2):

                @pl.when(line.sends(way, 0))
                def _():
                    line.copy(way, 0, half_chunks + at).start()

    def relay(part, step):
        line = lines[part]
        for chunk in range(GATED_CHUNKS):
            for way in range(2):

                @pl.when(line.receives(way, step))
                def _():
                    line.arrived(way, step, chunk)

                if step + 1 < chan_count - 1:

                    @pl.when(line.receives(way, step) & line.sends(way, step + 1))
                    def _():
                        line.copy(way, step + 1, chunk).start()

    ahead_outer, inner, back_outer = conv_phases(
        dims, signal, taps, skip, outer, ahead, behind, back, result, wide, spectra, total
    )
    take = pltpu.make_async_copy(gated.at[core], room, local_sem.at[0])
    take.start()
    begin(0, gated)
    take.wait()
    put = pltpu.make_async_copy(
        room, full.at[:, pl.ds(column(0, z, core), width)], local_sem.at[1]
    )
    put.start()
    ahead_outer()
    inner()
    relay(0, 0)
    back_outer()
    positions = 2 * rows
    cross = remote(
        result.at[pl.ds((1 - x) * positions, positions)],
        crossed,
        cross_sem.at[0],
        cross_sem.at[1],
        across,
    )
    cross.start()
    for step in range(1, chan_count - 2):
        relay(0, step)
    cross.wait()
    block = 64
    share = width // 2

    @pl.loop(0, positions // block)
    def _(at):
        start = pl.multiple_of(at * block, block)
        mine = result[pl.ds(pl.multiple_of(x * positions + start, block), block), :]
        other = crossed[pl.ds(start, block), :]
        low = jnp.where(x == 0, mine.astype(jnp.float32), other.astype(jnp.float32))
        high = jnp.where(x == 0, other.astype(jnp.float32), mine.astype(jnp.float32))
        asked = query[pl.ds(start, block), :].astype(jnp.float32)
        to = at // (rows // block)
        row = pl.ds(pl.multiple_of((at - to * (rows // block)) * block, block), block)
        ready[to, row, :share] = (asked[:, :share] * low).astype(jnp.bfloat16)
        ready[to, row, share:] = (asked[:, share:] * high).astype(jnp.bfloat16)

    begin(1, ready)
    last = pltpu.make_async_copy(
        ready.at[core], full.at[:, pl.ds(column(1, z, core), width)], local_sem.at[2]
    )
    last.start()
    relay(0, chan_count - 2)
    for step in range(chan_count - 1):
        relay(1, step)
    put.wait()
    last.wait()
    for copy in swaps:
        copy.wait_send()
    for line in lines:
        for step in range(chan_count - 1):
            for chunk in range(GATED_CHUNKS):
                for way in range(2):

                    @pl.when(line.sends(way, step))
                    def _():
                        line.copy(way, step, chunk).wait_send()


def mix_and_gather(gated, query, signal, taps, skip, chan_count):
    _, rows, width = gated.shape
    length, lanes = signal.shape
    first, second, kept, padded, tables = fourier_tables(length)
    dma = pltpu.SemaphoreType.DMA
    half_chunks = GATED_CHUNKS // 2
    vmem = pl.BlockSpec(memory_space=pltpu.VMEM)
    return pl.pallas_call(
        functools.partial(
            mix_and_gather_kernel, (first, second, kept, padded), chan_count
        ),
        out_shape=jax.ShapeDtypeStruct((rows, 4 * chan_count * width), gated.dtype),
        in_specs=[ANY] + [vmem] * 8,
        out_specs=ANY,
        scratch_shapes=[
            pltpu.VMEM((2 * lanes // 128, length, 128), jnp.float32),
            pltpu.VMEM((2 * lanes // 128, second * padded, 128), jnp.float32),
            pltpu.VMEM((lanes // 128, length, 128), jnp.float32),
            pltpu.VMEM((length, lanes), jnp.bfloat16),
            pltpu.VMEM((2 * rows, lanes), jnp.bfloat16),
            pltpu.VMEM((2, rows, width), jnp.bfloat16),
            pltpu.VMEM((rows, width), gated.dtype),
            dma((3,)),
            dma((2,)),
            dma((2, half_chunks)),
            dma((2, half_chunks)),
            dma((2, 2, chan_count - 1, GATED_CHUNKS)),
            dma((2, 2, chan_count - 1, GATED_CHUNKS)),
        ],
        compiler_params=pltpu.CompilerParams(
            collective_id=1, has_side_effects=True, vmem_limit_bytes=48 * 1024 * 1024
        ),
        name="mix_and_gather",
    )(gated, query, signal, taps, skip, *tables)


def chip_body(tokens, norm_gain, proj_weight, short_filter, long_filter, skip_gain, out_weight):
    seq_count, chan_count = lax.axis_size("seq"), lax.axis_size("chan")
    rows, width = tokens.shape
    depth, branches, local_chan = proj_weight.shape
    half = local_chan // 2
    share = half // 2
    lanes = share // 2
    s = lax.axis_index("seq")
    x, core = s // 2, s % 2
    weights = proj_weight.transpose(1, 0, 2)
    taps = (
        long_filter.astype(jnp.bfloat16)
        .reshape(2, 2, 2, lanes, rows)
        .transpose(0, 2, 4, 1, 3)
        .reshape(2, 2, rows, share)
    )
    whole, all_weights, all_taps = gather_inputs(tokens, weights, taps, chan_count)
    wide = whole.astype(jnp.float32)
    normed = (
        wide * lax.rsqrt(jnp.mean(wide * wide, axis=1, keepdims=True) + EPSILON) * norm_gain
    ).astype(jnp.bfloat16)
    projected = jnp.dot(normed, all_weights, preferred_element_type=jnp.float32).astype(
        jnp.bfloat16
    )
    rim = from_behind(projected[-(SHORT - 1) :], "seq", 2)
    short = lax.dynamic_slice_in_dim(short_filter, core * half, half, 2).reshape(
        SHORT, branches * half
    )
    extended = jnp.concatenate([rim, projected], axis=0).astype(jnp.float32)
    featured = jnp.zeros(projected.shape, jnp.float32)
    for tap in range(SHORT):
        start = SHORT - 1 - tap
        featured = featured + short[tap] * extended[start : start + projected.shape[0]]
    featured = featured.astype(jnp.bfloat16)
    middle = (
        featured[:, half : 2 * half].astype(jnp.float32)
        * featured[:, 2 * half :].astype(jnp.float32)
    ).astype(jnp.bfloat16)
    swap = [(at, (at + 2) % seq_count) for at in range(seq_count)]
    near = x == 0
    skip = lax.dynamic_slice_in_dim(skip_gain, core * half, half, 0).reshape(2, 2, lanes)
    skip = lax.dynamic_index_in_dim(skip, x, 1, keepdims=False)
    def joined(pair, other):
        left, right = pair[:, :lanes], pair[:, lanes:]
        kept = jnp.where(near, left, right)
        return jnp.concatenate(
            [jnp.where(near, kept, other), jnp.where(near, other, kept)], axis=0
        )

    pairs = [middle[:, :share], middle[:, share:]]
    others = [
        lax.ppermute(jnp.where(near, pair[:, lanes:], pair[:, :lanes]), "seq", swap)
        for pair in pairs
    ]
    longer = long_conv(joined(pairs[0], others[0]), all_taps[:, :lanes], skip[:1])
    longer, later = lax.optimization_barrier((longer, others[1]))
    signal = joined(pairs[1], later)
    early, late = longer[: 2 * rows], longer[2 * rows :]
    kept = jnp.where(near, early, late)
    other = lax.ppermute(jnp.where(near, late, early), "seq", swap)
    longer = jnp.concatenate(
        [jnp.where(near, kept, other), jnp.where(near, other, kept)], axis=1
    )
    gated = (featured[:, :share].astype(jnp.float32) * longer.astype(jnp.float32)).astype(
        jnp.bfloat16
    )
    full_mix = mix_and_gather(
        gated.reshape(2, rows, share),
        featured[:, share:half],
        signal,
        all_taps[:, lanes:],
        skip[1:],
        chan_count,
    )
    update = jnp.dot(full_mix, out_weight, preferred_element_type=jnp.float32)
    return (tokens.astype(jnp.float32) + update).astype(jnp.bfloat16)


def select_body(mesh):
    if mesh.shape["seq"] == 4 and mesh.shape["groups"] == 2:
        return chip_body
    return body


def solution(mesh):
    placed = (
        P(("groups", "seq"), "chan"),
        P(),
        P("seq", None, "chan"),
        P(None, None, "chan"),
        P("chan", "seq"),
        P("chan"),
        P(None, "chan"),
    )
    return jax.shard_map(
        select_body(mesh), mesh=mesh, in_specs=placed, out_specs=P(("groups", "seq"), "chan"), check_vma=False
    )
```

profile of v0, /device:TPU:2, one launch (start us, length us, event | category | flops | bytes accessed | tf_op | source)
XLA Modules:
  0.0 239.3 jit_solution(18159319055310198759)
XLA Ops:
  0.0 1.7 convert_element_type.43
  1.7 0.8 copy.16
  2.5 1.5 reshape.31.taps
  4.0 0.0 copy-start.10
  4.0 85.8 %gather_inputs.1 = (bf16[1024,4096]{1,0:T(8,128)(2,1)}, bf16[4096,1536]{1,0:T(8,128)(2,1)}, bf16[2048,256]{1,0:T(8,128)(2,1)}) custom-call(bf16[512,1024]{1,0:T(8,128)(2,1)} %tokens.1, bf16[3,1024,1024]{2,1,0:T(8,128)(2,1)} %bitcast.13, bf16[2,2,512,256]{3,2,1,0:T(8,128)(2,1)} %reshape.31.taps), custom_call_target="tpu_custom_call" | custom-call | tf_op jit(solution)/shard_map/gather_inputs/pallas_call | solution.py:483
  89.9 0.0 copy-start.5
  89.9 5.2 %fusion = f32[1024]{0:T(1024)S(1)} fusion(bf16[1024,4096]{1,0:T(8,128)(2,1)} %get-tuple-element.10), kind=kLoop, calls=%fused_computation.2 | loop fusion | flops 12581888 | bytes 8392704 | tf_op jit(solution)/shard_map/reduce_sum | solution.py:882
  95.1 0.0 copy-done.10
  95.1 0.5 copy-done.5
  95.6 0.0 copy-start.8
  95.6 15.9 %fusion.10 = bf16[1024,1536]{1,0:T(8,128)(2,1)S(1)} fusion(bf16[4096,1536]{1,0:T(8,128)(2,1)} %get-tuple-element.11, bf16[1024,4096]{1,0:T(8,128)(2,1)S(1)} %copy-done.5, f32[4096]{0:T(1024)S(1)} %copy-done.10, f32[1024]{0:T(1024)S(1)} %add_rsqrt_fusion), kind=kOutput, calls=%fused_computation.14 | convolution fusion | flops 12903251968 | bytes 24137728 | tf_op jit(solution)/shard_map/dot_general | solution.py:884
  111.6 1.5 collective-permute-start
  113.1 0.0 copy-done.8
  113.2 3.9 %collective-permute-done = bf16[2,1536]{1,0:T(2,128)(2,1)S(1)} collective-permute-done((bf16[2,1536]{1,0:T(2,128)(2,1)S(1)}, bf16[2,1536]{1,0:T(2,128)(2,1)S(1)}, u32[]{:S(2)}, u32[]{:S(2)}) %collective-permute-start) | collective-permute-done | bytes 6176 | tf_op jit(solution)/shard_map/ppermute | solution.py:22
  117.1 0.9 maximum_convert_fusion
  118.0 0.0 copy-start.6
  118.1 0.0 copy-start.9
  118.1 2.0 fusion.8
  120.1 0.0 copy-start.4
  120.1 0.3 multiply_convert_fusion
  120.4 0.1 collective-permute-start.1
  120.5 1.2 copy-done.4
  121.7 0.0 copy-done.6
  121.7 0.9 fusion.15
  122.6 0.0 copy-done.9
  122.6 0.1 dynamic_slice.11
  122.7 0.5 fusion.13
  123.2 1.1 slice.116.query
  124.3 3.8 %collective-permute-done.1 = bf16[1024,128]{1,0:T(8,128)(2,1)S(1)} collective-permute-done((bf16[1024,128]{1,0:T(8,128)(2,1)S(1)}, bf16[1024,128]{1,0:T(8,128)(2,1)S(1)}, u32[]{:S(2)}, u32[]{:S(2)}) %collective-permute-start.1) | collective-permute-done | bytes 262176 | tf_op jit(solution)/shard_map/ppermute | solution.py:914
  128.1 0.1 broadcast_select_fusion.9
  128.2 0.0 copy-start
  128.2 0.0 copy-start.1
  128.2 0.0 copy-start.2
  128.2 0.0 copy-start.3
  128.2 0.4 collective-permute-start.2
  128.6 0.8 pad_maximum_fusion.refs_0_
  129.4 16.7 %long_conv.1 = bf16[2048,128]{1,0:T(8,128)(2,1)} custom-call(bf16[2048,128]{1,0:T(8,128)(2,1)} %pad_maximum_fusion.refs_0_, bf16[2048,128]{1,0:T(8,128)(2,1)} %get-tuple-element.20.refs_1_, f32[1,128]{1,0:T(1,128)} %get-tuple-element.28.refs_2_, bf16[64,72,32]{2,1,0:T(8,128)(2,1)} %constant.53.clone.refs_3_.outer, ...), custom_call_target="tpu_custom_call" | custom-call | flops 1342177280 | bytes 1572864 | tf_op jit(solution)/shard_map/long_conv/pallas_call | solution.py:633
  146.1 0.0 collective-permute-done.2
  146.1 1.1 broadcast_select_fusion.5
  147.1 1.8 collective-permute-start.3
  148.9 0.1 broadcast_select_fusion.1
  149.0 0.0 copy-start.7
  149.1 4.9 %collective-permute-done.3 = bf16[1024,128]{1,0:T(8,128)(2,1)S(1)} collective-permute-done((bf16[1024,128]{1,0:T(8,128)(2,1)S(1)}, bf16[1024,128]{1,0:T(8,128)(2,1)S(1)}, u32[]{:S(2)}, u32[]{:S(2)}) %collective-permute-start.3) | collective-permute-done | bytes 262176 | tf_op jit(solution)/shard_map/ppermute | solution.py:922
  153.9 1.1 broadcast_select_fusion.4
  155.0 1.2 multiply_convert_fusion.1
  156.2 0.0 copy-done
  156.2 0.0 copy-done.1
  156.2 0.0 copy-done.2
  156.2 0.0 copy-done.3
  156.2 72.9 %mix_and_gather.1 = bf16[512,4096]{1,0:T(8,128)(2,1)} custom-call(bf16[2,512,256]{2,1,0:T(8,128)(2,1)S(1)} %bitcast.12, bf16[1024,256]{1,0:T(8,128)(2,1)S(1)} %slice.116.query, bf16[2048,128]{1,0:T(8,128)(2,1)S(1)} %pad_maximum_fusion.1.signal, bf16[2048,128]{1,0:T(8,128)(2,1)S(1)} %get-tuple-element.19.taps, f32[1,128]{1,0:T(1,128)S(1)} %get-tuple-element.27.skip, ...), custom_call_target="tpu_custom_call" | custom-call | tf_op jit(solution)/shard_map/mix_and_gather/pallas_call | solution.py:834
  229.1 0.0 copy-done.7
  229.2 10.1 %add_convert_fusion = bf16[512,1024]{1,0:T(8,128)(2,1)} fusion(bf16[512,1024]{1,0:T(8,128)(2,1)S(1)} %copy-done.7, bf16[512,4096]{1,0:T(8,128)(2,1)} %mix_and_gather.1, bf16[4096,1024]{1,0:T(8,128)(2,1)} %param.21), kind=kOutput, calls=%fused_computation.16 | convolution fusion | flops 4296540160 | bytes 14680064 | tf_op jit(solution)/shard_map/dot_general | solution.py:937
  (8 shorter events, 0.1 us)
Async XLA Ops:
  4.0 91.1 %copy-start.10 = (f32[4096]{0:T(1024)S(1)}, f32[4096]{0:T(1024)}, u32[]{:S(2)}) copy-start(f32[4096]{0:T(1024)} %param.16) | copy-start | bytes 49156
  89.9 5.8 %copy-start.5 = (bf16[1024,4096]{1,0:T(8,128)(2,1)S(1)}, bf16[1024,4096]{1,0:T(8,128)(2,1)}, u32[]{:S(2)}) copy-start(bf16[1024,4096]{1,0:T(8,128)(2,1)} %get-tuple-element.10) | copy-start | bytes 25165828
  95.6 17.4 %copy-start.8 = (f32[3,3,1024]{2,1,0:T(4,128)S(1)}, f32[3,3,1024]{2,1,0:T(4,128)}, u32[]{:S(2)}) copy-start(f32[3,3,1024]{2,1,0:T(4,128)} %param.18) | copy-start | bytes 110596
  111.6 5.5 %collective-permute-start = (bf16[2,1536]{1,0:T(2,128)(2,1)S(1)}, bf16[2,1536]{1,0:T(2,128)(2,1)S(1)}, u32[]{:S(2)}, u32[]{:S(2)}) collective-permute-start(bf16[2,1536]{1,0:T(2,128)(2,1)S(1)} %slice.105), channel_id=1, source_target_pairs={{0,8},{4,12},{1,9},{5,13},{2,10},{6,14},{3,11},{7,15},{16,24},{20,... | collective-permute-start | bytes 18440 | tf_op jit(solution)/shard_map/ppermute | solution.py:22
  118.0 3.7 %copy-start.6 = (bf16[2048,256]{1,0:T(8,128)(2,1)S(1)}, bf16[2048,256]{1,0:T(8,128)(2,1)}, u32[]{:S(2)}) copy-start(bf16[2048,256]{1,0:T(8,128)(2,1)} %get-tuple-element.12) | copy-start | bytes 3145732
  118.1 4.5 %copy-start.9 = (f32[1024]{0:T(1024)S(1)}, f32[1024]{0:T(1024)}, u32[]{:S(2)}) copy-start(f32[1024]{0:T(1024)} %param.20) | copy-start | bytes 12292
  120.1 1.6 copy-start.4
  120.4 7.7 %collective-permute-start.1 = (bf16[1024,128]{1,0:T(8,128)(2,1)S(1)}, bf16[1024,128]{1,0:T(8,128)(2,1)S(1)}, u32[]{:S(2)}, u32[]{:S(2)}) collective-permute-start(bf16[1024,128]{1,0:T(8,128)(2,1)S(1)} %broadcast_select_fusion.10), channel_id=1, source_target_pairs={{0,8},{4,12},{8,0},{12,4},{1,9},{5,13},{9,1},{13,5},{2,10},{6,14},... | collective-permute-start | bytes 786440 | tf_op jit(solution)/shard_map/ppermute | solution.py:914
  128.2 28.1 %copy-start = (bf16[64,72,32]{2,1,0:T(8,128)(2,1)S(1)}, bf16[64,72,32]{2,1,0:T(8,128)(2,1)}, u32[]{:S(2)}) copy-start(bf16[64,72,32]{2,1,0:T(8,128)(2,1)} %constant.53.clone.refs_3_.outer) | copy-start | bytes 884740
  128.2 28.1 %copy-start.1 = (bf16[64,32,72]{2,1,0:T(8,128)(2,1)S(1)}, bf16[64,32,72]{2,1,0:T(8,128)(2,1)}, u32[]{:S(2)}) copy-start(bf16[64,32,72]{2,1,0:T(8,128)(2,1)} %constant.56.clone.refs_6_.back) | copy-start | bytes 884740
  128.2 28.1 %copy-start.2 = (bf16[128,128]{1,0:T(8,128)(2,1)S(1)}, bf16[128,128]{1,0:T(8,128)(2,1)}, u32[]{:S(2)}) copy-start(bf16[128,128]{1,0:T(8,128)(2,1)} %constant.54.clone.refs_4_.ahead) | copy-start | bytes 98308
  128.2 28.0 %copy-start.3 = (bf16[128,128]{1,0:T(8,128)(2,1)S(1)}, bf16[128,128]{1,0:T(8,128)(2,1)}, u32[]{:S(2)}) copy-start(bf16[128,128]{1,0:T(8,128)(2,1)} %constant.55.clone.refs_5_.behind) | copy-start | bytes 98308
  128.2 17.9 %collective-permute-start.2 = (bf16[1024,128]{1,0:T(8,128)(2,1)S(1)}, bf16[1024,128]{1,0:T(8,128)(2,1)S(1)}, u32[]{:S(2)}, u32[]{:S(2)}) collective-permute-start(bf16[1024,128]{1,0:T(8,128)(2,1)S(1)} %get-tuple-element.21), channel_id=1, source_target_pairs={{0,8},{4,12},{8,0},{12,4},{1,9},{5,13},{9,1},{13,5},{2,10},{6,14},... | collective-permute-start | bytes 786440 | tf_op jit(solution)/shard_map/ppermute | solution.py:914
  147.1 6.8 %collective-permute-start.3 = (bf16[1024,128]{1,0:T(8,128)(2,1)S(1)}, bf16[1024,128]{1,0:T(8,128)(2,1)S(1)}, u32[]{:S(2)}, u32[]{:S(2)}) collective-permute-start(bf16[1024,128]{1,0:T(8,128)(2,1)S(1)} %broadcast_select_fusion.5), channel_id=1, source_target_pairs={{0,8},{4,12},{8,0},{12,4},{1,9},{5,13},{9,1},{13,5},{2,10},{6,14},... | collective-permute-start | bytes 786440 | tf_op jit(solution)/shard_map/ppermute | solution.py:922
  149.0 80.1 %copy-start.7 = (bf16[512,1024]{1,0:T(8,128)(2,1)S(1)}, bf16[512,1024]{1,0:T(8,128)(2,1)}, u32[]{:S(2)}) copy-start(bf16[512,1024]{1,0:T(8,128)(2,1)} %tokens.1) | copy-start | bytes 3145732
where the time goes:
time: 242 us; the launch traced here: 239 us
  Pallas kernels  175 us (72%)
  matrix products  26 us (11%)
  other arithmetic  14.6 us (6%)
  waiting for transfers between devices  12.6 us (5%)
  local copies, waits for them, and re-layouts  6.69 us (3%)
  starting transfers between devices  3.7 us (2%)
    pallas_call x1, Pallas kernels, gather_inputs(): pl.pallas_call(functools.partial(gather_inputs_kernel, chan_count), out_s...  85.8 us
    pallas_call x1, Pallas kernels, mix_and_gather(): pl.pallas_call(functools.partial(mix_and_gather_kernel, (first, second, k...  72.9 us
    pallas_call x1, Pallas kernels, long_conv(): pl.pallas_call(functools.partial(long_conv_kernel, (first, second, kept,...  16.7 us
    dot_general x1, matrix products, chip_body(): jnp.dot(normed, all_weights, preferred_element_type=jnp.float32)  15.9 us
    dot_general x1, matrix products, chip_body(): update = jnp.dot(full_mix, out_weight, preferred_element_type=jnp.float32)  10.1 us
    reduce_sum x1, other arithmetic, chip_body(): jnp.mean(wide * wide, axis=1, keepdims=True) + EPSILON  5.22 us
    ppermute x1, waiting for transfers between devices, chip_body(): other = lax.ppermute(jnp.where(near, late, early), 'seq', swap)  4.87 us
  transfers between devices with their start and end apart: 4, of which 3 were waited for; matrix products, arithmetic and copies ran while one was open for 1% of the time, Pallas kernels for 7%

commit v1 on v0

--- a/solution.py
+++ b/solution.py
@@ -152,7 +152,8 @@
 
 TOKEN_CHUNKS = 8
 WEIGHT_CHUNKS = 16
-GATED_CHUNKS = 4
+LANES = 128
+BLOCK = 128
 ANY = pl.BlockSpec(memory_space=pl.ANY)
 
 
@@ -256,7 +257,7 @@
     beside = (1 - y, s, z)
     rows, width = tokens.shape
     branches, depth, columns = weights.shape[0], weights.shape[1], weights.shape[2] // 2
-    lags = taps.shape[2]
+    lags, share = taps.shape[0], taps.shape[1] // 2
     half, half_lags = depth // 2, lags // 2
 
     greet(
@@ -297,16 +298,20 @@
             def _():
                 line.copy(way, 0, chunk, own).start()
 
-    for to in range(2):
-        copy = remote(
-            taps.at[to, 1 - x, pl.ds(y * half_lags, half_lags)],
+    def taps_across(to):
+        return remote(
+            taps.at[pl.ds(y * half_lags, half_lags), pl.ds(to * share, share)],
             tap_view(s, y),
             f_send.at[to],
             f_recv.at[core],
             across(to),
         )
-        copy.start()
-        pending.append(copy)
+
+    @pl.when(x == 0)
+    def _():
+        for to in range(2):
+            taps_across(to).start()
+
     for chunk in range(WEIGHT_CHUNKS):
         for to in range(2):
             view = weight_view(s, y, chunk)
@@ -336,7 +341,7 @@
             mate,
         ),
         remote(
-            taps.at[1 - core, x],
+            taps.at[:, pl.ds((1 - core) * share, share)],
             all_taps.at[pl.ds(s * lags, lags)],
             mate_send.at[2],
             mate_recv.at[2],
@@ -355,7 +360,7 @@
         ).start()
     ins = [
         pltpu.make_async_copy(tokens, token_room, local_sem.at[0]),
-        pltpu.make_async_copy(taps.at[core, x], tap_room, local_sem.at[1]),
+        pltpu.make_async_copy(taps.at[:, pl.ds(core * share, share)], tap_room, local_sem.at[1]),
     ] + [
         pltpu.make_async_copy(
             weights.at[b, :, pl.ds(core * columns, columns)],
@@ -386,12 +391,17 @@
         index = 3 + (way * (chan_count - 1) + step) * TOKEN_CHUNKS + chunk
         return remote(block, block, mate_send.at[index], mate_recv.at[index], mate)
 
-    for origin in range(2):
-        view = tap_view((1 - x) * 2 + origin, y)
-        remote(view, view, f_send.at[origin], f_recv.at[origin], beside).wait_recv()
-        copy = remote(view, view, f_send.at[2 + origin], f_recv.at[2 + origin], beside)
-        copy.start()
-        pending.append(copy)
+    def taps_beside(origin, part):
+        view = tap_view(origin, part)
+        return remote(view, view, f_send.at[2 + origin], f_recv.at[2 + origin], beside)
+
+    @pl.when(x == 1)
+    def _():
+        for origin in range(2):
+            view = tap_view(origin, y)
+            remote(view, view, f_send.at[origin], f_recv.at[origin], beside).wait_recv()
+            taps_beside(origin, y).start()
+
 
     steps = (chan_count - 1) * TOKEN_CHUNKS
     forwarded = 0
@@ -431,8 +441,18 @@
             remote(
                 view, view, y_send.at[origin, chunk], y_recv.at[origin, chunk], beside
             ).wait_recv()
-        view = tap_view(owner, 1 - y)
-        remote(view, view, f_send.at[2 + origin], f_recv.at[2 + origin], beside).wait_recv()
+
+    @pl.when(x == 1)
+    def _():
+        for origin in range(2):
+            taps_beside(origin, 1 - y).wait_recv()
+            taps_beside(origin, y).wait_send()
+
+    @pl.when(x == 0)
+    def _():
+        for to in range(2):
+            taps_across(to).wait_send()
+
     for copy in outs:
         copy.wait()
     for copy in mate_copies:
@@ -446,7 +466,7 @@
             all_weights.at[pl.ds(mate_s * depth, depth)],
             1,
         ),
-        (taps.at[0, 0], all_taps.at[pl.ds(mate_s * lags, lags)], 2),
+        (all_taps.at[pl.ds(mate_s * lags, lags)], all_taps.at[pl.ds(mate_s * lags, lags)], 2),
     ):
         remote(src, dst, mate_send.at[index], mate_recv.at[index], mate).wait_recv()
     for at in range(steps):
@@ -477,7 +497,7 @@
     rows, width = tokens.shape
     branches, depth, both = weights.shape
     columns = branches * both // 2
-    lags, share = taps.shape[2:]
+    lags, share = taps.shape[0], taps.shape[1] // 2
     mate_count = 3 + 2 * (chan_count - 1) * TOKEN_CHUNKS
     dma = pltpu.SemaphoreType.DMA
     return pl.pallas_call(
@@ -512,162 +532,43 @@
     )(tokens, weights, taps)
 
 
-def fourier_tables(length):
-    points = 2 * length
-    first = 1 << ((points.bit_length() - 1) // 2)
-    second = points // first
-    kept = first // 2 + 1
-    padded = -(-2 * kept // 8) * 8
-    low = np.arange(kept)
-    place = second * np.arange(first // 2)[None, :] + np.arange(second)[:, None]
-    angle = (low[None, :, None] * place[:, None, :] % points) * (2 * np.pi / points)
-    outer = np.zeros((second, padded, first // 2))
-    outer[:, :kept] = np.cos(angle)
-    outer[:, kept : 2 * kept] = -np.sin(angle)
-    gain = np.where((low == 0) | (low == first // 2), 1.0, 2.0)[None, None, :] / points
-    back = np.zeros((second, first // 2, padded))
-    back[:, :, :kept] = np.cos(angle).transpose(0, 2, 1) * gain
-    back[:, :, kept : 2 * kept] = -np.sin(angle).transpose(0, 2, 1) * gain
-    inner = (np.arange(second)[:, None] * np.arange(second)[None, :] % second) * (
-        2 * np.pi / second
-    )
-    cos, sin = np.cos(inner), np.sin(inner)
-    ahead = np.block([[cos, sin], [-sin, cos]])
-    behind = np.block([[cos, -sin], [sin, cos]])
-    return first, second, kept, padded, [
-        jnp.asarray(table, jnp.bfloat16) for table in (outer, ahead, behind, back)
-    ]
-
-
-def conv_phases(
-    dims, signal, taps, skip, outer, ahead, behind, back, result, wide, spectra, total
-):
-    first, second, kept, padded = dims
-    length, width = signal.shape
-    reach = first // 2
-    block = 64
-    lanes = 128
-    parts = width // lanes
-
-    lanes = 128
-    parts = width // lanes
-
-    def ahead_outer():
-        @pl.loop(0, length // block)
-        def _(at):
-            rows = pl.ds(pl.multiple_of(at * block, block), block)
-            for part in range(parts):
-                cols = pl.ds(part * lanes, lanes)
-                wide[part, rows, :] = signal[rows, cols].astype(jnp.float32)
-                wide[parts + part, rows, :] = taps[rows, cols].astype(jnp.float32)
-
-        for part in range(parts):
-            wide[parts + part, 0:1, :] = (
-                wide[parts + part, 0:1, :] + skip[:, part * lanes : (part + 1) * lanes]
-            )
-
-        @pl.loop(0, second, unroll=4)
-        def _(b):
-            picked = jnp.concatenate(
-                [wide.at[part][pl.ds(b, reach, stride=second), :] for part in range(2 * parts)],
-                axis=1,
-            ).astype(jnp.bfloat16)
-            found = jnp.dot(outer[b], picked, preferred_element_type=jnp.float32)
-            rows = pl.ds(pl.multiple_of(b * padded, 8), padded)
-            for part in range(2 * parts):
-                spectra[part, rows, :] = found[:, part * lanes : (part + 1) * lanes]
-
-    def inner():
-        def strided(start):
-            return [
-                spectra.at[part][pl.ds(start, second, stride=padded), :] for part in range(2 * parts)
-            ]
-
-        @pl.loop(0, kept, unroll=3)
-        def _(k):
-            real = jnp.concatenate(strided(k), axis=1)
-            imag = jnp.concatenate(strided(k + kept), axis=1)
-            both = jnp.concatenate([real, imag], axis=0).astype(jnp.bfloat16)
-            freq = jnp.dot(ahead[...], both, preferred_element_type=jnp.float32)
-            sr, si = freq[:second, :width], freq[second:, :width]
-            hr, hi = freq[:second, width:], freq[second:, width:]
-            product = jnp.concatenate([sr * hr - si * hi, sr * hi + si * hr], axis=0)
-            inv = jnp.dot(
-                behind[...], product.astype(jnp.bfloat16), preferred_element_type=jnp.float32
-            )
-            for part in range(parts):
-                cols = slice(part * lanes, (part + 1) * lanes)
-                spectra.at[part][pl.ds(k, second, stride=padded), :] = inv[:second, cols]
-                spectra.at[part][pl.ds(k + kept, second, stride=padded), :] = inv[second:, cols]
-
-    def back_outer():
-        @pl.loop(0, second, unroll=4)
-        def _(b):
-            rows = pl.ds(pl.multiple_of(b * padded, 8), padded)
-            filled = jnp.concatenate([spectra[part, rows, :] for part in range(parts)], axis=1)
-            found = jnp.dot(back[b], filled.astype(jnp.bfloat16), preferred_element_type=jnp.float32)
-            for part in range(parts):
-                total.at[part][pl.ds(b, reach, stride=second), :] = found[
-                    :, part * lanes : (part + 1) * lanes
-                ]
-
-        @pl.loop(0, length // block)
-        def _(at):
-            rows = pl.ds(pl.multiple_of(at * block, block), block)
-            for part in range(parts):
-                result[rows, part * lanes : (part + 1) * lanes] = total[part, rows, :].astype(
-                    jnp.bfloat16
-                )
-
-    return ahead_outer, inner, back_outer
-
-
-def long_conv_kernel(dims, *refs):
-    for phase in conv_phases(dims, *refs):
-        phase()
-
-
-def long_conv(signal, taps, skip):
-    length, width = signal.shape
-    first, second, kept, padded, tables = fourier_tables(length)
-    return pl.pallas_call(
-        functools.partial(long_conv_kernel, (first, second, kept, padded)),
-        out_shape=jax.ShapeDtypeStruct((length, width), jnp.bfloat16),
-        scratch_shapes=[
-            pltpu.VMEM((2 * width // 128, length, 128), jnp.float32),
-            pltpu.VMEM((2 * width // 128, second * padded, 128), jnp.float32),
-            pltpu.VMEM((width // 128, length, 128), jnp.float32),
-        ],
-        compiler_params=pltpu.CompilerParams(vmem_limit_bytes=56 * 1024 * 1024),
-        cost_estimate=pl.CostEstimate(
-            flops=2 * 64 * length * width * 40, bytes_accessed=6 * length * width, transcendentals=0
-        ),
-        name="long_conv",
-    )(signal, taps, skip, *tables)
-
-
-def mix_and_gather_kernel(
-    dims,
+def wave_table(rows):
+    place = 2 * np.arange(rows) + 1
+    angle = (place[:, None] * place[None, :] % (8 * rows)) * (np.pi / (4 * rows))
+    return jnp.asarray(np.concatenate([np.cos(angle), np.sin(angle)], axis=0), jnp.bfloat16)
+
+
+def mixer_kernel(
     chan_count,
-    gated,
+    projected,
+    short,
+    skip,
+    taps,
+    table_hbm,
+    tokens,
+    out_weight,
+    result,
+    table,
+    tap_room,
+    weight_room,
+    token_room,
+    edge,
+    extended,
     query,
     signal,
-    taps,
-    skip,
-    outer,
-    ahead,
-    behind,
-    back,
+    before,
+    turn,
+    early,
+    late,
+    freq,
+    mixed,
+    ready,
     full,
-    wide,
-    spectra,
     total,
-    result,
-    crossed,
-    ready,
-    room,
     local_sem,
-    cross_sem,
+    edge_sem,
+    before_send,
+    before_recv,
     mate_send,
     mate_recv,
     line_send,
@@ -677,9 +578,24 @@
     x, core = s // 2, s % 2
     mate = (y, s + 1 - 2 * core, z)
     across = (y, (1 - x) * 2 + core, z)
-    _, rows, width = gated.shape
-    half_chunks = GATED_CHUNKS // 2
-    chunk_rows = rows // half_chunks
+    length = projected.shape[0]
+    share = projected.shape[1] // 3
+    rows = length // 2
+    groups = share // LANES
+    rim = edge.shape[0]
+    steps = chan_count - 1
+
+    def local(index, src, dst):
+        return pltpu.make_async_copy(src, dst, local_sem.at[index])
+
+    loads = [
+        local(0, table_hbm, table),
+        local(1, taps, tap_room),
+        local(2, tokens, token_room),
+        local(3, out_weight, weight_room),
+    ]
+    for copy in loads:
+        copy.start()
     greet(
         [
             (mate, True),
@@ -688,194 +604,353 @@
             ((y, s, jnp.maximum(z - 1, 0)), z > 0),
         ]
     )
-
-    def column(part, owner, of):
-        return ((owner * 2 + of) * 2 + part) * width
-
-    lines = []
-    for part in range(2):
-
-        def view(owner, chunk, part=part):
-            side, at = divmod(chunk, half_chunks)
-            start = column(part, owner, core if side == 0 else 1 - core)
-            return full.at[pl.ds(at * chunk_rows, chunk_rows), pl.ds(start, width)]
-
-        lines.append(
-            Line(
-                view,
-                chan_count,
-                GATED_CHUNKS,
-                line_send.at[part],
-                line_recv.at[part],
-                lambda to: (y, s, to),
+    rim_copy = remote(
+        projected.at[pl.ds(length - rim, rim)], edge, edge_sem.at[0], edge_sem.at[1], across
+    )
+
+    @pl.when(x == 0)
+    def _():
+        rim_copy.start()
+
+    def before_copy(g):
+        return remote(
+            signal.at[g], before.at[g], before_send.at[g], before_recv.at[g], across
+        )
+
+    def swap_copy(g):
+        return remote(
+            ready.at[g], full.at[z, g, core], mate_send.at[g], mate_recv.at[g], mate
+        )
+
+    def sends(way, step):
+        if way == 0:
+            return (z - step >= 0) & (z + 1 < chan_count)
+        return (z + step < chan_count) & (z - 1 >= 0)
+
+    def receives(way, step):
+        if way == 0:
+            return z - 1 - step >= 0
+        return z + 1 + step < chan_count
+
+    def line_copy(way, step, g, of):
+        sign = 1 if way == 0 else -1
+        owner = jnp.clip(z - step * sign, 0, chan_count - 1)
+        target = jnp.clip(z + sign, 0, chan_count - 1)
+        block = full.at[owner, g, of]
+        return remote(
+            block,
+            block,
+            line_send.at[way, step, g, of],
+            line_recv.at[way, step, g, of],
+            (y, s, target),
+        )
+
+    def line_arrived(way, step, g, of):
+        sign = 1 if way == 0 else -1
+        owner = jnp.clip(z - (step + 1) * sign, 0, chan_count - 1)
+        block = full.at[owner, g, of]
+        remote(
+            block,
+            block,
+            line_send.at[way, step, g, of],
+            line_recv.at[way, step, g, of],
+            (y, s, z),
+        ).wait_recv()
+        return owner
+
+    def blocks(count):
+        return pl.loop(0, count // BLOCK)
+
+    def at_rows(i, base=0):
+        return pl.ds(pl.multiple_of(base + i * BLOCK, BLOCK), BLOCK)
+
+    def lanes_of(base, g):
+        return pl.ds(pl.multiple_of(base + g * LANES, LANES), LANES)
+
+    span = 2 * BLOCK
+
+    def spectrum(column):
+        @pl.loop(0, 2 * length // span)
+        def _(i):
+            at = pl.ds(pl.multiple_of(i * span, span), span)
+            freq[at, :] = jnp.dot(table[at, :], column(), preferred_element_type=jnp.float32)
+
+    @blocks(length)
+    def _(i):
+        place = lax.broadcasted_iota(jnp.int32, (BLOCK, LANES), 0) + i * BLOCK
+        angle = (2 * place + 1).astype(jnp.float32) * (math.pi / (4 * length))
+        turn[0, at_rows(i), :] = jnp.cos(angle)
+        turn[1, at_rows(i), :] = jnp.sin(angle)
+
+    loads[2].wait()
+
+    @blocks(rows)
+    def _(i):
+        total[at_rows(i), :] = token_room[at_rows(i), :].astype(jnp.float32)
+
+    loads[0].wait()
+    loads[1].wait()
+
+    @pl.when(x == 1)
+    def _():
+        rim_copy.wait_recv()
+
+    @pl.when(x == 0)
+    def _():
+        edge[...] = jnp.zeros(edge.shape, edge.dtype)
+
+    def featurize(g):
+        for b in range(3):
+            cols = lanes_of(b * share, g)
+            extended[b, 0:rim, :] = edge[:, cols].astype(jnp.float32)
+
+            @blocks(length)
+            def _(i):
+                extended[b, pl.ds(pl.multiple_of(rim + i * BLOCK, rim), BLOCK), :] = projected[at_rows(i), cols].astype(jnp.float32)
+
+        chosen = lanes_of(core * share, g)
+        weight = [[short[tap, b : b + 1, chosen] for b in range(3)] for tap in range(SHORT)]
+
+        @blocks(length)
+        def _(i):
+            found = []
+            for b in range(3):
+                value = jnp.zeros((BLOCK, LANES), jnp.float32)
+                for tap in range(SHORT):
+                    value = value + weight[tap][b] * extended[
+                        b, pl.ds(rim - tap + i * BLOCK, BLOCK), :
+                    ]
+                found.append(value.astype(jnp.bfloat16))
+            query[at_rows(i), :] = found[0]
+            signal[g, at_rows(i), :] = (
+                found[1].astype(jnp.float32) * found[2].astype(jnp.float32)
+            ).astype(jnp.bfloat16)
+
+    def tap_spectra(g):
+        scale = 1.0 / length
+        cols = lanes_of(0, g)
+
+        def turned(i):
+            low, high = at_rows(i), at_rows(i, length)
+            real, imag = freq[low, :], -freq[high, :]
+            cos, sin = turn[0, low, :], turn[1, low, :]
+            return (cos * real - sin * imag) * scale, (cos * imag + sin * real) * scale
+
+        spectrum(lambda: tap_room[0:length, cols])
+
+        @blocks(length)
+        def _(i):
+            early[0, at_rows(i), :], early[1, at_rows(i), :] = turned(i)
+
+        @pl.when(x == 1)
+        def _():
+            spectrum(lambda: tap_room[length : 2 * length, cols])
+
+            @blocks(length)
+            def _(i):
+                real, imag = turned(i)
+                place = lax.broadcasted_iota(jnp.int32, (BLOCK, LANES), 0)
+                sign = (1 - 2 * (place % 2)).astype(jnp.float32)
+                late[0, at_rows(i), :] = real - sign * early[1, at_rows(i), :]
+                late[1, at_rows(i), :] = imag + sign * early[0, at_rows(i), :]
+
+    def product(i, other):
+        low, high = at_rows(i), at_rows(i, length)
+        cos, sin = freq[low, :], freq[high, :]
+        real, imag = other[0, low, :], other[1, low, :]
+        return cos * real + sin * imag, sin * real - cos * imag
+
+    def convolve(g):
+        spectrum(lambda: signal[g])
+
+        @blocks(length)
+        def _(i):
+            mixed[at_rows(i), :], mixed[at_rows(i, length), :] = product(i, early)
+
+        @pl.when(x == 1)
+        def _():
+            before_copy(g).wait_recv()
+            spectrum(lambda: before[g])
+
+            @blocks(length)
+            def _(i):
+                real, imag = product(i, late)
+                mixed[at_rows(i), :] += real
+                mixed[at_rows(i, length), :] += imag
+
+        @pl.loop(0, length // span)
+        def _(i):
+            low = pl.ds(pl.multiple_of(i * span, span), span)
+            high = pl.ds(pl.multiple_of(length + i * span, span), span)
+            freq[low, :] = jnp.dot(
+                table[low, :], mixed[:length, :].astype(jnp.bfloat16),
+                preferred_element_type=jnp.float32,
+            ) + jnp.dot(
+                table[high, :], mixed[length:, :].astype(jnp.bfloat16),
+                preferred_element_type=jnp.float32,
             )
-        )
-    swaps = []
-
-    def begin(part, source):
-        line = lines[part]
-        for at in range(half_chunks):
-            piece = pl.ds(at * chunk_rows, chunk_rows)
-            copy = remote(
-                source.at[1 - core, piece],
-                full.at[piece, pl.ds(column(part, z, core), width)],
-                mate_send.at[part, at],
-                mate_recv.at[part, at],
-                mate,
+
+        gain = skip[:, lanes_of(core * share, g)]
+
+        def gated(at):
+            longer = freq[at, :] + gain * signal[g, at, :].astype(jnp.float32)
+            longer = longer.astype(jnp.bfloat16).astype(jnp.float32)
+            return (query[at, :].astype(jnp.float32) * longer).astype(jnp.bfloat16)
+
+        @blocks(rows)
+        def _(i):
+            full[z, g, core, at_rows(i), :] = gated(
+                pl.ds(pl.multiple_of(core * rows + i * BLOCK, BLOCK), BLOCK)
             )
-            copy.start()
-            swaps.append(copy)
-        for chunk in range(half_chunks):
-            own = source.at[core, pl.ds(chunk * chunk_rows, chunk_rows)]
-            for way in range(2):
-
-                @pl.when(line.sends(way, 0))
+            ready[g, at_rows(i), :] = gated(
+                pl.ds(pl.multiple_of((1 - core) * rows + i * BLOCK, BLOCK), BLOCK)
+            )
+
+    def accumulate(owner, g):
+        left = pl.ds(pl.multiple_of(owner * 2 * share + g * LANES, LANES), LANES)
+        right = pl.ds(pl.multiple_of((owner * 2 + 1) * share + g * LANES, LANES), LANES)
+
+        @pl.loop(0, total.shape[1] // span)
+        def _(i):
+            cols = pl.ds(pl.multiple_of(i * span, span), span)
+            block = jnp.concatenate([full[owner, g, 0], full[owner, g, 1]], axis=1)
+            weight = jnp.concatenate([weight_room[left, cols], weight_room[right, cols]], axis=0)
+            total[:, cols] += jnp.dot(block, weight, preferred_element_type=jnp.float32)
+
+    def begin(g):
+        swap_copy(g).start()
+        for way in range(2):
+
+            @pl.when(sends(way, 0))
+            def _():
+                line_copy(way, 0, g, core).start()
+
+        other = full.at[z, g, 1 - core]
+        remote(other, other, mate_send.at[g], mate_recv.at[g], mate).wait_recv()
+        for way in range(2):
+
+            @pl.when(sends(way, 0))
+            def _():
+                line_copy(way, 0, g, 1 - core).start()
+
+    def relay(step, g):
+        for way in range(2):
+
+            @pl.when(receives(way, step))
+            def _():
+                for of in range(2):
+                    owner = line_arrived(way, step, g, of)
+                    if step + 1 < steps:
+
+                        @pl.when(sends(way, step + 1))
+                        def _():
+                            line_copy(way, step + 1, g, of).start()
+
+                accumulate(owner, g)
+
+    @pl.loop(0, groups + steps)
+    def _(g):
+        @pl.when(g < groups)
+        def _():
+            featurize(g)
+
+            @pl.when(x == 0)
+            def _():
+                before_copy(g).start()
+
+            tap_spectra(g)
+            convolve(g)
+            begin(g)
+
+            @pl.when(g == 0)
+            def _():
+                loads[3].wait()
+
+            accumulate(z, g)
+
+        for step in range(steps):
+            at = g - 1 - step
+
+            @pl.when((at >= 0) & (at < groups))
+            def _():
+                relay(step, at)
+
+    @blocks(rows)
+    def _(i):
+        result[at_rows(i), :] = total[at_rows(i), :].astype(jnp.bfloat16)
+
+    @pl.when(x == 0)
+    def _():
+        rim_copy.wait_send()
+
+    for g in range(groups):
+        swap_copy(g).wait_send()
+
+        @pl.when(x == 0)
+        def _():
+            before_copy(g).wait_send()
+
+        for way in range(2):
+            for step in range(steps):
+
+                @pl.when(sends(way, step))
                 def _():
-                    line.copy(way, 0, chunk, own).start()
-
-        for at in range(half_chunks):
-            block = full.at[
-                pl.ds(at * chunk_rows, chunk_rows), pl.ds(column(part, z, 1 - core), width)
-            ]
-            remote(block, block, mate_send.at[part, at], mate_recv.at[part, at], mate).wait_recv()
-            for way in range(2):
-
-                @pl.when(line.sends(way, 0))
-                def _():
-                    line.copy(way, 0, half_chunks + at).start()
-
-    def relay(part, step):
-        line = lines[part]
-        for chunk in range(GATED_CHUNKS):
-            for way in range(2):
-
-                @pl.when(line.receives(way, step))
-                def _():
-                    line.arrived(way, step, chunk)
-
-                if step + 1 < chan_count - 1:
-
-                    @pl.when(line.receives(way, step) & line.sends(way, step + 1))
-                    def _():
-                        line.copy(way, step + 1, chunk).start()
-
-    ahead_outer, inner, back_outer = conv_phases(
-        dims, signal, taps, skip, outer, ahead, behind, back, result, wide, spectra, total
-    )
-    take = pltpu.make_async_copy(gated.at[core], room, local_sem.at[0])
-    take.start()
-    begin(0, gated)
-    take.wait()
-    put = pltpu.make_async_copy(
-        room, full.at[:, pl.ds(column(0, z, core), width)], local_sem.at[1]
-    )
-    put.start()
-    ahead_outer()
-    inner()
-    relay(0, 0)
-    back_outer()
-    positions = 2 * rows
-    cross = remote(
-        result.at[pl.ds((1 - x) * positions, positions)],
-        crossed,
-        cross_sem.at[0],
-        cross_sem.at[1],
-        across,
-    )
-    cross.start()
-    for step in range(1, chan_count - 2):
-        relay(0, step)
-    cross.wait()
-    block = 64
-    share = width // 2
-
-    @pl.loop(0, positions // block)
-    def _(at):
-        start = pl.multiple_of(at * block, block)
-        mine = result[pl.ds(pl.multiple_of(x * positions + start, block), block), :]
-        other = crossed[pl.ds(start, block), :]
-        low = jnp.where(x == 0, mine.astype(jnp.float32), other.astype(jnp.float32))
-        high = jnp.where(x == 0, other.astype(jnp.float32), mine.astype(jnp.float32))
-        asked = query[pl.ds(start, block), :].astype(jnp.float32)
-        to = at // (rows // block)
-        row = pl.ds(pl.multiple_of((at - to * (rows // block)) * block, block), block)
-        ready[to, row, :share] = (asked[:, :share] * low).astype(jnp.bfloat16)
-        ready[to, row, share:] = (asked[:, share:] * high).astype(jnp.bfloat16)
-
-    begin(1, ready)
-    last = pltpu.make_async_copy(
-        ready.at[core], full.at[:, pl.ds(column(1, z, core), width)], local_sem.at[2]
-    )
-    last.start()
-    relay(0, chan_count - 2)
-    for step in range(chan_count - 1):
-        relay(1, step)
-    put.wait()
-    last.wait()
-    for copy in swaps:
-        copy.wait_send()
-    for line in lines:
-        for step in range(chan_count - 1):
-            for chunk in range(GATED_CHUNKS):
-                for way in range(2):
-
-                    @pl.when(line.sends(way, step))
-                    def _():
-                        line.copy(way, step, chunk).wait_send()
-
-
-def mix_and_gather(gated, query, signal, taps, skip, chan_count):
-    _, rows, width = gated.shape
-    length, lanes = signal.shape
-    first, second, kept, padded, tables = fourier_tables(length)
+                    for of in range(2):
+                        line_copy(way, step, g, of).wait_send()
+
+
+def mixer(projected, short, skip, taps, tokens, out_weight, chan_count):
+    length, columns = projected.shape
+    share = columns // 3
+    rows, width = tokens.shape
+    groups = share // LANES
+    steps = chan_count - 1
     dma = pltpu.SemaphoreType.DMA
-    half_chunks = GATED_CHUNKS // 2
+    f32, bf16 = jnp.float32, jnp.bfloat16
     vmem = pl.BlockSpec(memory_space=pltpu.VMEM)
     return pl.pallas_call(
-        functools.partial(
-            mix_and_gather_kernel, (first, second, kept, padded), chan_count
-        ),
-        out_shape=jax.ShapeDtypeStruct((rows, 4 * chan_count * width), gated.dtype),
-        in_specs=[ANY] + [vmem] * 8,
-        out_specs=ANY,
+        functools.partial(mixer_kernel, chan_count),
+        out_shape=jax.ShapeDtypeStruct((rows, width), bf16),
+        in_specs=[vmem, vmem, vmem] + [ANY] * 4,
+        out_specs=vmem,
         scratch_shapes=[
-            pltpu.VMEM((2 * lanes // 128, length, 128), jnp.float32),
-            pltpu.VMEM((2 * lanes // 128, second * padded, 128), jnp.float32),
-            pltpu.VMEM((lanes // 128, length, 128), jnp.float32),
-            pltpu.VMEM((length, lanes), jnp.bfloat16),
-            pltpu.VMEM((2 * rows, lanes), jnp.bfloat16),
-            pltpu.VMEM((2, rows, width), jnp.bfloat16),
-            pltpu.VMEM((rows, width), gated.dtype),
-            dma((3,)),
+            pltpu.VMEM((2 * length, length), bf16),
+            pltpu.VMEM(taps.shape, bf16),
+            pltpu.VMEM(out_weight.shape, bf16),
+            pltpu.VMEM(tokens.shape, bf16),
+            pltpu.VMEM((16, columns), bf16),
+            pltpu.VMEM((3, length + 16, LANES), f32),
+            pltpu.VMEM((length, LANES), bf16),
+            pltpu.VMEM((groups, length, LANES), bf16),
+            pltpu.VMEM((groups, length, LANES), bf16),
+            pltpu.VMEM((2, length, LANES), f32),
+            pltpu.VMEM((2, length, LANES), f32),
+            pltpu.VMEM((2, length, LANES), f32),
+            pltpu.VMEM((2 * length, LANES), f32),
+            pltpu.VMEM((2 * length, LANES), f32),
+            pltpu.VMEM((groups, rows, LANES), bf16),
+            pltpu.VMEM((chan_count, groups, 2, rows, LANES), bf16),
+            pltpu.VMEM((rows, width), f32),
+            dma((4,)),
             dma((2,)),
-            dma((2, half_chunks)),
-            dma((2, half_chunks)),
-            dma((2, 2, chan_count - 1, GATED_CHUNKS)),
-            dma((2, 2, chan_count - 1, GATED_CHUNKS)),
+            dma((groups,)),
+            dma((groups,)),
+            dma((groups,)),
+            dma((groups,)),
+            dma((2, steps, groups, 2)),
+            dma((2, steps, groups, 2)),
         ],
         compiler_params=pltpu.CompilerParams(
-            collective_id=1, has_side_effects=True, vmem_limit_bytes=48 * 1024 * 1024
+            collective_id=1, has_side_effects=True, vmem_limit_bytes=50 * 1024 * 1024
         ),
-        name="mix_and_gather",
-    )(gated, query, signal, taps, skip, *tables)
+        name="mixer",
+    )(projected, short, skip, taps, wave_table(length), tokens, out_weight)
 
 
 def chip_body(tokens, norm_gain, proj_weight, short_filter, long_filter, skip_gain, out_weight):
-    seq_count, chan_count = lax.axis_size("seq"), lax.axis_size("chan")
-    rows, width = tokens.shape
-    depth, branches, local_chan = proj_weight.shape
-    half = local_chan // 2
-    share = half // 2
-    lanes = share // 2
-    s = lax.axis_index("seq")
-    x, core = s // 2, s % 2
+    chan_count = lax.axis_size("chan")
     weights = proj_weight.transpose(1, 0, 2)
-    taps = (
-        long_filter.astype(jnp.bfloat16)
-        .reshape(2, 2, 2, lanes, rows)
-        .transpose(0, 2, 4, 1, 3)
-        .reshape(2, 2, rows, share)
-    )
+    taps = long_filter.astype(jnp.bfloat16).T
     whole, all_weights, all_taps = gather_inputs(tokens, weights, taps, chan_count)
     wide = whole.astype(jnp.float32)
     normed = (
@@ -884,58 +959,9 @@
     projected = jnp.dot(normed, all_weights, preferred_element_type=jnp.float32).astype(
         jnp.bfloat16
     )
-    rim = from_behind(projected[-(SHORT - 1) :], "seq", 2)
-    short = lax.dynamic_slice_in_dim(short_filter, core * half, half, 2).reshape(
-        SHORT, branches * half
-    )
-    extended = jnp.concatenate([rim, projected], axis=0).astype(jnp.float32)
-    featured = jnp.zeros(projected.shape, jnp.float32)
-    for tap in range(SHORT):
-        start = SHORT - 1 - tap
-        featured = featured + short[tap] * extended[start : start + projected.shape[0]]
-    featured = featured.astype(jnp.bfloat16)
-    middle = (
-        featured[:, half : 2 * half].astype(jnp.float32)
-        * featured[:, 2 * half :].astype(jnp.float32)
-    ).astype(jnp.bfloat16)
-    swap = [(at, (at + 2) % seq_count) for at in range(seq_count)]
-    near = x == 0
-    skip = lax.dynamic_slice_in_dim(skip_gain, core * half, half, 0).reshape(2, 2, lanes)
-    skip = lax.dynamic_index_in_dim(skip, x, 1, keepdims=False)
-    def joined(pair, other):
-        left, right = pair[:, :lanes], pair[:, lanes:]
-        kept = jnp.where(near, left, right)
-        return jnp.concatenate(
-            [jnp.where(near, kept, other), jnp.where(near, other, kept)], axis=0
-        )
-
-    pairs = [middle[:, :share], middle[:, share:]]
-    others = [
-        lax.ppermute(jnp.where(near, pair[:, lanes:], pair[:, :lanes]), "seq", swap)
-        for pair in pairs
-    ]
-    longer = long_conv(joined(pairs[0], others[0]), all_taps[:, :lanes], skip[:1])
-    longer, later = lax.optimization_barrier((longer, others[1]))
-    signal = joined(pairs[1], later)
-    early, late = longer[: 2 * rows], longer[2 * rows :]
-    kept = jnp.where(near, early, late)
-    other = lax.ppermute(jnp.where(near, late, early), "seq", swap)
-    longer = jnp.concatenate(
-        [jnp.where(near, kept, other), jnp.where(near, other, kept)], axis=1
-    )
-    gated = (featured[:, :share].astype(jnp.float32) * longer.astype(jnp.float32)).astype(
-        jnp.bfloat16
-    )
-    full_mix = mix_and_gather(
-        gated.reshape(2, rows, share),
-        featured[:, share:half],
-        signal,
-        all_taps[:, lanes:],
-        skip[1:],
-        chan_count,
-    )
-    update = jnp.dot(full_mix, out_weight, preferred_element_type=jnp.float32)
-    return (tokens.astype(jnp.float32) + update).astype(jnp.bfloat16)
+    return mixer(
+        projected, short_filter, skip_gain[None, :], all_taps, tokens, out_weight, chan_count
+    )
 
 
 def select_body(mesh):

time: 242 us -> 226 us (0.934); the launches traced: 239 us -> 226 us
  Pallas kernels: 175 us -> 200 us
  waiting for transfers between devices: 12.6 us -> 0 us
  other arithmetic: 14.6 us -> 5.23 us
  matrix products: 26 us -> 17 us
  starting transfers between devices: 3.7 us -> 0 us
  local copies, waits for them, and re-layouts: 6.69 us -> 4.04 us
    pallas_call x2 -> x1, Pallas kernels: 89.6 us -> 109 us  [mixer(): pl.pallas_call(functools.partial(mixer_kernel, chan_count), out_shape=jax...]
    ppermute x4 -> x0, waiting for transfers between devices: 12.6 us -> none  [the longest x1 4.87 us: chip_body(): other = lax.ppermute(jnp.where(near, late, early), 'seq', swap)]
    dot_general x1 -> x0, matrix products: 10.1 us -> none  [chip_body(): update = jnp.dot(full_mix, out_weight, preferred_element_type=jnp.float32)]
    convert_element_type x5 -> x0, other arithmetic: 6.14 us -> none  [the longest x1 2 us: chip_body(): featured = featured.astype(jnp.bfloat16)]
    pallas_call x1, Pallas kernels: 85.8 us -> 91.4 us  [gather_inputs(): pl.pallas_call(functools.partial(gather_inputs_kernel, chan_count), out_s...]
    ppermute x4 -> x0, starting transfers between devices: 3.7 us -> none  [the longest x1 1.81 us: chip_body(): other = lax.ppermute(jnp.where(near, late, early), 'seq', swap)]
    slice x5 -> x0, local copies, waits for them, and re-layouts: 2.51 us -> none  [the longest x1 1.08 us: chip_body(): featured[:, share:half]]
  transfers between devices with their start and end apart: 4 -> 0, of which waited for: 3 -> 0; matrix products, arithmetic and copies ran while one was open for 1% -> 0% of each run, Pallas kernels for 7% -> 0%
where the time goes in v1:
time: 226 us
  Pallas kernels  200 us (88%)
  matrix products  17 us (8%)
  other arithmetic  5.23 us (2%)
  local copies, waits for them, and re-layouts  4.04 us (2%)
    pallas_call x1, Pallas kernels, mixer(): pl.pallas_call(functools.partial(mixer_kernel, chan_count), out_shape=jax...  109 us
    pallas_call x1, Pallas kernels, gather_inputs(): pl.pallas_call(functools.partial(gather_inputs_kernel, chan_count), out_s...  91.4 us
    dot_general x1, matrix products, chip_body(): jnp.dot(normed, all_weights, preferred_element_type=jnp.float32)  17 us
    reduce_sum x1, other arithmetic, chip_body(): jnp.mean(wide * wide, axis=1, keepdims=True) + EPSILON  5.22 us

profile of v1, /device:TPU:2, one launch (start us, length us, event | category | flops | bytes accessed | tf_op | source)
XLA Modules:
  0.0 226.2 jit_solution(14376792514940852081)
XLA Ops:
  0.0 2.5 %copy.9 = bf16[1024,512]{0,1:T(8,128)(2,1)} copy(f32[1024,512]{1,0:T(8,128)} %param.12) | data formatting | bytes 3145728 | tf_op args[4]
  2.5 0.0 copy-start.4
  2.5 91.4 %gather_inputs.1 = (bf16[1024,4096]{1,0:T(8,128)(2,1)}, bf16[4096,1536]{1,0:T(8,128)(2,1)}, bf16[2048,512]{1,0:T(8,128)(2,1)}) custom-call(bf16[512,1024]{1,0:T(8,128)(2,1)} %tokens.3, bf16[3,1024,1024]{2,1,0:T(8,128)(2,1)} %bitcast.7, bf16[512,1024]{1,0:T(8,128)(2,1)} %bitcast.8), custom_call_target="tpu_custom_call" | custom-call | tf_op jit(solution)/shard_map/gather_inputs/pallas_call | solution.py:503
  94.0 0.0 copy-start.3
  94.0 5.2 %fusion = f32[1024]{0:T(1024)S(1)} fusion(bf16[1024,4096]{1,0:T(8,128)(2,1)} %get-tuple-element.8), kind=kLoop, calls=%fused_computation.2 | loop fusion | flops 12581888 | bytes 8392704 | tf_op jit(solution)/shard_map/reduce_sum | solution.py:957
  99.2 0.0 copy-done.4
  99.2 0.5 copy-done.3
  99.8 0.0 copy-start
  99.8 0.0 copy-start.1
  99.8 0.0 copy-start.2
  99.8 17.0 %fusion.7.projected = bf16[1024,1536]{1,0:T(8,128)(2,1)} fusion(bf16[4096,1536]{1,0:T(8,128)(2,1)} %get-tuple-element.9, bf16[1024,4096]{1,0:T(8,128)(2,1)S(1)} %copy-done.3, f32[4096]{0:T(1024)S(1)} %copy-done.4, f32[1024]{0:T(1024)S(1)} %add_rsqrt_fusion), kind=kOutput, calls=%fused_computation.8 | convolution fusion | flops 12903251968 | bytes 24137728 | tf_op jit(solution)/shard_map/dot_general | solution.py:959
  116.7 0.0 copy-done
  116.7 0.0 copy-done.1
  116.7 0.0 copy-done.2
  116.8 108.5 %mixer.1 = bf16[512,1024]{1,0:T(8,128)(2,1)S(1)} custom-call(bf16[1024,1536]{1,0:T(8,128)(2,1)} %fusion.7.projected, f32[3,3,1024]{2,1,0:T(4,128)S(1)} %copy-done.1, f32[1,1024]{1,0:T(1,128)S(1)} %bitcast.6, bf16[2048,512]{1,0:T(8,128)(2,1)} %get-tuple-element.10.taps, bf16[2048,1024]{1,0:T(8,128)(2,1)} %constant.9.clone.table_hbm, ...), custom_call_target="tpu_custom_call" | custom-call | tf_op jit(solution)/shard_map/mixer/pallas_call | solution.py:911
  225.3 1.0 copy.11
  (1 shorter events, 0.0 us)
Async XLA Ops:
  2.5 96.7 %copy-start.4 = (f32[4096]{0:T(1024)S(1)}, f32[4096]{0:T(1024)}, u32[]{:S(2)}) copy-start(f32[4096]{0:T(1024)} %param.9) | copy-start | bytes 49156
  94.0 5.8 %copy-start.3 = (bf16[1024,4096]{1,0:T(8,128)(2,1)S(1)}, bf16[1024,4096]{1,0:T(8,128)(2,1)}, u32[]{:S(2)}) copy-start(bf16[1024,4096]{1,0:T(8,128)(2,1)} %get-tuple-element.8) | copy-start | bytes 25165828
  99.8 17.0 %copy-start = (bf16[512,1024]{1,0:T(8,128)(2,1)S(1)}, bf16[512,1024]{1,0:T(8,128)(2,1)}, u32[]{:S(2)}) copy-start(bf16[512,1024]{1,0:T(8,128)(2,1)} %tokens.3) | copy-start | bytes 3145732
  99.8 17.0 %copy-start.1 = (f32[3,3,1024]{2,1,0:T(4,128)S(1)}, f32[3,3,1024]{2,1,0:T(4,128)}, u32[]{:S(2)}) copy-start(f32[3,3,1024]{2,1,0:T(4,128)} %short.1) | copy-start | bytes 110596
  99.8 17.0 %copy-start.2 = (f32[1024]{0:T(1024)S(1)}, f32[1024]{0:T(1024)}, u32[]{:S(2)}) copy-start(f32[1024]{0:T(1024)} %param.13) | copy-start | bytes 12292

commit v2 on v1

v2 whole, which is shorter than its diff:
```python
import functools
import math

import jax
import jax.numpy as jnp
import numpy as np
from jax import lax
from jax.experimental import pallas as pl
from jax.experimental.pallas import tpu as pltpu
from jax.sharding import PartitionSpec as P

SHORT = 3


EPSILON = 1e-06
HIGHEST = lax.Precision.HIGHEST


def from_behind(value, axis, steps):
    count = lax.axis_size(axis)
    initial, last = (max(0, -steps), min(count, count - steps))
    return lax.ppermute(value, axis, [(source, source + steps) for source in range(initial, last)])


def angle_table(row_count, col_count, period, sign):
    row_index = lax.iota(jnp.int32, row_count)[:, None]
    col_index = lax.iota(jnp.int32, col_count)[None, :]
    angles = (row_index * col_index % period).astype(jnp.float32) * (sign * 2.0 * math.pi / period)
    return (jnp.cos(angles), jnp.sin(angles))


def forward_spectrum(signal_rows, first, second):
    channels = signal_rows.shape[0]
    grid_rows = signal_rows.reshape(channels, first, second)
    cos_first, sin_first = angle_table(first, first, first, -1.0)
    part_re = jnp.einsum("cab,ak->ckb", grid_rows, cos_first, precision=HIGHEST)
    part_im = jnp.einsum("cab,ak->ckb", grid_rows, sin_first, precision=HIGHEST)
    twist_cos, twist_sin = angle_table(first, second, first * second, -1.0)
    part_re, part_im = (
        part_re * twist_cos - part_im * twist_sin,
        part_re * twist_sin + part_im * twist_cos,
    )
    cos_second, sin_second = angle_table(second, second, second, -1.0)
    spectrum_real = jnp.einsum("ckb,bm->ckm", part_re, cos_second, precision=HIGHEST) - jnp.einsum(
        "ckb,bm->ckm", part_im, sin_second, precision=HIGHEST
    )
    spec_im = jnp.einsum("ckb,bm->ckm", part_re, sin_second, precision=HIGHEST) + jnp.einsum(
        "ckb,bm->ckm", part_im, cos_second, precision=HIGHEST
    )
    return (spectrum_real, spec_im)


def inverse_spectrum(spectrum_real, spec_im, first, second):
    channels = spectrum_real.shape[0]
    cos_second, sin_second = angle_table(second, second, second, 1.0)
    part_re = jnp.einsum("ckm,bm->ckb", spectrum_real, cos_second, precision=HIGHEST) - jnp.einsum(
        "ckm,bm->ckb", spec_im, sin_second, precision=HIGHEST
    )
    part_im = jnp.einsum("ckm,bm->ckb", spectrum_real, sin_second, precision=HIGHEST) + jnp.einsum(
        "ckm,bm->ckb", spec_im, cos_second, precision=HIGHEST
    )
    twist_cos, twist_sin = angle_table(first, second, first * second, 1.0)
    part_re, part_im = (
        part_re * twist_cos - part_im * twist_sin,
        part_re * twist_sin + part_im * twist_cos,
    )
    cos_first, sin_first = angle_table(first, first, first, 1.0)
    result = jnp.einsum("ckb,ak->cab", part_re, cos_first, precision=HIGHEST) - jnp.einsum(
        "ckb,ak->cab", part_im, sin_first, precision=HIGHEST
    )
    return result.reshape(channels, first * second) / (first * second)


def spectral_conv(signal_rows, filter_rows):
    channels, length = signal_rows.shape
    padded_len = 2 * length
    log_len = padded_len.bit_length() - 1
    first = 1 << log_len // 2
    second = padded_len // first
    zeros_tail = jnp.zeros((channels, length), jnp.float32)
    sig_re, sig_im = forward_spectrum(
        jnp.concatenate([signal_rows, zeros_tail], axis=1), first, second
    )
    tap_re, tap_im = forward_spectrum(
        jnp.concatenate([filter_rows, zeros_tail], axis=1), first, second
    )
    prod_re = sig_re * tap_re - sig_im * tap_im
    prod_im = sig_re * tap_im + sig_im * tap_re
    return inverse_spectrum(prod_re, prod_im, first, second)[:, :length]


def short_filter_output(projected, rim_cells, kernel_coefficients):
    count = kernel_coefficients.shape[0]
    steps_len = projected.shape[2]
    extended = jnp.concatenate([rim_cells, projected], axis=2).astype(jnp.float32)
    total = jnp.zeros(projected.shape, jnp.float32)
    for tap in range(count):
        total = (
            total
            + kernel_coefficients[tap][:, :, None]
            * extended[:, :, count - 1 - tap : count - 1 - tap + steps_len]
        )
    return total.astype(jnp.bfloat16)


def hyena_mixer(keys_rows, values_rows, long_taps, skip_part):
    middle = keys_rows.astype(jnp.float32) * values_rows.astype(jnp.float32)
    return (spectral_conv(middle, long_taps) + skip_part[:, None] * middle).astype(jnp.bfloat16)


def body(tokens, norm_gain, proj_weight, short_filter, long_filter, skip_gain, out_weight):
    seq_count = lax.axis_size("seq")
    local_rows = tokens.shape[0]
    local_chan = proj_weight.shape[2]
    subset = local_chan // seq_count
    length = local_rows * seq_count
    offset = lax.axis_index("seq") * subset
    whole = lax.all_gather(tokens, "chan", axis=1, tiled=True)
    wide = whole.astype(jnp.float32)
    rescaled_signal = (
        wide * lax.rsqrt(jnp.mean(wide * wide, axis=1, keepdims=True) + EPSILON) * norm_gain
    ).astype(jnp.bfloat16)
    projected = lax.dot_general(
        lax.all_gather(proj_weight, "seq", axis=0, tiled=True),
        rescaled_signal,
        (((0,), (1,)), ((), ())),
        preferred_element_type=jnp.float32,
    ).astype(jnp.bfloat16)
    taps_grid = long_filter.reshape(1, seq_count, subset, local_rows)
    long_taps = lax.all_to_all(taps_grid, "seq", split_axis=1, concat_axis=3, tiled=True).reshape(
        subset, length
    )
    skip_part = lax.dynamic_slice_in_dim(skip_gain, offset, subset, 0)
    rim_cells = from_behind(projected[:, :, local_rows - (SHORT - 1) :], "seq", 1)
    featured = short_filter_output(projected, rim_cells, short_filter)
    pair_grid = featured[1:].reshape(2, seq_count, subset, local_rows)
    moved = lax.all_to_all(pair_grid, "seq", split_axis=1, concat_axis=3, tiled=True).reshape(
        2, subset, length
    )
    result = hyena_mixer(moved[0], moved[1], long_taps, skip_part)
    returned = lax.all_to_all(
        result.reshape(1, subset, length), "seq", split_axis=2, concat_axis=0, tiled=True
    )
    returned = returned.reshape(local_chan, local_rows)
    gated = (featured[0].astype(jnp.float32) * returned.astype(jnp.float32)).astype(jnp.bfloat16)
    full_mix = lax.all_gather(gated, "chan", axis=0, tiled=True)
    update = lax.dot_general(
        full_mix, out_weight, (((0,), (0,)), ((), ())), preferred_element_type=jnp.float32
    )
    return (tokens.astype(jnp.float32) + update).astype(jnp.bfloat16)

LANES = 128
BLOCK = 128
SPAN = 512
TOKEN_CHUNKS = 8
WEIGHT_CHUNKS = 4
ANY = pl.BlockSpec(memory_space=pl.ANY)


def remote(src, dst, send_sem, recv_sem, where):
    return pltpu.make_async_remote_copy(
        src_ref=src,
        dst_ref=dst,
        send_sem=send_sem,
        recv_sem=recv_sem,
        device_id=where,
        device_id_type=pl.DeviceIdType.MESH,
    )


class Line:
    def __init__(self, view, count, send_sem, recv_sem, place):
        self.view, self.count, self.place = view, count, place
        self.send_sem, self.recv_sem = send_sem, recv_sem
        self.me = lax.axis_index("chan")

    def move(self, way, step, piece, block, target):
        index = (way, step) + piece
        return remote(
            block, block, self.send_sem.at[index], self.recv_sem.at[index], self.place(target)
        )

    def copy(self, way, step, piece):
        sign = 1 if way == 0 else -1
        owner = jnp.clip(self.me - step * sign, 0, self.count - 1)
        target = jnp.clip(self.me + sign, 0, self.count - 1)
        return self.move(way, step, piece, self.view(owner, *piece), target)

    def sends(self, way, step):
        if way == 0:
            return (self.me - step >= 0) & (self.me + 1 < self.count)
        return (self.me + step < self.count) & (self.me - 1 >= 0)

    def receives(self, way, step):
        if way == 0:
            return self.me - 1 - step >= 0
        return self.me + 1 + step < self.count

    def source(self, way, step):
        sign = 1 if way == 0 else -1
        return jnp.clip(self.me - (step + 1) * sign, 0, self.count - 1)

    def arrived(self, way, step, piece):
        owner = self.source(way, step)
        self.move(way, step, piece, self.view(owner, *piece), self.me).wait_recv()
        return owner


def block_kernel(
    chan_count,
    tokens,
    gain,
    weights,
    short,
    long_taps,
    skip,
    out_weight,
    result,
    stream,
    weight,
    sums,
    scale,
    partial,
    room,
    out_room,
    table,
    taps,
    turn,
    spectra,
    freq,
    mixed,
    edge_out,
    edge,
    extended,
    query,
    signal,
    before,
    ready,
    full,
    total,
    local_sem,
    mate_send,
    mate_recv,
    token_send,
    token_recv,
    sums_send,
    sums_recv,
    x_send,
    x_recv,
    y_send,
    y_recv,
    tap_send,
    tap_recv,
    edge_send,
    edge_recv,
    before_send,
    before_recv,
    swap_send,
    swap_recv,
    line_send,
    line_recv,
):
    y, s, z = (lax.axis_index(name) for name in ("groups", "seq", "chan"))
    x, core = s // 2, s % 2
    mate_s = s + 1 - 2 * core
    mate = (y, mate_s, z)
    across = (y, (1 - x) * 2 + core, z)
    aslant = (y, (1 - x) * 2 + 1 - core, z)
    beside = (1 - y, s, z)
    rows, width = tokens.shape
    length = 2 * rows
    branches, depth = weights.shape[0], weights.shape[1]
    half = depth // 2
    share = weights.shape[2] // 2
    groups = share // LANES
    rim = edge.shape[2]
    steps = chan_count - 1
    token_rows = rows // TOKEN_CHUNKS
    weight_rows = half // WEIGHT_CHUNKS

    column_peers = [mate] + [
        (y, 2 * x + of, lax.rem(z + by, chan_count))
        for by in range(1, chan_count)
        for of in (core, 1 - core)
    ]
    peers = column_peers + [across, aslant, beside]

    def rows_at(i, count, base=0):
        return pl.ds(pl.multiple_of(base + i * count, count), count)

    def at_rows(i):
        return rows_at(i, BLOCK)

    def blocks(count):
        return pl.loop(0, count // BLOCK)

    def lanes_of(base, g):
        return pl.ds(pl.multiple_of(base + g * LANES, LANES), LANES)

    tap_stage = [(0, 0), (0, length), (1, 0), (1, length)]
    tap_loads = [
        pltpu.make_async_copy(
            long_taps.at[:, pl.ds(j * LANES, LANES)],
            freq.at[which, pl.ds(start, length)],
            local_sem.at[4 + j],
        )
        for j, (which, start) in enumerate(tap_stage)
    ]
    token_load = pltpu.make_async_copy(tokens, room, local_sem.at[0])
    out_load = pltpu.make_async_copy(out_weight, out_room, local_sem.at[1])
    token_load.start()
    for copy in tap_loads:
        copy.start()
    for g in range(groups):
        for b in range(branches):
            pltpu.make_async_copy(
                weights.at[b, :, lanes_of(core * share, g)],
                weight.at[g, s, :, pl.ds(b * LANES, LANES)],
                local_sem.at[2],
            ).start()
    out_load.start()

    barrier = pltpu.get_barrier_semaphore()
    for peer in peers:
        pl.semaphore_signal(barrier, inc=1, device_id=peer, device_id_type=pl.DeviceIdType.MESH)

    sums[core, z] = jnp.zeros(sums.shape[2:], jnp.float32)
    own_gain = gain[:, pl.ds(pl.multiple_of(z * width, width), width)]
    token_load.wait()

    @blocks(rows)
    def _(i):
        raw = room[at_rows(i), :].astype(jnp.float32)
        total[at_rows(i), :] = raw
        stream[z, pl.ds(pl.multiple_of(core * rows + i * BLOCK, BLOCK), BLOCK), :] = (
            raw * own_gain
        ).astype(jnp.bfloat16)
        square = raw * raw
        found = square[:, :LANES]
        for part in range(1, width // LANES):
            found = found + square[:, part * LANES : (part + 1) * LANES]
        sums[core, z, pl.ds(i, 1), :] = jnp.sum(found.T, axis=0, keepdims=True)

    pl.semaphore_wait(barrier, len(peers))

    def token_view(owner, chunk):
        return stream.at[owner, rows_at(chunk, token_rows, core * rows), :]

    token_line = Line(
        token_view, chan_count, token_send, token_recv, lambda to: (y, s, to)
    )
    for chunk in range(TOKEN_CHUNKS):
        for way in range(2):

            @pl.when(token_line.sends(way, 0))
            def _():
                token_line.copy(way, 0, (chunk,)).start()

    def own_half(owner, of):
        return stream.at[owner, pl.ds(pl.multiple_of(of * rows, rows), rows), :]

    def mate_tokens():
        return remote(
            own_half(z, core), own_half(z, core), mate_send.at[0], mate_recv.at[0], mate
        )

    mate_tokens().start()
    sum_copies = [
        remote(
            sums.at[core, z], sums.at[core, z], sums_send.at[at], sums_recv.at[core, z], peer
        )
        for at, peer in enumerate(column_peers)
    ]
    for copy in sum_copies:
        copy.start()
    for g in range(groups):
        for b in range(branches):
            remote(
                weights.at[b, :, lanes_of((1 - core) * share, g)],
                weight.at[g, s, :, pl.ds(b * LANES, LANES)],
                mate_send.at[1],
                mate_recv.at[1],
                mate,
            ).start()

    for j, (which, start) in enumerate(tap_stage):
        tap_loads[j].wait()

        @pl.loop(0, groups)
        def _(g):
            mine = freq[which, rows_at(core * groups + g, BLOCK, start), :]
            taps[g, pl.ds(pl.multiple_of(s * rows + j * LANES, LANES), LANES), :] = mine.T.astype(
                jnp.bfloat16
            )
            other = freq[which, rows_at((1 - core) * groups + g, BLOCK, start), :]
            ready[g, j * LANES : (j + 1) * LANES, :] = other.T.astype(jnp.bfloat16)

    def tap_part(owner, part):
        return taps.at[
            :, pl.ds(pl.multiple_of(owner * rows + part * (rows // 2), rows // 2), rows // 2), :
        ]

    def taps_across(to):
        src = tap_part(s, y) if to == 0 else ready.at[
            :, pl.ds(pl.multiple_of(y * (rows // 2), rows // 2), rows // 2), :
        ]
        return remote(
            src,
            tap_part(s, y),
            tap_send.at[to],
            tap_recv.at[core],
            across if to == 0 else aslant,
        )

    def taps_beside(origin, part):
        view = tap_part(origin, part)
        return remote(view, view, tap_send.at[2 + origin], tap_recv.at[2 + origin], beside)

    def taps_mate():
        return remote(
            ready,
            taps.at[:, pl.ds(pl.multiple_of(s * rows, rows), rows), :],
            mate_send.at[2],
            mate_recv.at[2],
            mate,
        )

    @pl.when(x == 0)
    def _():
        taps_across(0).start()
        taps_across(1).start()

        @pl.loop(0, groups)
        def _(g):
            taps[g, length:, :] = jnp.zeros((length, LANES), jnp.bfloat16)

    taps_mate().start()

    def weight_view(owner, part, g, c):
        return weight.at[g, owner, rows_at(c, weight_rows, part * half), :]

    def weight_sent(to, g, c):
        view = weight_view(s, y, g, c)
        return remote(
            view, view, x_send.at[to, g, c], x_recv.at[core, g, c], across if to == 0 else aslant
        )

    def send_weights(g):
        for c in range(WEIGHT_CHUNKS):
            for to in range(2):
                side = core if to == 0 else 1 - core
                view = weight_view(s, y, g, c)
                for b in range(branches):
                    remote(
                        weights.at[
                            b,
                            rows_at(c, weight_rows, y * half),
                            pl.ds(pl.multiple_of(side * share + g * LANES, LANES), LANES),
                        ],
                        view.at[:, pl.ds(b * LANES, LANES)],
                        x_send.at[to, g, c],
                        x_recv.at[core, g, c],
                        across if to == 0 else aslant,
                    ).start()

    for g in range(groups - 1):
        send_weights(g)

    def beside_copy(origin, part, g, c):
        view = weight_view((1 - x) * 2 + origin, part, g, c)
        return remote(view, view, y_send.at[origin, g, c], y_recv.at[origin, g, c], beside)

    def forward(g, c):
        for origin in range(2):
            view = weight_view((1 - x) * 2 + origin, y, g, c)
            remote(
                view, view, x_send.at[origin, g, c], x_recv.at[origin, g, c], beside
            ).wait_recv()
            beside_copy(origin, y, g, c).start()

    def await_beside(g):
        for c in range(WEIGHT_CHUNKS):
            for origin in range(2):
                beside_copy(origin, 1 - y, g, c).wait_recv()

    @blocks(length)
    def _(i):
        row = lax.broadcasted_iota(jnp.int32, (BLOCK, LANES), 0) + i * BLOCK
        lane = lax.broadcasted_iota(jnp.int32, (BLOCK, LANES), 1)
        unit = math.pi / (4 * length)
        odd = 2 * row + 1
        small = odd.astype(jnp.float32) * unit
        turn[0, at_rows(i), :] = jnp.cos(small)
        turn[1, at_rows(i), :] = jnp.sin(small)
        period = 8 * length
        angle = (odd * (2 * lane + 1) % period).astype(jnp.float32) * unit
        cos, sin = jnp.cos(angle), jnp.sin(angle)
        stride = (odd * (2 * LANES) % period).astype(jnp.float32) * unit
        step_cos, step_sin = jnp.cos(stride), jnp.sin(stride)
        for a in range(length // LANES):
            table[at_rows(i), a * LANES : (a + 1) * LANES] = cos.astype(jnp.bfloat16)
            table[rows_at(i, BLOCK, length), a * LANES : (a + 1) * LANES] = sin.astype(
                jnp.bfloat16
            )
            cos, sin = cos * step_cos - sin * step_sin, sin * step_cos + cos * step_sin

    for g in range(groups):

        @blocks(length)
        def _(i):
            partial[g, at_rows(i), :] = jnp.zeros((BLOCK, branches * LANES), jnp.float32)

    def spectrum(which, column):
        @pl.loop(0, 2 * length // SPAN)
        def _(i):
            at = rows_at(i, SPAN)
            freq[which, at, :] = jnp.dot(
                table[at, :], column(), preferred_element_type=jnp.float32
            )

    def tap_spectra(g):
        @pl.loop(0, 2 * length // SPAN)
        def _(i):
            at = rows_at(i, SPAN)
            both = jnp.concatenate([taps[g, :length, :], taps[g, length:, :]], axis=1)
            found = jnp.dot(table[at, :], both, preferred_element_type=jnp.float32)
            freq[0, at, :] = found[:, :LANES]
            freq[1, at, :] = found[:, LANES:]

        @blocks(length)
        def _(i):
            low, high = at_rows(i), rows_at(i, BLOCK, length)
            cos, sin = turn[0, low, :], turn[1, low, :]

            def turned(which):
                real, imag = freq[which, low, :], -freq[which, high, :]
                return (cos * real - sin * imag) / length, (cos * imag + sin * real) / length

            real, imag = turned(0)
            late_real, late_imag = turned(1)
            place = lax.broadcasted_iota(jnp.int32, (BLOCK, LANES), 0)
            sign = (1 - 2 * (place % 2)).astype(jnp.float32)
            spectra[g, 0, low, :] = real.astype(jnp.bfloat16)
            spectra[g, 1, low, :] = imag.astype(jnp.bfloat16)
            spectra[g, 2, low, :] = (late_real - sign * imag).astype(jnp.bfloat16)
            spectra[g, 3, low, :] = (late_imag + sign * real).astype(jnp.bfloat16)

    def project(g, owner):
        @pl.loop(0, length // SPAN)
        def _(i):
            at = rows_at(i, SPAN)
            partial[g, at, :] += jnp.dot(
                stream[owner, at, :], weight[g, owner], preferred_element_type=jnp.float32
            )

    def distance(owner):
        return jnp.abs(z - owner)

    def to_mate(way, step, chunk):
        block = token_view(token_line.source(way, step), chunk)
        index = 3 + way * steps + step
        return remote(block, block, mate_send.at[index], mate_recv.at[index], mate)

    def mate_half(way, step, of):
        block = own_half(token_line.source(way, step), of)
        index = 3 + way * steps + step
        return remote(block, block, mate_send.at[index], mate_recv.at[index], mate)

    def await_mate(step):
        for way in range(2):

            @pl.when(token_line.receives(way, step))
            def _():
                mate_half(way, step, 1 - core).wait_recv()

    @pl.loop(0, steps * TOKEN_CHUNKS)
    def _(tick):
        step, chunk = tick // TOKEN_CHUNKS, tick % TOKEN_CHUNKS
        for way in range(2):

            @pl.when(token_line.receives(way, step))
            def _():
                token_line.arrived(way, step, (chunk,))
                to_mate(way, step, chunk).start()

            @pl.when(
                (step + 1 < steps)
                & token_line.receives(way, step)
                & token_line.sends(way, step + 1)
            )
            def _():
                token_line.copy(way, step + 1, (chunk,)).start()

        @pl.when((tick == TOKEN_CHUNKS // 2) & (x == 1))
        def _():
            for origin in range(2):
                view = tap_part(origin, y)
                remote(
                    view, view, tap_send.at[origin], tap_recv.at[origin], beside
                ).wait_recv()
                taps_beside(origin, y).start()

        @pl.when((tick % 2 == 1) & (tick >= 3) & (tick < 3 + 4 * WEIGHT_CHUNKS))
        def _():
            at = (tick - 3) // 2
            forward(at // WEIGHT_CHUNKS, at % WEIGHT_CHUNKS)

        @pl.when(tick == TOKEN_CHUNKS)
        def _():
            mate_half_own = own_half(z, 1 - core)
            remote(
                mate_half_own, mate_half_own, mate_send.at[0], mate_recv.at[0], mate
            ).wait_recv()
            await_mate(0)
            pltpu.make_async_copy(
                weight.at[:, s], weight.at[:, s], local_sem.at[2]
            ).wait()
            other = weight.at[:, mate_s]
            remote(other, other, mate_send.at[1], mate_recv.at[1], mate).wait_recv()
            other = taps.at[:, pl.ds(pl.multiple_of(mate_s * rows, rows), rows), :]
            remote(other, other, mate_send.at[2], mate_recv.at[2], mate).wait_recv()

            @pl.when(x == 1)
            def _():
                for origin in range(2):
                    taps_beside(origin, 1 - y).wait_recv()

        @pl.when((step == 1) & (chunk % 2 == 0))
        def _():
            tap_spectra(chunk // 2)

        @pl.when(tick == 2 * TOKEN_CHUNKS)
        def _():
            await_mate(1)

        owner = 2 * x + chunk // groups
        far = distance(owner)

        @pl.when(((step == 1) & (far <= 1)) | ((step == 2) & (far == 2)))
        def _():
            project(chunk % groups, owner)

    for g in range(2):
        await_beside(g)

        @pl.loop(0, 2)
        def _(at):
            owner = 2 * (1 - x) + at

            @pl.when(distance(owner) <= 2)
            def _():
                project(g, owner)

    await_mate(2)
    for by in range(1, chan_count):
        for of in range(2):
            view = sums.at[of, lax.rem(z + by, chan_count)]
            remote(
                view, view, sums_send.at[0], sums_recv.at[of, lax.rem(z + by, chan_count)], mate
            ).wait_recv()
    view = sums.at[1 - core, z]
    remote(view, view, sums_send.at[0], sums_recv.at[1 - core, z], mate).wait_recv()

    @blocks(length)
    def _(i):
        of, at = i // (rows // BLOCK), i % (rows // BLOCK)
        found = sums[of, 0, pl.ds(at, 1), :]
        for owner in range(1, chan_count):
            found = found + sums[of, owner, pl.ds(at, 1), :]
        found = lax.rsqrt(found / (chan_count * width) + EPSILON)
        scale[at_rows(i), :] = jnp.broadcast_to(found, (BLOCK, LANES)).T

    taps_mate().wait_send()

    @pl.when(x == 0)
    def _():
        taps_across(0).wait_send()
        taps_across(1).wait_send()

    def edge_copy(g):
        return remote(
            edge_out.at[g], edge.at[g], edge_send.at[g], edge_recv.at[g], across
        )

    def before_copy(g):
        return remote(
            signal.at[g], before.at[g], before_send.at[g], before_recv.at[g], across
        )

    def swap_copy(g):
        return remote(
            ready.at[g], full.at[z, g, core], swap_send.at[g], swap_recv.at[g], mate
        )

    line = Line(
        lambda owner, g, of: full.at[owner, g, of],
        chan_count,
        line_send,
        line_recv,
        lambda to: (y, s, to),
    )

    def projected(g, b, at):
        return (partial[g, at, b * LANES : (b + 1) * LANES] * scale[at, :]).astype(jnp.bfloat16)

    def featurize(g):
        @pl.when(x == 0)
        def _():
            for b in range(branches):
                edge_out[g, b] = projected(g, b, pl.ds(length - rim, rim))
                extended[b, 0:rim, :] = jnp.zeros((rim, LANES), jnp.float32)
            edge_copy(g).start()

        @blocks(length)
        def _(i):
            for b in range(branches):
                extended[b, pl.ds(pl.multiple_of(rim + i * BLOCK, rim), BLOCK), :] = projected(
                    g, b, at_rows(i)
                ).astype(jnp.float32)

        @pl.when(x == 1)
        def _():
            edge_copy(g).wait_recv()
            for b in range(branches):
                extended[b, 0:rim, :] = edge[g, b].astype(jnp.float32)

        chosen = lanes_of(core * share, g)
        coefficient = [
            [short[tap, b : b + 1, chosen] for b in range(branches)] for tap in range(SHORT)
        ]

        @blocks(length)
        def _(i):
            found = []
            for b in range(branches):
                value = jnp.zeros((BLOCK, LANES), jnp.float32)
                for tap in range(SHORT):
                    value = value + coefficient[tap][b] * extended[
                        b, pl.ds(rim - tap + i * BLOCK, BLOCK), :
                    ]
                found.append(value.astype(jnp.bfloat16))
            query[at_rows(i), :] = found[0]
            signal[g, at_rows(i), :] = (
                found[1].astype(jnp.float32) * found[2].astype(jnp.float32)
            ).astype(jnp.bfloat16)

    def convolve(g):
        spectrum(0, lambda: signal[g])

        def product(i, which, first):
            low, high = at_rows(i), rows_at(i, BLOCK, length)
            cos, sin = freq[which, low, :], freq[which, high, :]
            real = spectra[g, first, low, :].astype(jnp.float32)
            imag = spectra[g, first + 1, low, :].astype(jnp.float32)
            return cos * real + sin * imag, sin * real - cos * imag

        @pl.when(x == 0)
        def _():
            @blocks(length)
            def _(i):
                real, imag = product(i, 0, 0)
                mixed[at_rows(i), :] = real.astype(jnp.bfloat16)
                mixed[rows_at(i, BLOCK, length), :] = imag.astype(jnp.bfloat16)

        @pl.when(x == 1)
        def _():
            before_copy(g).wait_recv()
            spectrum(1, lambda: before[g])

            @blocks(length)
            def _(i):
                real, imag = product(i, 0, 0)
                more_real, more_imag = product(i, 1, 2)
                mixed[at_rows(i), :] = (real + more_real).astype(jnp.bfloat16)
                mixed[rows_at(i, BLOCK, length), :] = (imag + more_imag).astype(jnp.bfloat16)

        @pl.loop(0, length // SPAN)
        def _(i):
            low, high = rows_at(i, SPAN), rows_at(i, SPAN, length)
            freq[0, low, :] = jnp.dot(
                table[low, :], mixed[:length, :], preferred_element_type=jnp.float32
            ) + jnp.dot(table[high, :], mixed[length:, :], preferred_element_type=jnp.float32)

        direct = skip[:, lanes_of(core * share, g)]

        def gated(at):
            longer = freq[0, at, :] + direct * signal[g, at, :].astype(jnp.float32)
            longer = longer.astype(jnp.bfloat16).astype(jnp.float32)
            return (query[at, :].astype(jnp.float32) * longer).astype(jnp.bfloat16)

        @blocks(rows)
        def _(i):
            full[z, g, core, at_rows(i), :] = gated(
                pl.ds(pl.multiple_of(core * rows + i * BLOCK, BLOCK), BLOCK)
            )
            ready[g, at_rows(i), :] = gated(
                pl.ds(pl.multiple_of((1 - core) * rows + i * BLOCK, BLOCK), BLOCK)
            )

    def accumulate(owner, g):
        left = pl.ds(pl.multiple_of(owner * 2 * share + g * LANES, LANES), LANES)
        right = pl.ds(pl.multiple_of((owner * 2 + 1) * share + g * LANES, LANES), LANES)

        @pl.loop(0, total.shape[1] // (2 * LANES))
        def _(i):
            cols = rows_at(i, 2 * LANES)
            block = jnp.concatenate([full[owner, g, 0], full[owner, g, 1]], axis=1)
            kernel = jnp.concatenate([out_room[left, cols], out_room[right, cols]], axis=0)
            total[:, cols] += jnp.dot(block, kernel, preferred_element_type=jnp.float32)

    def begin(g):
        swap_copy(g).start()
        for way in range(2):

            @pl.when(line.sends(way, 0))
            def _():
                line.copy(way, 0, (g, core)).start()

        other = full.at[z, g, 1 - core]
        remote(other, other, swap_send.at[g], swap_recv.at[g], mate).wait_recv()
        for way in range(2):

            @pl.when(line.sends(way, 0))
            def _():
                line.copy(way, 0, (g, 1 - core)).start()

    def relay(step, g):
        for way in range(2):

            @pl.when(line.receives(way, step))
            def _():
                for of in range(2):
                    owner = line.arrived(way, step, (g, of))
                    if step + 1 < steps:

                        @pl.when(line.sends(way, step + 1))
                        def _():
                            line.copy(way, step + 1, (g, of)).start()

                accumulate(owner, g)

    @pl.loop(0, groups + steps)
    def _(g):
        @pl.when(g < groups)
        def _():
            @pl.when(g >= 2)
            def _():
                await_beside(g)

            @pl.loop(0, chan_count)
            def _(owner):
                @pl.when((distance(owner) > 2) | ((owner // 2 != x) & (g >= 2)))
                def _():
                    project(g, owner)

            featurize(g)

            @pl.when(x == 0)
            def _():
                before_copy(g).start()

            @pl.when(g == 0)
            def _():
                send_weights(groups - 1)

            convolve(g)
            begin(g)

            @pl.when(g < groups - 2)
            def _():
                for c in range(WEIGHT_CHUNKS):
                    forward(g + 2, c)

            @pl.when(g == 0)
            def _():
                out_load.wait()

            accumulate(z, g)

        for step in range(steps):
            at = g - 1 - step

            @pl.when((at >= 0) & (at < groups))
            def _():
                relay(step, at)

    @blocks(rows)
    def _(i):
        result[at_rows(i), :] = total[at_rows(i), :].astype(jnp.bfloat16)

    mate_tokens().wait_send()
    other = weight.at[:, s]
    remote(other, other, mate_send.at[1], mate_recv.at[1], mate).wait_send()
    for copy in sum_copies:
        copy.wait_send()

    @pl.when(x == 1)
    def _():
        for origin in range(2):
            taps_beside(origin, y).wait_send()

    @pl.loop(0, groups)
    def _(g):
        for c in range(WEIGHT_CHUNKS):
            for to in range(2):
                weight_sent(to, g, c).wait_send()
                beside_copy(to, y, g, c).wait_send()
        swap_copy(g).wait_send()

        @pl.when(x == 0)
        def _():
            edge_copy(g).wait_send()
            before_copy(g).wait_send()

        for way in range(2):
            for step in range(steps):

                @pl.when(line.sends(way, step))
                def _():
                    for of in range(2):
                        line.copy(way, step, (g, of)).wait_send()

    for way in range(2):
        for step in range(steps):

            @pl.when(token_line.receives(way, step))
            def _():
                mate_half(way, step, core).wait_send()

            @pl.when(token_line.sends(way, step))
            def _():
                for chunk in range(TOKEN_CHUNKS):
                    token_line.copy(way, step, (chunk,)).wait_send()


def chip_body(tokens, norm_gain, proj_weight, short_filter, long_filter, skip_gain, out_weight):
    chan_count = lax.axis_size("chan")
    rows, width = tokens.shape
    depth, branches, local_chan = proj_weight.shape
    length, share = 2 * rows, local_chan // 2
    groups = share // LANES
    steps = chan_count - 1
    dma = pltpu.SemaphoreType.DMA
    f32, bf16 = jnp.float32, jnp.bfloat16
    vmem = pl.BlockSpec(memory_space=pltpu.VMEM)
    return pl.pallas_call(
        functools.partial(block_kernel, chan_count),
        out_shape=jax.ShapeDtypeStruct((rows, width), bf16),
        in_specs=[ANY, vmem, ANY, vmem, ANY, vmem, ANY],
        out_specs=vmem,
        scratch_shapes=[
            pltpu.VMEM((chan_count, length, width), bf16),
            pltpu.VMEM((groups, 4, depth, branches * LANES), bf16),
            pltpu.VMEM((2, chan_count, 8, LANES), f32),
            pltpu.VMEM((length, LANES), f32),
            pltpu.VMEM((groups, length, branches * LANES), f32),
            pltpu.VMEM((rows, width), bf16),
            pltpu.VMEM(out_weight.shape, bf16),
            pltpu.VMEM((2 * length, length), bf16),
            pltpu.VMEM((groups, 2 * length, LANES), bf16),
            pltpu.VMEM((2, length, LANES), f32),
            pltpu.VMEM((groups, 4, length, LANES), bf16),
            pltpu.VMEM((2, 2 * length, LANES), f32),
            pltpu.VMEM((2 * length, LANES), bf16),
            pltpu.VMEM((groups, branches, 16, LANES), bf16),
            pltpu.VMEM((groups, branches, 16, LANES), bf16),
            pltpu.VMEM((branches, length + 16, LANES), f32),
            pltpu.VMEM((length, LANES), bf16),
            pltpu.VMEM((groups, length, LANES), bf16),
            pltpu.VMEM((groups, length, LANES), bf16),
            pltpu.VMEM((groups, rows, LANES), bf16),
            pltpu.VMEM((chan_count, groups, 2, rows, LANES), bf16),
            pltpu.VMEM((rows, width), f32),
            dma((8,)),
            dma((3 + 2 * steps,)),
            dma((3 + 2 * steps,)),
            dma((2, steps, TOKEN_CHUNKS)),
            dma((2, steps, TOKEN_CHUNKS)),
            dma((2 * chan_count - 1,)),
            dma((2, chan_count)),
            dma((2, groups, WEIGHT_CHUNKS)),
            dma((2, groups, WEIGHT_CHUNKS)),
            dma((2, groups, WEIGHT_CHUNKS)),
            dma((2, groups, WEIGHT_CHUNKS)),
            dma((4,)),
            dma((4,)),
            dma((groups,)),
            dma((groups,)),
            dma((groups,)),
            dma((groups,)),
            dma((groups,)),
            dma((groups,)),
            dma((2, steps, groups, 2)),
            dma((2, steps, groups, 2)),
        ],
        compiler_params=pltpu.CompilerParams(
            collective_id=0, has_side_effects=True, vmem_limit_bytes=63 * 1024 * 1024
        ),
        name="block",
    )(
        tokens,
        norm_gain[None, :],
        proj_weight.transpose(1, 0, 2),
        short_filter,
        long_filter,
        skip_gain[None, :],
        out_weight,
    )


def select_body(mesh):
    if mesh.shape["seq"] == 4 and mesh.shape["groups"] == 2:
        return chip_body
    return body


def solution(mesh):
    placed = (
        P(("groups", "seq"), "chan"),
        P(),
        P("seq", None, "chan"),
        P(None, None, "chan"),
        P("chan", "seq"),
        P("chan"),
        P(None, "chan"),
    )
    return jax.shard_map(
        select_body(mesh), mesh=mesh, in_specs=placed, out_specs=P(("groups", "seq"), "chan"), check_vma=False
    )
```

time: 226 us -> 180 us (0.80)
  Pallas kernels: 200 us -> 177 us
  matrix products: 17 us -> 0 us
  other arithmetic: 5.23 us -> 0 us
    pallas_call x2 -> x1, Pallas kernels: 200 us -> 177 us  [chip_body(): pl.pallas_call(functools.partial(block_kernel, chan_count), out_shape=jax...]
    dot_general x1 -> x0, matrix products: 17 us -> none  [chip_body(): jnp.dot(normed, all_weights, preferred_element_type=jnp.float32)]
    reduce_sum x1 -> x0, other arithmetic: 5.22 us -> none  [chip_body(): jnp.mean(wide * wide, axis=1, keepdims=True) + EPSILON]
where the time goes in v2:
time: 180 us; the launch traced here: 179 us
  Pallas kernels  177 us (98%)
  local copies, waits for them, and re-layouts  2.26 us (1%)
    pallas_call x1, Pallas kernels, chip_body(): pl.pallas_call(functools.partial(block_kernel, chan_count), out_shape=jax...  177 us

profile of v2, /device:TPU:2, one launch (start us, length us, event | category | flops | bytes accessed | tf_op | source)
XLA Modules:
  0.0 179.4 jit_solution(12806963019288493224)
XLA Ops:
  0.0 177.1 %block.1 = bf16[512,1024]{1,0:T(8,128)(2,1)} custom-call(bf16[512,1024]{1,0:T(8,128)(2,1)} %tokens.1, f32[1,4096]{1,0:T(1,128)} %bitcast.4, bf16[3,1024,1024]{2,1,0:T(8,128)(2,1)} %bitcast.3, f32[3,3,1024]{2,1,0:T(4,128)} %short.1, f32[1024,512]{1,0:T(8,128)} %long_taps.1, f32[1,1024]{1,0:T(1,128)} %bitcast.5, bf16[4096,1024]{1,0:T(8,128)(2,1)} %out_weight.1), custom_call_target="tpu_custom_call" | custom-call | tf_op jit(solution)/shard_map/block/pallas_call | solution.py:946
  177.1 2.3 %copy.9 = bf16[512,1024]{1,0:T(8,128)(2,1)} copy(bf16[512,1024]{1,0:T(8,128)(2,1)} %block.1) | data formatting | bytes 2097152

commit v3 on v2

--- a/solution.py
+++ b/solution.py
@@ -180,25 +180,23 @@
             block, block, self.send_sem.at[index], self.recv_sem.at[index], self.place(target)
         )
 
+    def source(self, way, step):
+        return jnp.clip(self.me - (step + 1) * (1 - 2 * way), 0, self.count - 1)
+
     def copy(self, way, step, piece):
-        sign = 1 if way == 0 else -1
-        owner = jnp.clip(self.me - step * sign, 0, self.count - 1)
-        target = jnp.clip(self.me + sign, 0, self.count - 1)
+        owner = self.source(way, step - 1)
+        target = self.source(way, -2)
         return self.move(way, step, piece, self.view(owner, *piece), target)
 
+    def inside(self, way, by):
+        place = self.me + by * (1 - 2 * way)
+        return (place >= 0) & (place < self.count)
+
     def sends(self, way, step):
-        if way == 0:
-            return (self.me - step >= 0) & (self.me + 1 < self.count)
-        return (self.me + step < self.count) & (self.me - 1 >= 0)
+        return self.inside(way, -step) & self.inside(way, 1)
 
     def receives(self, way, step):
-        if way == 0:
-            return self.me - 1 - step >= 0
-        return self.me + 1 + step < self.count
-
-    def source(self, way, step):
-        sign = 1 if way == 0 else -1
-        return jnp.clip(self.me - (step + 1) * sign, 0, self.count - 1)
+        return self.inside(way, -1 - step)
 
     def arrived(self, way, step, piece):
         owner = self.source(way, step)
@@ -445,8 +443,8 @@
             view, view, x_send.at[to, g, c], x_recv.at[core, g, c], across if to == 0 else aslant
         )
 
-    def send_weights(g):
-        for c in range(WEIGHT_CHUNKS):
+    def send_weights(g, chunks=range(WEIGHT_CHUNKS)):
+        for c in chunks:
             for to in range(2):
                 side = core if to == 0 else 1 - core
                 view = weight_view(s, y, g, c)
@@ -465,6 +463,12 @@
 
     for g in range(groups - 1):
         send_weights(g)
+    send_weights(groups - 1, range(WEIGHT_CHUNKS - 2))
+
+    @pl.when(x == 1)
+    def _():
+        send_weights(groups - 1, range(WEIGHT_CHUNKS - 2, WEIGHT_CHUNKS))
+
 
     def beside_copy(origin, part, g, c):
         view = weight_view((1 - x) * 2 + origin, part, g, c)
@@ -553,8 +557,15 @@
                 stream[owner, at, :], weight[g, owner], preferred_element_type=jnp.float32
             )
 
-    def distance(owner):
-        return jnp.abs(z - owner)
+    at_end = (z == 0) | (z == chan_count - 1)
+
+    def projects_early(g, owner):
+        far = jnp.abs(z - owner)
+        own = owner // 2 == x
+        return (
+            (own & ((far <= 1) | ((far == 2) & (at_end | (g == 0)))))
+            | (jnp.logical_not(own) & (far <= 2) & ((g == 0) | ((g == 1) & at_end)))
+        )
 
     def to_mate(way, step, chunk):
         block = token_view(token_line.source(way, step), chunk)
@@ -634,22 +645,28 @@
             await_mate(1)
 
         owner = 2 * x + chunk // groups
-        far = distance(owner)
-
-        @pl.when(((step == 1) & (far <= 1)) | ((step == 2) & (far == 2)))
+        far = jnp.abs(z - owner)
+
+        @pl.when(
+            projects_early(chunk % groups, owner)
+            & (((step == 1) & (far <= 1)) | ((step == 2) & (far == 2)))
+        )
         def _():
             project(chunk % groups, owner)
 
-    for g in range(2):
-        await_beside(g)
-
-        @pl.loop(0, 2)
-        def _(at):
-            owner = 2 * (1 - x) + at
-
-            @pl.when(distance(owner) <= 2)
-            def _():
-                project(g, owner)
+        @pl.when(tick == 2 * TOKEN_CHUNKS)
+        def _():
+            await_beside(0)
+
+        @pl.when((tick == 2 * TOKEN_CHUNKS + TOKEN_CHUNKS // 2) & at_end)
+        def _():
+            await_beside(1)
+
+        guest = 2 * (1 - x) + (chunk // 2) % 2
+
+        @pl.when((step == 2) & (chunk % 2 == 0) & projects_early(chunk // 4, guest))
+        def _():
+            project(chunk // 4, guest)
 
     await_mate(2)
     for by in range(1, chan_count):
@@ -824,32 +841,67 @@
             def _():
                 line.copy(way, 0, (g, 1 - core)).start()
 
-    def relay(step, g):
+    def relay(way, step, g):
+        @pl.when(line.receives(way, step))
+        def _():
+            for of in range(2):
+                owner = line.arrived(way, step, (g, of))
+                if step + 1 < steps:
+
+                    @pl.when(line.sends(way, step + 1))
+                    def _():
+                        line.copy(way, step + 1, (g, of)).start()
+
+            accumulate(owner, g)
+
+    def settle():
+        mate_tokens().wait_send()
+        other = weight.at[:, s]
+        remote(other, other, mate_send.at[1], mate_recv.at[1], mate).wait_send()
+        for copy in sum_copies:
+            copy.wait_send()
+
+        @pl.when(x == 1)
+        def _():
+            for origin in range(2):
+                taps_beside(origin, y).wait_send()
+
+        @pl.loop(0, groups)
+        def _(g):
+            for c in range(WEIGHT_CHUNKS):
+                for to in range(2):
+                    weight_sent(to, g, c).wait_send()
+                    beside_copy(to, y, g, c).wait_send()
+
+            @pl.when(x == 0)
+            def _():
+                edge_copy(g).wait_send()
+                before_copy(g).wait_send()
+
         for way in range(2):
-
-            @pl.when(line.receives(way, step))
-            def _():
-                for of in range(2):
-                    owner = line.arrived(way, step, (g, of))
-                    if step + 1 < steps:
-
-                        @pl.when(line.sends(way, step + 1))
-                        def _():
-                            line.copy(way, step + 1, (g, of)).start()
-
-                accumulate(owner, g)
-
-    @pl.loop(0, groups + steps)
+            for step in range(steps):
+
+                @pl.when(token_line.receives(way, step))
+                def _():
+                    mate_half(way, step, core).wait_send()
+
+                @pl.when(token_line.sends(way, step))
+                def _():
+                    @pl.loop(0, TOKEN_CHUNKS)
+                    def _(chunk):
+                        token_line.copy(way, step, (chunk,)).wait_send()
+
+    @pl.loop(0, 2 * groups + steps)
     def _(g):
         @pl.when(g < groups)
         def _():
-            @pl.when(g >= 2)
+            @pl.when((g >= 2) | ((g == 1) & jnp.logical_not(at_end)))
             def _():
                 await_beside(g)
 
             @pl.loop(0, chan_count)
             def _(owner):
-                @pl.when((distance(owner) > 2) | ((owner // 2 != x) & (g >= 2)))
+                @pl.when(jnp.logical_not(projects_early(g, owner)))
                 def _():
                     project(g, owner)
 
@@ -859,9 +911,9 @@
             def _():
                 before_copy(g).start()
 
-            @pl.when(g == 0)
-            def _():
-                send_weights(groups - 1)
+            @pl.when((x == 0) & (g < 2))
+            def _():
+                send_weights(groups - 1, [WEIGHT_CHUNKS - 2 + g])
 
             convolve(g)
             begin(g)
@@ -877,40 +929,28 @@
 
             accumulate(z, g)
 
-        for step in range(steps):
-            at = g - 1 - step
-
-            @pl.when((at >= 0) & (at < groups))
-            def _():
-                relay(step, at)
+        @pl.when(g == groups + 1)
+        def _():
+            settle()
+
+        @pl.loop(0, 2)
+        def _(k):
+            way = jnp.where(z < chan_count // 2, 1 - k, k)
+            lag = jnp.where(at_end, groups, 1 + k)
+            for step in range(steps):
+                at = g - lag - step * jnp.where(at_end, 1, 2 - k)
+
+                @pl.when((at >= 0) & (at < groups))
+                def _():
+                    relay(way, step, at)
 
     @blocks(rows)
     def _(i):
         result[at_rows(i), :] = total[at_rows(i), :].astype(jnp.bfloat16)
 
-    mate_tokens().wait_send()
-    other = weight.at[:, s]
-    remote(other, other, mate_send.at[1], mate_recv.at[1], mate).wait_send()
-    for copy in sum_copies:
-        copy.wait_send()
-
-    @pl.when(x == 1)
-    def _():
-        for origin in range(2):
-            taps_beside(origin, y).wait_send()
-
     @pl.loop(0, groups)
     def _(g):
-        for c in range(WEIGHT_CHUNKS):
-            for to in range(2):
-                weight_sent(to, g, c).wait_send()
-                beside_copy(to, y, g, c).wait_send()
         swap_copy(g).wait_send()
-
-        @pl.when(x == 0)
-        def _():
-            edge_copy(g).wait_send()
-            before_copy(g).wait_send()
 
         for way in range(2):
             for step in range(steps):
@@ -919,18 +959,6 @@
                 def _():
                     for of in range(2):
                         line.copy(way, step, (g, of)).wait_send()
-
-    for way in range(2):
-        for step in range(steps):
-
-            @pl.when(token_line.receives(way, step))
-            def _():
-                mate_half(way, step, core).wait_send()
-
-            @pl.when(token_line.sends(way, step))
-            def _():
-                for chunk in range(TOKEN_CHUNKS):
-                    token_line.copy(way, step, (chunk,)).wait_send()
 
 
 def chip_body(tokens, norm_gain, proj_weight, short_filter, long_filter, skip_gain, out_weight):
@@ -1009,7 +1037,7 @@
 
 
 def select_body(mesh):
-    if mesh.shape["seq"] == 4 and mesh.shape["groups"] == 2:
+    if (mesh.shape["groups"], mesh.shape["seq"], mesh.shape["chan"]) == (2, 4, 4):
         return chip_body
     return body
 

time: 180 us -> 185 us (1.028)
  Pallas kernels: 177 us -> 182 us
    pallas_call x1, Pallas kernels: 177 us -> 182 us  [chip_body(): pl.pallas_call(functools.partial(block_kernel, chan_count), out_shape=jax...]
where the time goes in v3:
time: 185 us; the launch traced here: 184 us
  Pallas kernels  182 us (98%)
  local copies, waits for them, and re-layouts  2.26 us (1%)
    pallas_call x1, Pallas kernels, chip_body(): pl.pallas_call(functools.partial(block_kernel, chan_count), out_shape=jax...  182 us

profile of v3, /device:TPU:2, one launch (start us, length us, event | category | flops | bytes accessed | tf_op | source)
XLA Modules:
  0.0 184.3 jit_solution(565394620808224838)
XLA Ops:
  0.0 182.1 %block.1 = bf16[512,1024]{1,0:T(8,128)(2,1)} custom-call(bf16[512,1024]{1,0:T(8,128)(2,1)} %tokens.1, f32[1,4096]{1,0:T(1,128)} %bitcast.4, bf16[3,1024,1024]{2,1,0:T(8,128)(2,1)} %bitcast.3, f32[3,3,1024]{2,1,0:T(4,128)} %short.1, f32[1024,512]{1,0:T(8,128)} %long_taps.1, f32[1,1024]{1,0:T(1,128)} %bitcast.5, bf16[4096,1024]{1,0:T(8,128)(2,1)} %out_weight.1), custom_call_target="tpu_custom_call" | custom-call | tf_op jit(solution)/shard_map/block/pallas_call | solution.py:974
  182.1 2.3 %copy.9 = bf16[512,1024]{1,0:T(8,128)(2,1)} copy(bf16[512,1024]{1,0:T(8,128)(2,1)} %block.1) | data formatting | bytes 2097152

commit v4 on v3

--- a/solution.py
+++ b/solution.py
@@ -463,11 +463,10 @@
 
     for g in range(groups - 1):
         send_weights(g)
-    send_weights(groups - 1, range(WEIGHT_CHUNKS - 2))
 
     @pl.when(x == 1)
     def _():
-        send_weights(groups - 1, range(WEIGHT_CHUNKS - 2, WEIGHT_CHUNKS))
+        send_weights(groups - 1)
 
 
     def beside_copy(origin, part, g, c):
@@ -611,7 +610,7 @@
                 ).wait_recv()
                 taps_beside(origin, y).start()
 
-        @pl.when((tick % 2 == 1) & (tick >= 3) & (tick < 3 + 4 * WEIGHT_CHUNKS))
+        @pl.when((tick % 2 == 1) & (tick >= 3) & (tick < 7 + 4 * WEIGHT_CHUNKS))
         def _():
             at = (tick - 3) // 2
             forward(at // WEIGHT_CHUNKS, at % WEIGHT_CHUNKS)
@@ -911,17 +910,24 @@
             def _():
                 before_copy(g).start()
 
-            @pl.when((x == 0) & (g < 2))
-            def _():
-                send_weights(groups - 1, [WEIGHT_CHUNKS - 2 + g])
+            for at in range(2):
+
+                @pl.when((x == 0) & (g == at))
+                def _():
+                    send_weights(groups - 1, [2 * at, 2 * at + 1])
+
+            @pl.when(g == 0)
+            def _():
+                forward(groups - 2, 2)
+                forward(groups - 2, 3)
 
             convolve(g)
             begin(g)
 
-            @pl.when(g < groups - 2)
-            def _():
-                for c in range(WEIGHT_CHUNKS):
-                    forward(g + 2, c)
+            @pl.when(g < 2)
+            def _():
+                forward(groups - 1, 2 * g)
+                forward(groups - 1, 2 * g + 1)
 
             @pl.when(g == 0)
             def _():

time: 185 us -> 174 us (0.941)
  Pallas kernels: 182 us -> 172 us
    pallas_call x1, Pallas kernels: 182 us -> 172 us  [chip_body(): pl.pallas_call(functools.partial(block_kernel, chan_count), out_shape=jax...]
where the time goes in v4:
time: 174 us
  Pallas kernels  172 us (99%)
  local copies, waits for them, and re-layouts  2.26 us (1%)
    pallas_call x1, Pallas kernels, chip_body(): pl.pallas_call(functools.partial(block_kernel, chan_count), out_shape=jax...  172 us

profile of v4, /device:TPU:2, one launch (start us, length us, event | category | flops | bytes accessed | tf_op | source)
XLA Modules:
  0.0 174.0 jit_solution(4688488292623664799)
XLA Ops:
  0.0 171.7 %block.1 = bf16[512,1024]{1,0:T(8,128)(2,1)} custom-call(bf16[512,1024]{1,0:T(8,128)(2,1)} %tokens.1, f32[1,4096]{1,0:T(1,128)} %bitcast.4, bf16[3,1024,1024]{2,1,0:T(8,128)(2,1)} %bitcast.3, f32[3,3,1024]{2,1,0:T(4,128)} %short.1, f32[1024,512]{1,0:T(8,128)} %long_taps.1, f32[1,1024]{1,0:T(1,128)} %bitcast.5, bf16[4096,1024]{1,0:T(8,128)(2,1)} %out_weight.1), custom_call_target="tpu_custom_call" | custom-call | tf_op jit(solution)/shard_map/block/pallas_call | solution.py:980
  171.7 2.3 %copy.9 = bf16[512,1024]{1,0:T(8,128)(2,1)} copy(bf16[512,1024]{1,0:T(8,128)(2,1)} %block.1) | data formatting | bytes 2097152

commit v5 on v4

--- a/solution.py
+++ b/solution.py
@@ -461,13 +461,14 @@
                         across if to == 0 else aslant,
                     ).start()
 
-    for g in range(groups - 1):
+    for g in range(groups - 2):
         send_weights(g)
+    send_weights(groups - 2, range(3))
 
     @pl.when(x == 1)
     def _():
+        send_weights(groups - 2, [3])
         send_weights(groups - 1)
-
 
     def beside_copy(origin, part, g, c):
         view = weight_view((1 - x) * 2 + origin, part, g, c)
@@ -521,14 +522,20 @@
                 table[at, :], column(), preferred_element_type=jnp.float32
             )
 
-    def tap_spectra(g):
+    def spectrum_pair(columns):
         @pl.loop(0, 2 * length // SPAN)
         def _(i):
             at = rows_at(i, SPAN)
-            both = jnp.concatenate([taps[g, :length, :], taps[g, length:, :]], axis=1)
-            found = jnp.dot(table[at, :], both, preferred_element_type=jnp.float32)
+            found = jnp.dot(
+                table[at, :],
+                jnp.concatenate(columns(), axis=1),
+                preferred_element_type=jnp.float32,
+            )
             freq[0, at, :] = found[:, :LANES]
             freq[1, at, :] = found[:, LANES:]
+
+    def tap_spectra(g):
+        spectrum_pair(lambda: [taps[g, :length, :], taps[g, length:, :]])
 
         @blocks(length)
         def _(i):
@@ -761,7 +768,11 @@
             ).astype(jnp.bfloat16)
 
     def convolve(g):
-        spectrum(0, lambda: signal[g])
+        joint = (x == 1) & (g > 0)
+
+        @pl.when(jnp.logical_not(joint))
+        def _():
+            spectrum(0, lambda: signal[g])
 
         def product(i, which, first):
             low, high = at_rows(i), rows_at(i, BLOCK, length)
@@ -781,7 +792,14 @@
         @pl.when(x == 1)
         def _():
             before_copy(g).wait_recv()
-            spectrum(1, lambda: before[g])
+
+            @pl.when(g == 0)
+            def _():
+                spectrum(1, lambda: before[g])
+
+            @pl.when(g > 0)
+            def _():
+                spectrum_pair(lambda: [signal[g], before[g]])
 
             @blocks(length)
             def _(i):
@@ -832,6 +850,7 @@
             def _():
                 line.copy(way, 0, (g, core)).start()
 
+    def begin_other(g):
         other = full.at[z, g, 1 - core]
         remote(other, other, swap_send.at[g], swap_recv.at[g], mate).wait_recv()
         for way in range(2):
@@ -839,19 +858,6 @@
             @pl.when(line.sends(way, 0))
             def _():
                 line.copy(way, 0, (g, 1 - core)).start()
-
-    def relay(way, step, g):
-        @pl.when(line.receives(way, step))
-        def _():
-            for of in range(2):
-                owner = line.arrived(way, step, (g, of))
-                if step + 1 < steps:
-
-                    @pl.when(line.sends(way, step + 1))
-                    def _():
-                        line.copy(way, step + 1, (g, of)).start()
-
-            accumulate(owner, g)
 
     def settle():
         mate_tokens().wait_send()
@@ -890,6 +896,9 @@
                     def _(chunk):
                         token_line.copy(way, step, (chunk,)).wait_send()
 
+    def way_of(k):
+        return jnp.where(z < chan_count // 2, 1 - k, k)
+
     @pl.loop(0, 2 * groups + steps)
     def _(g):
         @pl.when(g < groups)
@@ -904,51 +913,91 @@
                 def _():
                     project(g, owner)
 
+            @pl.when(g == 1)
+            def _():
+                forward(groups - 2, 3)
+                forward(groups - 1, 0)
+
+            @pl.when(g == 2)
+            def _():
+                forward(groups - 1, 1)
+                forward(groups - 1, 2)
+
+        @pl.loop(0, 2)
+        def _(k):
+            way = way_of(k)
+            for step in range(steps - 1):
+                at = g - 1 - k - 2 * step
+
+                @pl.when(
+                    (at >= 0)
+                    & (at < groups)
+                    & line.receives(way, step)
+                    & line.sends(way, step + 1)
+                )
+                def _():
+                    for of in range(2):
+                        line.arrived(way, step, (at, of))
+                        line.copy(way, step + 1, (at, of)).start()
+
+        @pl.when(g < groups)
+        def _():
             featurize(g)
 
             @pl.when(x == 0)
             def _():
                 before_copy(g).start()
 
-            for at in range(2):
-
-                @pl.when((x == 0) & (g == at))
+                @pl.when(g == 0)
                 def _():
-                    send_weights(groups - 1, [2 * at, 2 * at + 1])
+                    send_weights(groups - 2, [3])
+                    send_weights(groups - 1, [0])
+
+                @pl.when(g == 1)
+                def _():
+                    send_weights(groups - 1, [1, 2, 3])
 
             @pl.when(g == 0)
             def _():
                 forward(groups - 2, 2)
-                forward(groups - 2, 3)
 
             convolve(g)
             begin(g)
 
-            @pl.when(g < 2)
-            def _():
-                forward(groups - 1, 2 * g)
-                forward(groups - 1, 2 * g + 1)
-
-            @pl.when(g == 0)
-            def _():
-                out_load.wait()
-
-            accumulate(z, g)
-
-        @pl.when(g == groups + 1)
-        def _():
-            settle()
+            @pl.when(g == 2)
+            def _():
+                forward(groups - 1, 3)
+
+            begin_other(g)
+
+        @pl.when(g == groups)
+        def _():
+            out_load.wait()
+
+        own = g - groups
+
+        @pl.when((own >= 0) & (own < groups))
+        def _():
+            accumulate(z, own)
 
         @pl.loop(0, 2)
         def _(k):
-            way = jnp.where(z < chan_count // 2, 1 - k, k)
-            lag = jnp.where(at_end, groups, 1 + k)
+            way = way_of(k)
             for step in range(steps):
-                at = g - lag - step * jnp.where(at_end, 1, 2 - k)
-
-                @pl.when((at >= 0) & (at < groups))
+                at = g - groups - step
+
+                @pl.when((at >= 0) & (at < groups) & line.receives(way, step))
                 def _():
-                    relay(way, step, at)
+                    @pl.when(jnp.logical_not(line.sends(way, step + 1)))
+                    def _():
+                        for of in range(2):
+                            line.arrived(way, step, (at, of))
+
+                    accumulate(line.source(way, step), at)
+
+        @pl.when(g == groups + 1)
+        def _():
+            settle()
 
     @blocks(rows)
     def _(i):

time: 174 us -> 167 us (0.960)
  Pallas kernels: 172 us -> 164 us
    pallas_call x1, Pallas kernels: 172 us -> 164 us  [chip_body(): pl.pallas_call(functools.partial(block_kernel, chan_count), out_shape=jax...]
where the time goes in v5:
time: 167 us; the launch traced here: 166 us
  Pallas kernels  164 us (98%)
  local copies, waits for them, and re-layouts  2.26 us (1%)
    pallas_call x1, Pallas kernels, chip_body(): pl.pallas_call(functools.partial(block_kernel, chan_count), out_shape=jax...  164 us

profile of v5, /device:TPU:2, one launch (start us, length us, event | category | flops | bytes accessed | tf_op | source)
XLA Modules:
  0.0 166.3 jit_solution(4518566249503157496)
XLA Ops:
  0.0 164.1 %block.1 = bf16[512,1024]{1,0:T(8,128)(2,1)} custom-call(bf16[512,1024]{1,0:T(8,128)(2,1)} %tokens.1, f32[1,4096]{1,0:T(1,128)} %bitcast.4, bf16[3,1024,1024]{2,1,0:T(8,128)(2,1)} %bitcast.3, f32[3,3,1024]{2,1,0:T(4,128)} %short.1, f32[1024,512]{1,0:T(8,128)} %long_taps.1, f32[1,1024]{1,0:T(1,128)} %bitcast.5, bf16[4096,1024]{1,0:T(8,128)(2,1)} %out_weight.1), custom_call_target="tpu_custom_call" | custom-call | tf_op jit(solution)/shard_map/block/pallas_call | solution.py:1029
  164.1 2.3 %copy.9 = bf16[512,1024]{1,0:T(8,128)(2,1)} copy(bf16[512,1024]{1,0:T(8,128)(2,1)} %block.1) | data formatting | bytes 2097152

commit v6 on v5

--- a/solution.py
+++ b/solution.py
@@ -175,10 +175,11 @@
         self.me = lax.axis_index("chan")
 
     def move(self, way, step, piece, block, target):
-        index = (way, step) + piece
-        return remote(
-            block, block, self.send_sem.at[index], self.recv_sem.at[index], self.place(target)
-        )
+        recv = self.recv_sem.at[(way, step) + piece]
+        return remote(block, block, self.send_sem.at[way, step], recv, self.place(target))
+
+    def drain(self, way, step, first, block):
+        self.move(way, step, first, block(self.source(way, step - 1)), self.me).wait_send()
 
     def source(self, way, step):
         return jnp.clip(self.me - (step + 1) * (1 - 2 * way), 0, self.count - 1)
@@ -219,11 +220,9 @@
     sums,
     scale,
     partial,
-    room,
     out_room,
     table,
     taps,
-    turn,
     spectra,
     freq,
     mixed,
@@ -304,9 +303,12 @@
         )
         for j, (which, start) in enumerate(tap_stage)
     ]
-    token_load = pltpu.make_async_copy(tokens, room, local_sem.at[0])
+    token_load = pltpu.make_async_copy(tokens, result, local_sem.at[0])
     out_load = pltpu.make_async_copy(out_weight, out_room, local_sem.at[1])
     token_load.start()
+    barrier = pltpu.get_barrier_semaphore()
+    for peer in peers:
+        pl.semaphore_signal(barrier, inc=1, device_id=peer, device_id_type=pl.DeviceIdType.MESH)
     for copy in tap_loads:
         copy.start()
     for g in range(groups):
@@ -318,17 +320,13 @@
             ).start()
     out_load.start()
 
-    barrier = pltpu.get_barrier_semaphore()
-    for peer in peers:
-        pl.semaphore_signal(barrier, inc=1, device_id=peer, device_id_type=pl.DeviceIdType.MESH)
-
     sums[core, z] = jnp.zeros(sums.shape[2:], jnp.float32)
     own_gain = gain[:, pl.ds(pl.multiple_of(z * width, width), width)]
     token_load.wait()
 
     @blocks(rows)
     def _(i):
-        raw = room[at_rows(i), :].astype(jnp.float32)
+        raw = result[at_rows(i), :].astype(jnp.float32)
         total[at_rows(i), :] = raw
         stream[z, pl.ds(pl.multiple_of(core * rows + i * BLOCK, BLOCK), BLOCK), :] = (
             raw * own_gain
@@ -437,11 +435,8 @@
     def weight_view(owner, part, g, c):
         return weight.at[g, owner, rows_at(c, weight_rows, part * half), :]
 
-    def weight_sent(to, g, c):
-        view = weight_view(s, y, g, c)
-        return remote(
-            view, view, x_send.at[to, g, c], x_recv.at[core, g, c], across if to == 0 else aslant
-        )
+    def weight_half(owner, part):
+        return weight.at[:, owner, pl.ds(pl.multiple_of(part * half, half), half), :]
 
     def send_weights(g, chunks=range(WEIGHT_CHUNKS)):
         for c in chunks:
@@ -456,7 +451,7 @@
                             pl.ds(pl.multiple_of(side * share + g * LANES, LANES), LANES),
                         ],
                         view.at[:, pl.ds(b * LANES, LANES)],
-                        x_send.at[to, g, c],
+                        x_send.at[to],
                         x_recv.at[core, g, c],
                         across if to == 0 else aslant,
                     ).start()
@@ -465,27 +460,35 @@
         send_weights(g)
     send_weights(groups - 2, range(3))
 
+    at_end = (z == 0) | (z == chan_count - 1)
+
+    @pl.when((x == 1) | at_end)
+    def _():
+        send_weights(groups - 2, [3])
+        send_weights(groups - 1, [0, 1])
+
     @pl.when(x == 1)
     def _():
-        send_weights(groups - 2, [3])
-        send_weights(groups - 1)
+        send_weights(groups - 1, [2, 3])
 
     def beside_copy(origin, part, g, c):
         view = weight_view((1 - x) * 2 + origin, part, g, c)
-        return remote(view, view, y_send.at[origin, g, c], y_recv.at[origin, g, c], beside)
+        return remote(view, view, y_send.at[origin], y_recv.at[origin, g], beside)
 
     def forward(g, c):
         for origin in range(2):
             view = weight_view((1 - x) * 2 + origin, y, g, c)
             remote(
-                view, view, x_send.at[origin, g, c], x_recv.at[origin, g, c], beside
+                view, view, x_send.at[origin], x_recv.at[origin, g, c], beside
             ).wait_recv()
             beside_copy(origin, y, g, c).start()
 
     def await_beside(g):
-        for c in range(WEIGHT_CHUNKS):
-            for origin in range(2):
-                beside_copy(origin, 1 - y, g, c).wait_recv()
+        for origin in range(2):
+            view = weight.at[
+                g, (1 - x) * 2 + origin, pl.ds(pl.multiple_of((1 - y) * half, half), half), :
+            ]
+            remote(view, view, y_send.at[origin], y_recv.at[origin, g], beside).wait_recv()
 
     @blocks(length)
     def _(i):
@@ -494,8 +497,8 @@
         unit = math.pi / (4 * length)
         odd = 2 * row + 1
         small = odd.astype(jnp.float32) * unit
-        turn[0, at_rows(i), :] = jnp.cos(small)
-        turn[1, at_rows(i), :] = jnp.sin(small)
+        extended[0, at_rows(i), :] = jnp.cos(small)
+        extended[1, at_rows(i), :] = jnp.sin(small)
         period = 8 * length
         angle = (odd * (2 * lane + 1) % period).astype(jnp.float32) * unit
         cos, sin = jnp.cos(angle), jnp.sin(angle)
@@ -540,7 +543,7 @@
         @blocks(length)
         def _(i):
             low, high = at_rows(i), rows_at(i, BLOCK, length)
-            cos, sin = turn[0, low, :], turn[1, low, :]
+            cos, sin = extended[0, low, :], extended[1, low, :]
 
             def turned(which):
                 real, imag = freq[which, low, :], -freq[which, high, :]
@@ -562,8 +565,6 @@
             partial[g, at, :] += jnp.dot(
                 stream[owner, at, :], weight[g, owner], preferred_element_type=jnp.float32
             )
-
-    at_end = (z == 0) | (z == chan_count - 1)
 
     def projects_early(g, owner):
         far = jnp.abs(z - owner)
@@ -702,17 +703,17 @@
 
     def edge_copy(g):
         return remote(
-            edge_out.at[g], edge.at[g], edge_send.at[g], edge_recv.at[g], across
+            edge_out.at[g], edge.at[g], edge_send.at[0], edge_recv.at[g], across
         )
 
     def before_copy(g):
         return remote(
-            signal.at[g], before.at[g], before_send.at[g], before_recv.at[g], across
+            signal.at[g], before.at[g], before_send.at[0], before_recv.at[g], across
         )
 
     def swap_copy(g):
         return remote(
-            ready.at[g], full.at[z, g, core], swap_send.at[g], swap_recv.at[g], mate
+            ready.at[g], full.at[z, g, core], swap_send.at[0], swap_recv.at[g], mate
         )
 
     line = Line(
@@ -852,7 +853,7 @@
 
     def begin_other(g):
         other = full.at[z, g, 1 - core]
-        remote(other, other, swap_send.at[g], swap_recv.at[g], mate).wait_recv()
+        remote(other, other, swap_send.at[0], swap_recv.at[g], mate).wait_recv()
         for way in range(2):
 
             @pl.when(line.sends(way, 0))
@@ -871,17 +872,16 @@
             for origin in range(2):
                 taps_beside(origin, y).wait_send()
 
-        @pl.loop(0, groups)
-        def _(g):
-            for c in range(WEIGHT_CHUNKS):
-                for to in range(2):
-                    weight_sent(to, g, c).wait_send()
-                    beside_copy(to, y, g, c).wait_send()
-
-            @pl.when(x == 0)
-            def _():
-                edge_copy(g).wait_send()
-                before_copy(g).wait_send()
+        for at in range(2):
+            view = weight_half(s, y)
+            remote(view, view, x_send.at[at], x_recv.at[0, 0, 0], across).wait_send()
+            view = weight_half((1 - x) * 2 + at, y)
+            remote(view, view, y_send.at[at], y_recv.at[at, 0], beside).wait_send()
+
+        @pl.when(x == 0)
+        def _():
+            remote(edge_out, edge, edge_send.at[0], edge_recv.at[0], across).wait_send()
+            remote(signal, before, before_send.at[0], before_recv.at[0], across).wait_send()
 
         for way in range(2):
             for step in range(steps):
@@ -892,12 +892,27 @@
 
                 @pl.when(token_line.sends(way, step))
                 def _():
-                    @pl.loop(0, TOKEN_CHUNKS)
-                    def _(chunk):
-                        token_line.copy(way, step, (chunk,)).wait_send()
+                    token_line.drain(way, step, (0,), lambda owner: own_half(owner, core))
 
     def way_of(k):
         return jnp.where(z < chan_count // 2, 1 - k, k)
+
+    def late_forwards(g, at, inner, outer):
+        for here, pieces in ((jnp.logical_not(at_end), inner), (at_end, outer)):
+
+            @pl.when((g == at) & here)
+            def _():
+                for group, c in pieces:
+                    forward(group, c)
+
+    def pass_on(way, step, at):
+        @pl.when(
+            (at >= 0) & (at < groups) & line.receives(way, step) & line.sends(way, step + 1)
+        )
+        def _():
+            for of in range(2):
+                line.arrived(way, step, (at, of))
+                line.copy(way, step + 1, (at, of)).start()
 
     @pl.loop(0, 2 * groups + steps)
     def _(g):
@@ -913,32 +928,12 @@
                 def _():
                     project(g, owner)
 
-            @pl.when(g == 1)
-            def _():
-                forward(groups - 2, 3)
-                forward(groups - 1, 0)
-
-            @pl.when(g == 2)
-            def _():
-                forward(groups - 1, 1)
-                forward(groups - 1, 2)
+            late_forwards(g, 1, [(groups - 2, 3), (groups - 1, 0)], [(groups - 1, 0), (groups - 1, 1)])
+            late_forwards(g, 2, [(groups - 1, 1), (groups - 1, 2)], [(groups - 1, 3)])
 
         @pl.loop(0, 2)
         def _(k):
-            way = way_of(k)
-            for step in range(steps - 1):
-                at = g - 1 - k - 2 * step
-
-                @pl.when(
-                    (at >= 0)
-                    & (at < groups)
-                    & line.receives(way, step)
-                    & line.sends(way, step + 1)
-                )
-                def _():
-                    for of in range(2):
-                        line.arrived(way, step, (at, of))
-                        line.copy(way, step + 1, (at, of)).start()
+            pass_on(way_of(k), 0, g - 1 - k)
 
         @pl.when(g < groups)
         def _():
@@ -948,33 +943,37 @@
             def _():
                 before_copy(g).start()
 
-                @pl.when(g == 0)
-                def _():
-                    send_weights(groups - 2, [3])
-                    send_weights(groups - 1, [0])
-
-                @pl.when(g == 1)
-                def _():
-                    send_weights(groups - 1, [1, 2, 3])
-
-            @pl.when(g == 0)
-            def _():
-                forward(groups - 2, 2)
-
+                for at, inner, outer in (
+                    (0, [(groups - 2, 3), (groups - 1, 0)], [(groups - 1, 2)]),
+                    (1, [(groups - 1, 1), (groups - 1, 2)], [(groups - 1, 3)]),
+                    (2, [(groups - 1, 3)], []),
+                ):
+
+                    @pl.when((g == at) & jnp.logical_not(at_end))
+                    def _():
+                        for group, c in inner:
+                            send_weights(group, [c])
+
+                    @pl.when((g == at) & at_end)
+                    def _():
+                        for group, c in outer:
+                            send_weights(group, [c])
+
+            late_forwards(g, 0, [(groups - 2, 2)], [(groups - 2, 2), (groups - 2, 3)])
             convolve(g)
             begin(g)
-
-            @pl.when(g == 2)
-            def _():
-                forward(groups - 1, 3)
-
+            late_forwards(g, 1, [], [(groups - 1, 2)])
+            late_forwards(g, 2, [(groups - 1, 3)], [])
             begin_other(g)
 
-        @pl.when(g == groups)
+        for step in range(1, steps - 1):
+            pass_on(way_of(0), step, g - 1 - step)
+
+        @pl.when(g == groups - 1)
         def _():
             out_load.wait()
 
-        own = g - groups
+        own = jnp.where(at_end, g - groups, g - groups + 1)
 
         @pl.when((own >= 0) & (own < groups))
         def _():
@@ -984,7 +983,7 @@
         def _(k):
             way = way_of(k)
             for step in range(steps):
-                at = g - groups - step
+                at = own - jnp.where(at_end, step, 0)
 
                 @pl.when((at >= 0) & (at < groups) & line.receives(way, step))
                 def _():
@@ -1003,17 +1002,13 @@
     def _(i):
         result[at_rows(i), :] = total[at_rows(i), :].astype(jnp.bfloat16)
 
-    @pl.loop(0, groups)
-    def _(g):
-        swap_copy(g).wait_send()
-
-        for way in range(2):
-            for step in range(steps):
-
-                @pl.when(line.sends(way, step))
-                def _():
-                    for of in range(2):
-                        line.copy(way, step, (g, of)).wait_send()
+    remote(ready, ready, swap_send.at[0], swap_recv.at[0], mate).wait_send()
+    for way in range(2):
+        for step in range(steps):
+
+            @pl.when(line.sends(way, step))
+            def _():
+                line.drain(way, step, (0, 0), lambda owner: full.at[owner])
 
 
 def chip_body(tokens, norm_gain, proj_weight, short_filter, long_filter, skip_gain, out_weight):
@@ -1037,11 +1032,9 @@
             pltpu.VMEM((2, chan_count, 8, LANES), f32),
             pltpu.VMEM((length, LANES), f32),
             pltpu.VMEM((groups, length, branches * LANES), f32),
-            pltpu.VMEM((rows, width), bf16),
             pltpu.VMEM(out_weight.shape, bf16),
             pltpu.VMEM((2 * length, length), bf16),
             pltpu.VMEM((groups, 2 * length, LANES), bf16),
-            pltpu.VMEM((2, length, LANES), f32),
             pltpu.VMEM((groups, 4, length, LANES), bf16),
             pltpu.VMEM((2, 2 * length, LANES), f32),
             pltpu.VMEM((2 * length, LANES), bf16),
@@ -1057,27 +1050,27 @@
             dma((8,)),
             dma((3 + 2 * steps,)),
             dma((3 + 2 * steps,)),
-            dma((2, steps, TOKEN_CHUNKS)),
+            dma((2, steps)),
             dma((2, steps, TOKEN_CHUNKS)),
             dma((2 * chan_count - 1,)),
             dma((2, chan_count)),
+            dma((2,)),
             dma((2, groups, WEIGHT_CHUNKS)),
-            dma((2, groups, WEIGHT_CHUNKS)),
-            dma((2, groups, WEIGHT_CHUNKS)),
-            dma((2, groups, WEIGHT_CHUNKS)),
+            dma((2,)),
+            dma((2, groups)),
             dma((4,)),
             dma((4,)),
+            dma((1,)),
             dma((groups,)),
+            dma((1,)),
             dma((groups,)),
+            dma((1,)),
             dma((groups,)),
-            dma((groups,)),
-            dma((groups,)),
-            dma((groups,)),
-            dma((2, steps, groups, 2)),
+            dma((2, steps)),
             dma((2, steps, groups, 2)),
         ],
         compiler_params=pltpu.CompilerParams(
-            collective_id=0, has_side_effects=True, vmem_limit_bytes=63 * 1024 * 1024
+            collective_id=0, has_side_effects=True, vmem_limit_bytes=61 * 1024 * 1024
         ),
         name="block",
     )(

time: 167 us -> 158 us (0.946)
  Pallas kernels: 164 us -> 154 us
    pallas_call x1, Pallas kernels: 164 us -> 154 us  [chip_body(): pl.pallas_call(functools.partial(block_kernel, chan_count), out_shape=jax...]
where the time goes in v6:
time: 158 us; the launch traced here: 156 us
  Pallas kernels  154 us (97%)
  local copies, waits for them, and re-layouts  2.26 us (1%)
    pallas_call x1, Pallas kernels, chip_body(): pl.pallas_call(functools.partial(block_kernel, chan_count), out_shape=jax...  154 us

profile of v6, /device:TPU:2, one launch (start us, length us, event | category | flops | bytes accessed | tf_op | source)
XLA Modules:
  0.0 156.5 jit_solution(12541011347836894898)
XLA Ops:
  0.0 154.2 %block.1 = bf16[512,1024]{1,0:T(8,128)(2,1)} custom-call(bf16[512,1024]{1,0:T(8,128)(2,1)} %tokens.1, f32[1,4096]{1,0:T(1,128)} %bitcast.4, bf16[3,1024,1024]{2,1,0:T(8,128)(2,1)} %bitcast.3, f32[3,3,1024]{2,1,0:T(4,128)} %short.1, f32[1024,512]{1,0:T(8,128)} %long_taps.1, f32[1,1024]{1,0:T(1,128)} %bitcast.5, bf16[4096,1024]{1,0:T(8,128)(2,1)} %out_weight.1), custom_call_target="tpu_custom_call" | custom-call | tf_op jit(solution)/shard_map/block/pallas_call | solution.py:1024
  154.2 2.3 %copy.9 = bf16[512,1024]{1,0:T(8,128)(2,1)} copy(bf16[512,1024]{1,0:T(8,128)(2,1)} %block.1) | data formatting | bytes 2097152

commit v7 on v6

--- a/solution.py
+++ b/solution.py
@@ -220,7 +220,6 @@
     sums,
     scale,
     partial,
-    out_room,
     table,
     taps,
     spectra,
@@ -304,7 +303,6 @@
         for j, (which, start) in enumerate(tap_stage)
     ]
     token_load = pltpu.make_async_copy(tokens, result, local_sem.at[0])
-    out_load = pltpu.make_async_copy(out_weight, out_room, local_sem.at[1])
     token_load.start()
     barrier = pltpu.get_barrier_semaphore()
     for peer in peers:
@@ -318,7 +316,6 @@
                 weight.at[g, s, :, pl.ds(b * LANES, LANES)],
                 local_sem.at[2],
             ).start()
-    out_load.start()
 
     sums[core, z] = jnp.zeros(sums.shape[2:], jnp.float32)
     own_gain = gain[:, pl.ds(pl.multiple_of(z * width, width), width)]
@@ -832,15 +829,20 @@
                 pl.ds(pl.multiple_of((1 - core) * rows + i * BLOCK, BLOCK), BLOCK)
             )
 
+    def load_out():
+        for owner in range(chan_count):
+            pltpu.make_async_copy(
+                out_weight.at[pl.ds(owner * length, length)], stream.at[owner], local_sem.at[1]
+            ).start()
+
     def accumulate(owner, g):
-        left = pl.ds(pl.multiple_of(owner * 2 * share + g * LANES, LANES), LANES)
-        right = pl.ds(pl.multiple_of((owner * 2 + 1) * share + g * LANES, LANES), LANES)
-
         @pl.loop(0, total.shape[1] // (2 * LANES))
         def _(i):
             cols = rows_at(i, 2 * LANES)
             block = jnp.concatenate([full[owner, g, 0], full[owner, g, 1]], axis=1)
-            kernel = jnp.concatenate([out_room[left, cols], out_room[right, cols]], axis=0)
+            kernel = jnp.concatenate(
+                [stream[owner, lanes_of(of * share, g), cols] for of in range(2)], axis=0
+            )
             total[:, cols] += jnp.dot(block, kernel, preferred_element_type=jnp.float32)
 
     def begin(g):
@@ -861,7 +863,6 @@
                 line.copy(way, 0, (g, 1 - core)).start()
 
     def settle():
-        mate_tokens().wait_send()
         other = weight.at[:, s]
         remote(other, other, mate_send.at[1], mate_recv.at[1], mate).wait_send()
         for copy in sum_copies:
@@ -883,6 +884,8 @@
             remote(edge_out, edge, edge_send.at[0], edge_recv.at[0], across).wait_send()
             remote(signal, before, before_send.at[0], before_recv.at[0], across).wait_send()
 
+    def settle_tokens():
+        mate_tokens().wait_send()
         for way in range(2):
             for step in range(steps):
 
@@ -914,76 +917,104 @@
                 line.arrived(way, step, (at, of))
                 line.copy(way, step + 1, (at, of)).start()
 
-    @pl.loop(0, 2 * groups + steps)
+    near, away = way_of(0), way_of(1)
+
+    @pl.loop(0, groups)
     def _(g):
-        @pl.when(g < groups)
-        def _():
-            @pl.when((g >= 2) | ((g == 1) & jnp.logical_not(at_end)))
-            def _():
-                await_beside(g)
-
-            @pl.loop(0, chan_count)
-            def _(owner):
-                @pl.when(jnp.logical_not(projects_early(g, owner)))
+        @pl.when(g == 3)
+        def _():
+            pass_on(away, 0, 1)
+
+        @pl.when((g >= 2) | ((g == 1) & jnp.logical_not(at_end)))
+        def _():
+            await_beside(g)
+
+        @pl.when(g == 3)
+        def _():
+            pass_on(near, 0, 2)
+
+        @pl.loop(0, chan_count)
+        def _(owner):
+            @pl.when(jnp.logical_not(projects_early(g, owner)))
+            def _():
+                project(g, owner)
+
+        @pl.when(g == groups - 1)
+        def _():
+            settle_tokens()
+            load_out()
+
+        late_forwards(g, 1, [(groups - 2, 3), (groups - 1, 0)], [(groups - 1, 0), (groups - 1, 1)])
+        late_forwards(g, 2, [(groups - 1, 1), (groups - 1, 2)], [(groups - 1, 3)])
+
+        @pl.when((g == 1) | (g == 2))
+        def _():
+            pass_on(near, 0, g - 1)
+
+        @pl.when(g == 2)
+        def _():
+            pass_on(away, 0, 0)
+
+        featurize(g)
+
+        @pl.when(x == 0)
+        def _():
+            before_copy(g).start()
+
+            for at, inner, outer in (
+                (0, [(groups - 2, 3), (groups - 1, 0)], [(groups - 1, 2)]),
+                (1, [(groups - 1, 1), (groups - 1, 2)], [(groups - 1, 3)]),
+                (2, [(groups - 1, 3)], []),
+            ):
+
+                @pl.when((g == at) & jnp.logical_not(at_end))
                 def _():
-                    project(g, owner)
-
-            late_forwards(g, 1, [(groups - 2, 3), (groups - 1, 0)], [(groups - 1, 0), (groups - 1, 1)])
-            late_forwards(g, 2, [(groups - 1, 1), (groups - 1, 2)], [(groups - 1, 3)])
+                    for group, c in inner:
+                        send_weights(group, [c])
+
+                @pl.when((g == at) & at_end)
+                def _():
+                    for group, c in outer:
+                        send_weights(group, [c])
+
+        late_forwards(g, 0, [(groups - 2, 2)], [(groups - 2, 2), (groups - 2, 3)])
+        convolve(g)
+        begin(g)
+        late_forwards(g, 1, [], [(groups - 1, 2)])
+        late_forwards(g, 2, [(groups - 1, 3)], [])
+        begin_other(g)
+
+        @pl.when(g == 2)
+        def _():
+            pass_on(near, 1, 0)
+
+    pltpu.make_async_copy(stream, stream, local_sem.at[1]).wait()
+
+    @pl.loop(0, groups + steps - 1)
+    def _(n):
+        for at, pieces in (
+            (0, [(near, 1, 1), (away, 0, 2)]),
+            (1, [(near, 0, 3), (near, 1, 2), (away, 0, 3)]),
+            (3, [(near, 1, 3)]),
+        ):
+
+            @pl.when(n == at)
+            def _():
+                for way, step, group in pieces:
+                    pass_on(way, step, group)
+
+        @pl.when(n == 2)
+        def _():
+            settle()
+
+        @pl.when(n < groups)
+        def _():
+            accumulate(z, n)
 
         @pl.loop(0, 2)
-        def _(k):
-            pass_on(way_of(k), 0, g - 1 - k)
-
-        @pl.when(g < groups)
-        def _():
-            featurize(g)
-
-            @pl.when(x == 0)
-            def _():
-                before_copy(g).start()
-
-                for at, inner, outer in (
-                    (0, [(groups - 2, 3), (groups - 1, 0)], [(groups - 1, 2)]),
-                    (1, [(groups - 1, 1), (groups - 1, 2)], [(groups - 1, 3)]),
-                    (2, [(groups - 1, 3)], []),
-                ):
-
-                    @pl.when((g == at) & jnp.logical_not(at_end))
-                    def _():
-                        for group, c in inner:
-                            send_weights(group, [c])
-
-                    @pl.when((g == at) & at_end)
-                    def _():
-                        for group, c in outer:
-                            send_weights(group, [c])
-
-            late_forwards(g, 0, [(groups - 2, 2)], [(groups - 2, 2), (groups - 2, 3)])
-            convolve(g)
-            begin(g)
-            late_forwards(g, 1, [], [(groups - 1, 2)])
-            late_forwards(g, 2, [(groups - 1, 3)], [])
-            begin_other(g)
-
-        for step in range(1, steps - 1):
-            pass_on(way_of(0), step, g - 1 - step)
-
-        @pl.when(g == groups - 1)
-        def _():
-            out_load.wait()
-
-        own = jnp.where(at_end, g - groups, g - groups + 1)
-
-        @pl.when((own >= 0) & (own < groups))
-        def _():
-            accumulate(z, own)
-
-        @pl.loop(0, 2)
-        def _(k):
-            way = way_of(k)
+        def _(way):
             for step in range(steps):
-                at = own - jnp.where(at_end, step, 0)
+                at = n - jnp.where(at_end, step, 0)
 
                 @pl.when((at >= 0) & (at < groups) & line.receives(way, step))
                 def _():
@@ -993,10 +1024,6 @@
                             line.arrived(way, step, (at, of))
 
                     accumulate(line.source(way, step), at)
-
-        @pl.when(g == groups + 1)
-        def _():
-            settle()
 
     @blocks(rows)
     def _(i):
@@ -1032,7 +1059,6 @@
             pltpu.VMEM((2, chan_count, 8, LANES), f32),
             pltpu.VMEM((length, LANES), f32),
             pltpu.VMEM((groups, length, branches * LANES), f32),
-            pltpu.VMEM(out_weight.shape, bf16),
             pltpu.VMEM((2 * length, length), bf16),
             pltpu.VMEM((groups, 2 * length, LANES), bf16),
             pltpu.VMEM((groups, 4, length, LANES), bf16),
@@ -1070,7 +1096,7 @@
             dma((2, steps, groups, 2)),
         ],
         compiler_params=pltpu.CompilerParams(
-            collective_id=0, has_side_effects=True, vmem_limit_bytes=61 * 1024 * 1024
+            collective_id=0, has_side_effects=True, vmem_limit_bytes=52 * 1024 * 1024
         ),
         name="block",
     )(

time: 158 us -> 155 us (0.981); the launches traced: 156 us -> 155 us
  Pallas kernels: 154 us -> 152 us
    pallas_call x1, Pallas kernels: 154 us -> 152 us  [chip_body(): pl.pallas_call(functools.partial(block_kernel, chan_count), out_shape=jax...]
    unnamed x1 -> x7, local copies, waits for them, and re-layouts: 2.26 us -> 3.17 us
where the time goes in v7:
time: 155 us
  Pallas kernels  152 us (98%)
  local copies, waits for them, and re-layouts  3.17 us (2%)
    pallas_call x1, Pallas kernels, chip_body(): pl.pallas_call(functools.partial(block_kernel, chan_count), out_shape=jax...  152 us
    unnamed x7, local copies, waits for them, and re-layouts  3.17 us

profile of v7, /device:TPU:2, one launch (start us, length us, event | category | flops | bytes accessed | tf_op | source)
XLA Modules:
  0.0 155.2 jit_solution(5042565197992436759)
XLA Ops:
  0.0 0.0 copy-start
  0.0 0.8 copy-done
  0.8 0.0 copy-start.1
  0.8 0.7 copy-done.1
  1.5 0.0 copy-start.2
  1.5 0.7 copy-done.2
  2.2 152.0 %block.1 = bf16[512,1024]{1,0:T(8,128)(2,1)S(1)} custom-call(bf16[512,1024]{1,0:T(8,128)(2,1)} %tokens.1, f32[1,4096]{1,0:T(1,128)S(1)} %bitcast.3, bf16[3,1024,1024]{2,1,0:T(8,128)(2,1)} %bitcast.5, f32[3,3,1024]{2,1,0:T(4,128)S(1)} %copy-done, f32[1024,512]{1,0:T(8,128)} %long_taps.1, f32[1,1024]{1,0:T(1,128)S(1)} %bitcast.4, bf16[4096,1024]{1,0:T(8,128)(2,1)} %out_weight.1), custom_call_target="tpu_custom_call" | custom-call | tf_op jit(solution)/shard_map/block/pallas_call | solution.py:1051
  154.2 1.0 copy.9
Async XLA Ops:
  0.0 0.8 copy-start
  0.8 0.7 copy-start.1
  1.5 0.7 copy-start.2

commit v8 on v7

--- a/solution.py
+++ b/solution.py
@@ -154,7 +154,7 @@
 SPAN = 512
 TOKEN_CHUNKS = 8
 WEIGHT_CHUNKS = 4
-ANY = pl.BlockSpec(memory_space=pl.ANY)
+HBM = pl.BlockSpec(memory_space=pltpu.HBM)
 
 
 def remote(src, dst, send_sem, recv_sem, where):
@@ -208,13 +208,16 @@
 def block_kernel(
     chan_count,
     tokens,
-    gain,
+    gain_hbm,
     weights,
-    short,
+    short_hbm,
     long_taps,
-    skip,
+    skip_hbm,
     out_weight,
     result,
+    gain,
+    short,
+    skip,
     stream,
     weight,
     sums,
@@ -304,6 +307,16 @@
     ]
     token_load = pltpu.make_async_copy(tokens, result, local_sem.at[0])
     token_load.start()
+    small_loads = [
+        pltpu.make_async_copy(src, dst, local_sem.at[at])
+        for src, dst, at in (
+            (gain_hbm.at[:, pl.ds(pl.multiple_of(z * width, width), width)], gain, 3),
+            (short_hbm, short, 8),
+            (skip_hbm, skip, 9),
+        )
+    ]
+    for copy in small_loads:
+        copy.start()
     barrier = pltpu.get_barrier_semaphore()
     for peer in peers:
         pl.semaphore_signal(barrier, inc=1, device_id=peer, device_id_type=pl.DeviceIdType.MESH)
@@ -318,7 +331,8 @@
             ).start()
 
     sums[core, z] = jnp.zeros(sums.shape[2:], jnp.float32)
-    own_gain = gain[:, pl.ds(pl.multiple_of(z * width, width), width)]
+    small_loads[0].wait()
+    own_gain = gain[...]
     token_load.wait()
 
     @blocks(rows)
@@ -913,10 +927,12 @@
             (at >= 0) & (at < groups) & line.receives(way, step) & line.sends(way, step + 1)
         )
         def _():
-            for of in range(2):
+            for of in (core, 1 - core):
                 line.arrived(way, step, (at, of))
                 line.copy(way, step + 1, (at, of)).start()
 
+    for copy in small_loads[1:]:
+        copy.wait()
     near, away = way_of(0), way_of(1)
 
     @pl.loop(0, groups)
@@ -943,17 +959,6 @@
         def _():
             settle_tokens()
             load_out()
-
-        late_forwards(g, 1, [(groups - 2, 3), (groups - 1, 0)], [(groups - 1, 0), (groups - 1, 1)])
-        late_forwards(g, 2, [(groups - 1, 1), (groups - 1, 2)], [(groups - 1, 3)])
-
-        @pl.when((g == 1) | (g == 2))
-        def _():
-            pass_on(near, 0, g - 1)
-
-        @pl.when(g == 2)
-        def _():
-            pass_on(away, 0, 0)
 
         featurize(g)
 
@@ -976,6 +981,17 @@
                 def _():
                     for group, c in outer:
                         send_weights(group, [c])
+
+        late_forwards(g, 1, [(groups - 2, 3), (groups - 1, 0)], [(groups - 1, 0), (groups - 1, 1)])
+        late_forwards(g, 2, [(groups - 1, 1), (groups - 1, 2)], [(groups - 1, 3)])
+
+        @pl.when((g == 1) | (g == 2))
+        def _():
+            pass_on(near, 0, g - 1)
+
+        @pl.when(g == 2)
+        def _():
+            pass_on(away, 0, 0)
 
         late_forwards(g, 0, [(groups - 2, 2)], [(groups - 2, 2), (groups - 2, 3)])
         convolve(g)
@@ -1051,9 +1067,12 @@
     return pl.pallas_call(
         functools.partial(block_kernel, chan_count),
         out_shape=jax.ShapeDtypeStruct((rows, width), bf16),
-        in_specs=[ANY, vmem, ANY, vmem, ANY, vmem, ANY],
+        in_specs=[HBM] * 7,
         out_specs=vmem,
         scratch_shapes=[
+            pltpu.VMEM((1, width), f32),
+            pltpu.VMEM(short_filter.shape, f32),
+            pltpu.VMEM((1, local_chan), f32),
             pltpu.VMEM((chan_count, length, width), bf16),
             pltpu.VMEM((groups, 4, depth, branches * LANES), bf16),
             pltpu.VMEM((2, chan_count, 8, LANES), f32),
@@ -1073,7 +1092,7 @@
             pltpu.VMEM((groups, rows, LANES), bf16),
             pltpu.VMEM((chan_count, groups, 2, rows, LANES), bf16),
             pltpu.VMEM((rows, width), f32),
-            dma((8,)),
+            dma((10,)),
             dma((3 + 2 * steps,)),
             dma((3 + 2 * steps,)),
             dma((2, steps)),
@@ -1101,11 +1120,11 @@
         name="block",
     )(
         tokens,
-        norm_gain[None, :],
+        pltpu.with_memory_space_constraint(norm_gain[None, :], pltpu.HBM),
         proj_weight.transpose(1, 0, 2),
-        short_filter,
+        pltpu.with_memory_space_constraint(short_filter, pltpu.HBM),
         long_filter,
-        skip_gain[None, :],
+        pltpu.with_memory_space_constraint(skip_gain[None, :], pltpu.HBM),
         out_weight,
     )
 

time: 155 us -> 153 us (0.987)
  local copies, waits for them, and re-layouts: 3.17 us -> 0.97 us
    unnamed x7 -> x1, local copies, waits for them, and re-layouts: 3.17 us -> 0.97 us
where the time goes in v8:
time: 153 us
  Pallas kernels  152 us (99%)
    pallas_call x1, Pallas kernels, chip_body(): pl.pallas_call(functools.partial(block_kernel, chan_count), out_shape=jax...  152 us

profile of v8, /device:TPU:2, one launch (start us, length us, event | category | flops | bytes accessed | tf_op | source)
XLA Modules:
  0.0 153.0 jit_solution(5170632646277498454)
XLA Ops:
  0.0 152.0 %block.1 = bf16[512,1024]{1,0:T(8,128)(2,1)S(1)} custom-call(bf16[512,1024]{1,0:T(8,128)(2,1)} %tokens.1, f32[1,4096]{1,0:T(1,128)} %bitcast.4, bf16[3,1024,1024]{2,1,0:T(8,128)(2,1)} %bitcast.3, f32[3,3,1024]{2,1,0:T(4,128)} %short_hbm.1, f32[1024,512]{1,0:T(8,128)} %long_taps.1, f32[1,1024]{1,0:T(1,128)} %bitcast.5, bf16[4096,1024]{1,0:T(8,128)(2,1)} %out_weight.1), custom_call_target="tpu_custom_call" | custom-call | tf_op jit(solution)/shard_map/block/pallas_call | solution.py:1067
  152.0 1.0 copy.9

commit v9 on v8

--- a/solution.py
+++ b/solution.py
@@ -939,15 +939,18 @@
     def _(g):
         @pl.when(g == 3)
         def _():
+            pass_on(near, 0, 2)
+            pass_on(near, 1, 0)
+
+        late_forwards(g, 3, [(groups - 1, 3)], [])
+
+        @pl.when(g == 3)
+        def _():
             pass_on(away, 0, 1)
 
         @pl.when((g >= 2) | ((g == 1) & jnp.logical_not(at_end)))
         def _():
             await_beside(g)
-
-        @pl.when(g == 3)
-        def _():
-            pass_on(near, 0, 2)
 
         @pl.loop(0, chan_count)
         def _(owner):
@@ -967,9 +970,9 @@
             before_copy(g).start()
 
             for at, inner, outer in (
-                (0, [(groups - 2, 3), (groups - 1, 0)], [(groups - 1, 2)]),
-                (1, [(groups - 1, 1), (groups - 1, 2)], [(groups - 1, 3)]),
-                (2, [(groups - 1, 3)], []),
+                (0, [], [(groups - 1, 2)]),
+                (1, [(groups - 2, 3), (groups - 1, 0)], [(groups - 1, 3)]),
+                (2, [(groups - 1, 1), (groups - 1, 2), (groups - 1, 3)], []),
             ):
 
                 @pl.when((g == at) & jnp.logical_not(at_end))
@@ -982,27 +985,24 @@
                     for group, c in outer:
                         send_weights(group, [c])
 
-        late_forwards(g, 1, [(groups - 2, 3), (groups - 1, 0)], [(groups - 1, 0), (groups - 1, 1)])
-        late_forwards(g, 2, [(groups - 1, 1), (groups - 1, 2)], [(groups - 1, 3)])
+        late_forwards(g, 1, [(groups - 2, 3)], [(groups - 1, 0), (groups - 1, 1)])
+        late_forwards(g, 2, [(groups - 1, 0)], [(groups - 1, 3)])
 
         @pl.when((g == 1) | (g == 2))
         def _():
             pass_on(near, 0, g - 1)
-
-        @pl.when(g == 2)
-        def _():
-            pass_on(away, 0, 0)
 
         late_forwards(g, 0, [(groups - 2, 2)], [(groups - 2, 2), (groups - 2, 3)])
         convolve(g)
         begin(g)
         late_forwards(g, 1, [], [(groups - 1, 2)])
-        late_forwards(g, 2, [(groups - 1, 3)], [])
         begin_other(g)
 
         @pl.when(g == 2)
         def _():
-            pass_on(near, 1, 0)
+            pass_on(away, 0, 0)
+
+        late_forwards(g, 2, [(groups - 1, 1), (groups - 1, 2)], [])
 
     pltpu.make_async_copy(stream, stream, local_sem.at[1]).wait()
 

time: 153 us -> 160 us (1.046)
  Pallas kernels: 152 us -> 159 us
    pallas_call x1, Pallas kernels: 152 us -> 159 us  [chip_body(): pl.pallas_call(functools.partial(block_kernel, chan_count), out_shape=jax...]
where the time goes in v9:
time: 160 us
  Pallas kernels  159 us (99%)
    pallas_call x1, Pallas kernels, chip_body(): pl.pallas_call(functools.partial(block_kernel, chan_count), out_shape=jax...  159 us

profile of v9, /device:TPU:2, one launch (start us, length us, event | category | flops | bytes accessed | tf_op | source)
XLA Modules:
  0.0 159.7 jit_solution(4749021744102597413)
XLA Ops:
  0.0 158.7 %block.1 = bf16[512,1024]{1,0:T(8,128)(2,1)S(1)} custom-call(bf16[512,1024]{1,0:T(8,128)(2,1)} %tokens.1, f32[1,4096]{1,0:T(1,128)} %bitcast.4, bf16[3,1024,1024]{2,1,0:T(8,128)(2,1)} %bitcast.3, f32[3,3,1024]{2,1,0:T(4,128)} %short_hbm.1, f32[1024,512]{1,0:T(8,128)} %long_taps.1, f32[1,1024]{1,0:T(1,128)} %bitcast.5, bf16[4096,1024]{1,0:T(8,128)(2,1)} %out_weight.1), custom_call_target="tpu_custom_call" | custom-call | tf_op jit(solution)/shard_map/block/pallas_call | solution.py:1067
  158.7 1.0 copy.9

commit v10 on v9

--- a/solution.py
+++ b/solution.py
@@ -937,15 +937,11 @@
 
     @pl.loop(0, groups)
     def _(g):
+        late_forwards(g, 3, [(groups - 1, 3)], [])
+
         @pl.when(g == 3)
         def _():
             pass_on(near, 0, 2)
-            pass_on(near, 1, 0)
-
-        late_forwards(g, 3, [(groups - 1, 3)], [])
-
-        @pl.when(g == 3)
-        def _():
             pass_on(away, 0, 1)
 
         @pl.when((g >= 2) | ((g == 1) & jnp.logical_not(at_end)))
@@ -991,6 +987,10 @@
         @pl.when((g == 1) | (g == 2))
         def _():
             pass_on(near, 0, g - 1)
+
+        @pl.when(g == 3)
+        def _():
+            pass_on(near, 1, 0)
 
         late_forwards(g, 0, [(groups - 2, 2)], [(groups - 2, 2), (groups - 2, 3)])
         convolve(g)

time: 160 us -> 159 us (level)
  no operation moved by 1% of the time
where the time goes in v10:
time: 159 us
  Pallas kernels  158 us (99%)
    pallas_call x1, Pallas kernels, chip_body(): pl.pallas_call(functools.partial(block_kernel, chan_count), out_shape=jax...  158 us

profile of v10, /device:TPU:2, one launch (start us, length us, event | category | flops | bytes accessed | tf_op | source)
XLA Modules:
  0.0 158.7 jit_solution(18209451494908850622)
XLA Ops:
  0.0 157.7 %block.1 = bf16[512,1024]{1,0:T(8,128)(2,1)S(1)} custom-call(bf16[512,1024]{1,0:T(8,128)(2,1)} %tokens.1, f32[1,4096]{1,0:T(1,128)} %bitcast.4, bf16[3,1024,1024]{2,1,0:T(8,128)(2,1)} %bitcast.3, f32[3,3,1024]{2,1,0:T(4,128)} %short_hbm.1, f32[1024,512]{1,0:T(8,128)} %long_taps.1, f32[1,1024]{1,0:T(1,128)} %bitcast.5, bf16[4096,1024]{1,0:T(8,128)(2,1)} %out_weight.1), custom_call_target="tpu_custom_call" | custom-call | tf_op jit(solution)/shard_map/block/pallas_call | solution.py:1067
  157.7 1.0 copy.9

commit v11 on v8

--- a/solution.py
+++ b/solution.py
@@ -940,14 +940,11 @@
         @pl.when(g == 3)
         def _():
             pass_on(away, 0, 1)
+            pass_on(near, 0, 2)
 
         @pl.when((g >= 2) | ((g == 1) & jnp.logical_not(at_end)))
         def _():
             await_beside(g)
-
-        @pl.when(g == 3)
-        def _():
-            pass_on(near, 0, 2)
 
         @pl.loop(0, chan_count)
         def _(owner):
@@ -967,9 +964,9 @@
             before_copy(g).start()
 
             for at, inner, outer in (
-                (0, [(groups - 2, 3), (groups - 1, 0)], [(groups - 1, 2)]),
-                (1, [(groups - 1, 1), (groups - 1, 2)], [(groups - 1, 3)]),
-                (2, [(groups - 1, 3)], []),
+                (0, [], [(groups - 1, 2)]),
+                (1, [(groups - 2, 3), (groups - 1, 0), (groups - 1, 1)], [(groups - 1, 3)]),
+                (2, [(groups - 1, 2), (groups - 1, 3)], []),
             ):
 
                 @pl.when((g == at) & jnp.logical_not(at_end))
@@ -982,8 +979,8 @@
                     for group, c in outer:
                         send_weights(group, [c])
 
-        late_forwards(g, 1, [(groups - 2, 3), (groups - 1, 0)], [(groups - 1, 0), (groups - 1, 1)])
-        late_forwards(g, 2, [(groups - 1, 1), (groups - 1, 2)], [(groups - 1, 3)])
+        late_forwards(g, 1, [(groups - 2, 3)], [(groups - 1, 0), (groups - 1, 1)])
+        late_forwards(g, 2, [(groups - 1, 0), (groups - 1, 1)], [(groups - 1, 3)])
 
         @pl.when((g == 1) | (g == 2))
         def _():
@@ -997,12 +994,15 @@
         convolve(g)
         begin(g)
         late_forwards(g, 1, [], [(groups - 1, 2)])
+        begin_other(g)
+
+        late_forwards(g, 2, [(groups - 1, 2)], [])
+
+        @pl.when(g == 2)
+        def _():
+            pass_on(near, 1, 0)
+
         late_forwards(g, 2, [(groups - 1, 3)], [])
-        begin_other(g)
-
-        @pl.when(g == 2)
-        def _():
-            pass_on(near, 1, 0)
 
     pltpu.make_async_copy(stream, stream, local_sem.at[1]).wait()
 

time: 153 us -> 154 us (level)
  no operation moved by 1% of the time
where the time goes in v11:
time: 154 us
  Pallas kernels  153 us (99%)
    pallas_call x1, Pallas kernels, chip_body(): pl.pallas_call(functools.partial(block_kernel, chan_count), out_shape=jax...  153 us

profile of v11, /device:TPU:2, one launch (start us, length us, event | category | flops | bytes accessed | tf_op | source)
XLA Modules:
  0.0 153.8 jit_solution(12718598279022800328)
XLA Ops:
  0.0 152.8 %block.1 = bf16[512,1024]{1,0:T(8,128)(2,1)S(1)} custom-call(bf16[512,1024]{1,0:T(8,128)(2,1)} %tokens.1, f32[1,4096]{1,0:T(1,128)} %bitcast.4, bf16[3,1024,1024]{2,1,0:T(8,128)(2,1)} %bitcast.3, f32[3,3,1024]{2,1,0:T(4,128)} %short_hbm.1, f32[1024,512]{1,0:T(8,128)} %long_taps.1, f32[1,1024]{1,0:T(1,128)} %bitcast.5, bf16[4096,1024]{1,0:T(8,128)(2,1)} %out_weight.1), custom_call_target="tpu_custom_call" | custom-call | tf_op jit(solution)/shard_map/block/pallas_call | solution.py:1067
  152.9 1.0 copy.9

commit v12 on v11

--- a/solution.py
+++ b/solution.py
@@ -175,7 +175,8 @@
         self.me = lax.axis_index("chan")
 
     def move(self, way, step, piece, block, target):
-        recv = self.recv_sem.at[(way, step) + piece]
+        slot = jnp.minimum(jnp.where(way == 0, step, target + step), self.count - 2)
+        recv = self.recv_sem.at[(slot,) + piece]
         return remote(block, block, self.send_sem.at[way, step], recv, self.place(target))
 
     def drain(self, way, step, first, block):
@@ -990,27 +991,30 @@
         def _():
             pass_on(away, 0, 0)
 
+        @pl.when(g == 3)
+        def _():
+            pass_on(near, 1, 1)
+            pass_on(away, 0, 2)
+
         late_forwards(g, 0, [(groups - 2, 2)], [(groups - 2, 2), (groups - 2, 3)])
         convolve(g)
         begin(g)
         late_forwards(g, 1, [], [(groups - 1, 2)])
         begin_other(g)
 
-        late_forwards(g, 2, [(groups - 1, 2)], [])
+        late_forwards(g, 2, [(groups - 1, 2), (groups - 1, 3)], [])
 
         @pl.when(g == 2)
         def _():
             pass_on(near, 1, 0)
-
-        late_forwards(g, 2, [(groups - 1, 3)], [])
 
     pltpu.make_async_copy(stream, stream, local_sem.at[1]).wait()
 
     @pl.loop(0, groups + steps - 1)
     def _(n):
         for at, pieces in (
-            (0, [(near, 1, 1), (away, 0, 2)]),
-            (1, [(near, 0, 3), (near, 1, 2), (away, 0, 3)]),
+            (0, [(near, 1, 2)]),
+            (1, [(near, 0, 3), (away, 0, 3)]),
             (3, [(near, 1, 3)]),
         ):
 
@@ -1096,7 +1100,7 @@
             dma((3 + 2 * steps,)),
             dma((3 + 2 * steps,)),
             dma((2, steps)),
-            dma((2, steps, TOKEN_CHUNKS)),
+            dma((steps, TOKEN_CHUNKS)),
             dma((2 * chan_count - 1,)),
             dma((2, chan_count)),
             dma((2,)),
@@ -1112,7 +1116,7 @@
             dma((1,)),
             dma((groups,)),
             dma((2, steps)),
-            dma((2, steps, groups, 2)),
+            dma((steps, groups, 2)),
         ],
         compiler_params=pltpu.CompilerParams(
             collective_id=0, has_side_effects=True, vmem_limit_bytes=52 * 1024 * 1024

time: 154 us -> 151 us (0.981)
  Pallas kernels: 153 us -> 149 us
    pallas_call x1, Pallas kernels: 153 us -> 149 us  [chip_body(): pl.pallas_call(functools.partial(block_kernel, chan_count), out_shape=jax...]
where the time goes in v12:
time: 151 us; the launch traced here: 150 us
  Pallas kernels  149 us (99%)
    pallas_call x1, Pallas kernels, chip_body(): pl.pallas_call(functools.partial(block_kernel, chan_count), out_shape=jax...  149 us

profile of v12, /device:TPU:2, one launch (start us, length us, event | category | flops | bytes accessed | tf_op | source)
XLA Modules:
  0.0 150.3 jit_solution(1529370587763453226)
XLA Ops:
  0.0 149.3 %block.1 = bf16[512,1024]{1,0:T(8,128)(2,1)S(1)} custom-call(bf16[512,1024]{1,0:T(8,128)(2,1)} %tokens.1, f32[1,4096]{1,0:T(1,128)} %bitcast.4, bf16[3,1024,1024]{2,1,0:T(8,128)(2,1)} %bitcast.3, f32[3,3,1024]{2,1,0:T(4,128)} %short_hbm.1, f32[1024,512]{1,0:T(8,128)} %long_taps.1, f32[1,1024]{1,0:T(1,128)} %bitcast.5, bf16[4096,1024]{1,0:T(8,128)(2,1)} %out_weight.1), custom_call_target="tpu_custom_call" | custom-call | tf_op jit(solution)/shard_map/block/pallas_call | solution.py:1071
  149.3 1.0 copy.9

commit v13 on v12

--- a/solution.py
+++ b/solution.py
@@ -470,13 +470,13 @@
 
     for g in range(groups - 2):
         send_weights(g)
-    send_weights(groups - 2, range(3))
+    send_weights(groups - 2, range(2))
 
     at_end = (z == 0) | (z == chan_count - 1)
 
     @pl.when((x == 1) | at_end)
     def _():
-        send_weights(groups - 2, [3])
+        send_weights(groups - 2, [2, 3])
         send_weights(groups - 1, [0, 1])
 
     @pl.when(x == 1)
@@ -965,7 +965,7 @@
             before_copy(g).start()
 
             for at, inner, outer in (
-                (0, [], [(groups - 1, 2)]),
+                (0, [(groups - 2, 2)], [(groups - 1, 2)]),
                 (1, [(groups - 2, 3), (groups - 1, 0), (groups - 1, 1)], [(groups - 1, 3)]),
                 (2, [(groups - 1, 2), (groups - 1, 3)], []),
             ):
@@ -980,15 +980,16 @@
                     for group, c in outer:
                         send_weights(group, [c])
 
+        @pl.when(g == 1)
+        def _():
+            pass_on(near, 0, 0)
+
         late_forwards(g, 1, [(groups - 2, 3)], [(groups - 1, 0), (groups - 1, 1)])
         late_forwards(g, 2, [(groups - 1, 0), (groups - 1, 1)], [(groups - 1, 3)])
 
-        @pl.when((g == 1) | (g == 2))
-        def _():
-            pass_on(near, 0, g - 1)
-
         @pl.when(g == 2)
         def _():
+            pass_on(near, 0, 1)
             pass_on(away, 0, 0)
 
         @pl.when(g == 3)
@@ -996,9 +997,10 @@
             pass_on(near, 1, 1)
             pass_on(away, 0, 2)
 
-        late_forwards(g, 0, [(groups - 2, 2)], [(groups - 2, 2), (groups - 2, 3)])
+        late_forwards(g, 0, [], [(groups - 2, 2), (groups - 2, 3)])
         convolve(g)
         begin(g)
+        late_forwards(g, 0, [(groups - 2, 2)], [])
         late_forwards(g, 1, [], [(groups - 1, 2)])
         begin_other(g)
 

time: 151 us -> 151 us (level)
  no operation moved by 1% of the time
where the time goes in v13:
time: 151 us
  Pallas kernels  150 us (99%)
    pallas_call x1, Pallas kernels, chip_body(): pl.pallas_call(functools.partial(block_kernel, chan_count), out_shape=jax...  150 us

profile of v13, /device:TPU:2, one launch (start us, length us, event | category | flops | bytes accessed | tf_op | source)
XLA Modules:
  0.0 151.1 jit_solution(3869630460538808548)
XLA Ops:
  0.0 150.1 %block.1 = bf16[512,1024]{1,0:T(8,128)(2,1)S(1)} custom-call(bf16[512,1024]{1,0:T(8,128)(2,1)} %tokens.1, f32[1,4096]{1,0:T(1,128)} %bitcast.4, bf16[3,1024,1024]{2,1,0:T(8,128)(2,1)} %bitcast.3, f32[3,3,1024]{2,1,0:T(4,128)} %short_hbm.1, f32[1024,512]{1,0:T(8,128)} %long_taps.1, f32[1,1024]{1,0:T(1,128)} %bitcast.5, bf16[4096,1024]{1,0:T(8,128)(2,1)} %out_weight.1), custom_call_target="tpu_custom_call" | custom-call | tf_op jit(solution)/shard_map/block/pallas_call | solution.py:1073
  150.1 1.0 copy.9

commit v14 on v13

--- a/solution.py
+++ b/solution.py
@@ -151,7 +151,7 @@
 
 LANES = 128
 BLOCK = 128
-SPAN = 512
+SPAN = 1024
 TOKEN_CHUNKS = 8
 WEIGHT_CHUNKS = 4
 HBM = pl.BlockSpec(memory_space=pltpu.HBM)
@@ -1016,7 +1016,7 @@
     def _(n):
         for at, pieces in (
             (0, [(near, 1, 2)]),
-            (1, [(near, 0, 3), (away, 0, 3)]),
+            (1, [(away, 0, 3), (near, 0, 3)]),
             (3, [(near, 1, 3)]),
         ):
 

time: 151 us -> 149 us (0.987)
  Pallas kernels: 150 us -> 148 us
    pallas_call x1, Pallas kernels: 150 us -> 148 us  [chip_body(): pl.pallas_call(functools.partial(block_kernel, chan_count), out_shape=jax...]
where the time goes in v14:
time: 149 us
  Pallas kernels  148 us (99%)
    pallas_call x1, Pallas kernels, chip_body(): pl.pallas_call(functools.partial(block_kernel, chan_count), out_shape=jax...  148 us

profile of v14, /device:TPU:2, one launch (start us, length us, event | category | flops | bytes accessed | tf_op | source)
XLA Modules:
  0.0 149.0 jit_solution(17272306322180445837)
XLA Ops:
  0.0 148.0 %block.1 = bf16[512,1024]{1,0:T(8,128)(2,1)S(1)} custom-call(bf16[512,1024]{1,0:T(8,128)(2,1)} %tokens.1, f32[1,4096]{1,0:T(1,128)} %bitcast.4, bf16[3,1024,1024]{2,1,0:T(8,128)(2,1)} %bitcast.3, f32[3,3,1024]{2,1,0:T(4,128)} %short_hbm.1, f32[1024,512]{1,0:T(8,128)} %long_taps.1, f32[1,1024]{1,0:T(1,128)} %bitcast.5, bf16[4096,1024]{1,0:T(8,128)(2,1)} %out_weight.1), custom_call_target="tpu_custom_call" | custom-call | tf_op jit(solution)/shard_map/block/pallas_call | solution.py:1073
  148.0 1.0 copy.9

commit v15 on v14

--- a/solution.py
+++ b/solution.py
@@ -938,6 +938,10 @@
 
     @pl.loop(0, groups)
     def _(g):
+        @pl.when(g == 2)
+        def _():
+            pass_on(near, 0, 1)
+
         @pl.when(g == 3)
         def _():
             pass_on(away, 0, 1)
@@ -966,8 +970,8 @@
 
             for at, inner, outer in (
                 (0, [(groups - 2, 2)], [(groups - 1, 2)]),
-                (1, [(groups - 2, 3), (groups - 1, 0), (groups - 1, 1)], [(groups - 1, 3)]),
-                (2, [(groups - 1, 2), (groups - 1, 3)], []),
+                (1, [(groups - 2, 3), (groups - 1, 0)], [(groups - 1, 3)]),
+                (2, [(groups - 1, 1), (groups - 1, 2), (groups - 1, 3)], []),
             ):
 
                 @pl.when((g == at) & jnp.logical_not(at_end))
@@ -984,13 +988,8 @@
         def _():
             pass_on(near, 0, 0)
 
-        late_forwards(g, 1, [(groups - 2, 3)], [(groups - 1, 0), (groups - 1, 1)])
-        late_forwards(g, 2, [(groups - 1, 0), (groups - 1, 1)], [(groups - 1, 3)])
-
-        @pl.when(g == 2)
-        def _():
-            pass_on(near, 0, 1)
-            pass_on(away, 0, 0)
+        late_forwards(g, 1, [], [(groups - 1, 0), (groups - 1, 1)])
+        late_forwards(g, 2, [(groups - 1, 0)], [(groups - 1, 3)])
 
         @pl.when(g == 3)
         def _():
@@ -1001,14 +1000,20 @@
         convolve(g)
         begin(g)
         late_forwards(g, 0, [(groups - 2, 2)], [])
-        late_forwards(g, 1, [], [(groups - 1, 2)])
+        late_forwards(g, 1, [(groups - 2, 3)], [(groups - 1, 2)])
         begin_other(g)
 
-        late_forwards(g, 2, [(groups - 1, 2), (groups - 1, 3)], [])
-
         @pl.when(g == 2)
         def _():
+            pass_on(away, 0, 0)
+
+        late_forwards(g, 2, [(groups - 1, 1), (groups - 1, 2)], [])
+
+        @pl.when(g == 2)
+        def _():
             pass_on(near, 1, 0)
+
+        late_forwards(g, 2, [(groups - 1, 3)], [])
 
     pltpu.make_async_copy(stream, stream, local_sem.at[1]).wait()
 

time: 149 us -> 152 us (1.020)
  Pallas kernels: 148 us -> 151 us
    pallas_call x1, Pallas kernels: 148 us -> 151 us  [chip_body(): pl.pallas_call(functools.partial(block_kernel, chan_count), out_shape=jax...]
where the time goes in v15:
time: 152 us
  Pallas kernels  151 us (99%)
    pallas_call x1, Pallas kernels, chip_body(): pl.pallas_call(functools.partial(block_kernel, chan_count), out_shape=jax...  151 us

profile of v15, /device:TPU:2, one launch (start us, length us, event | category | flops | bytes accessed | tf_op | source)
XLA Modules:
  0.0 151.7 jit_solution(12822810067920643136)
XLA Ops:
  0.0 150.7 %block.1 = bf16[512,1024]{1,0:T(8,128)(2,1)S(1)} custom-call(bf16[512,1024]{1,0:T(8,128)(2,1)} %tokens.1, f32[1,4096]{1,0:T(1,128)} %bitcast.4, bf16[3,1024,1024]{2,1,0:T(8,128)(2,1)} %bitcast.3, f32[3,3,1024]{2,1,0:T(4,128)} %short_hbm.1, f32[1024,512]{1,0:T(8,128)} %long_taps.1, f32[1,1024]{1,0:T(1,128)} %bitcast.5, bf16[4096,1024]{1,0:T(8,128)(2,1)} %out_weight.1), custom_call_target="tpu_custom_call" | custom-call | tf_op jit(solution)/shard_map/block/pallas_call | solution.py:1078
  150.7 1.0 copy.9

commit v16 on v14

--- a/solution.py
+++ b/solution.py
@@ -851,9 +851,9 @@
             ).start()
 
     def accumulate(owner, g):
-        @pl.loop(0, total.shape[1] // (2 * LANES))
+        @pl.loop(0, total.shape[1] // (8 * LANES))
         def _(i):
-            cols = rows_at(i, 2 * LANES)
+            cols = rows_at(i, 8 * LANES)
             block = jnp.concatenate([full[owner, g, 0], full[owner, g, 1]], axis=1)
             kernel = jnp.concatenate(
                 [stream[owner, lanes_of(of * share, g), cols] for of in range(2)], axis=0

time: 149 us -> 149 us (level)
  no operation moved by 1% of the time
where the time goes in v16:
time: 149 us
  Pallas kernels  148 us (99%)
    pallas_call x1, Pallas kernels, chip_body(): pl.pallas_call(functools.partial(block_kernel, chan_count), out_shape=jax...  148 us

profile of v16, /device:TPU:2, one launch (start us, length us, event | category | flops | bytes accessed | tf_op | source)
XLA Modules:
  0.0 148.5 jit_solution(14763943752578829997)
XLA Ops:
  0.0 147.5 %block.1 = bf16[512,1024]{1,0:T(8,128)(2,1)S(1)} custom-call(bf16[512,1024]{1,0:T(8,128)(2,1)} %tokens.1, f32[1,4096]{1,0:T(1,128)} %bitcast.4, bf16[3,1024,1024]{2,1,0:T(8,128)(2,1)} %bitcast.3, f32[3,3,1024]{2,1,0:T(4,128)} %short_hbm.1, f32[1024,512]{1,0:T(8,128)} %long_taps.1, f32[1,1024]{1,0:T(1,128)} %bitcast.5, bf16[4096,1024]{1,0:T(8,128)(2,1)} %out_weight.1), custom_call_target="tpu_custom_call" | custom-call | tf_op jit(solution)/shard_map/block/pallas_call | solution.py:1073
  147.5 1.0 copy.9

commit v17 on v16

--- a/solution.py
+++ b/solution.py
@@ -984,7 +984,7 @@
         def _():
             pass_on(near, 0, 0)
 
-        late_forwards(g, 1, [(groups - 2, 3)], [(groups - 1, 0), (groups - 1, 1)])
+        late_forwards(g, 1, [], [(groups - 1, 0), (groups - 1, 1)])
         late_forwards(g, 2, [(groups - 1, 0), (groups - 1, 1)], [(groups - 1, 3)])
 
         @pl.when(g == 2)
@@ -1001,7 +1001,7 @@
         convolve(g)
         begin(g)
         late_forwards(g, 0, [(groups - 2, 2)], [])
-        late_forwards(g, 1, [], [(groups - 1, 2)])
+        late_forwards(g, 1, [(groups - 2, 3)], [(groups - 1, 2)])
         begin_other(g)
 
         late_forwards(g, 2, [(groups - 1, 2), (groups - 1, 3)], [])

time: 149 us -> 149 us (level)
  no operation moved by 1% of the time
where the time goes in v17:
time: 149 us
  Pallas kernels  148 us (99%)
    pallas_call x1, Pallas kernels, chip_body(): pl.pallas_call(functools.partial(block_kernel, chan_count), out_shape=jax...  148 us

profile of v17, /device:TPU:2, one launch (start us, length us, event | category | flops | bytes accessed | tf_op | source)
XLA Modules:
  0.0 148.5 jit_solution(14510558998504135118)
XLA Ops:
  0.0 147.5 %block.1 = bf16[512,1024]{1,0:T(8,128)(2,1)S(1)} custom-call(bf16[512,1024]{1,0:T(8,128)(2,1)} %tokens.1, f32[1,4096]{1,0:T(1,128)} %bitcast.4, bf16[3,1024,1024]{2,1,0:T(8,128)(2,1)} %bitcast.3, f32[3,3,1024]{2,1,0:T(4,128)} %short_hbm.1, f32[1024,512]{1,0:T(8,128)} %long_taps.1, f32[1,1024]{1,0:T(1,128)} %bitcast.5, bf16[4096,1024]{1,0:T(8,128)(2,1)} %out_weight.1), custom_call_target="tpu_custom_call" | custom-call | tf_op jit(solution)/shard_map/block/pallas_call | solution.py:1073
  147.5 1.0 copy.9
